TPU v7x, 32 devices: a whole 2x2x4 slice. The times are simulated.
32 devices in a mesh: dp: 4 (over y, x), fsdp: 8 (over z, core).
Axes of the slice: x: 2, y: 2, z: 4, core: 2. Of those that a mesh axis runs over, the one named last changes fastest.
Arguments:
- tokens: bfloat16 [4096, 8192], P('dp', 'fsdp'), may hold values from -72 to 72
- w_query: bfloat16 [8192, 8192], P('dp', 'fsdp'), may hold values from -0.0625 to 0.0625
- w_output: bfloat16 [8192, 8192], P('dp', 'fsdp'), may hold values from -0.5 to 0.5
- neighbor_shard: int32 [64, 2], P('dp'), may hold values from 0 to 3, all different within a row; in each aligned block of 16 rows (0 to 15, 16 to 31, ...) at most 12 rows name the same one
- neighbor_block: int32 [64, 2], P('dp'), may hold values from 0 to 31
- kv_store: bfloat16 [4, 32, 2, 128, 8192], P('dp', None, None, None, 'fsdp'), may hold values from -350 to 350
Outputs:
- cross_output: bfloat16 [4096, 8192], P('dp', 'fsdp')
Inputs may be any that keep to these rules, and one draw needn't show every extreme that they name: `neighbor_shard`: the 2 neighbours of one span lie in different shards. Among the 16 spans of one token group no shard is named by more than 12 spans, a bound that some block reaches.
All inputs are finite; a program needn't handle non-finite values.
Results may differ from a plain program's by a relative error of at most 0.0049.
The roundings to bfloat16 on the way count: a program that leaves them out, or rounds other values in their place, can miss the bound.
Values may be sent and summed in bfloat16 or wider, within the bound.
No kernel may reach another device: no remote copies, remote signals or barrier semaphores. Data moves between devices by JAX's collectives and lax.ppermute only.
A program may use at most 320 MiB of HBM per device.

v0:
```python
import jax
import jax.numpy as jnp
from jax import lax
from jax.sharding import PartitionSpec as P

HEAD_DIM = 128
NEIGH = 2


EPSILON = 1e-05


def normalize(features):
    widened = features.astype(jnp.float32)
    mean_square = jnp.mean(widened * widened, axis=1, keepdims=True)
    return (widened * lax.rsqrt(mean_square + EPSILON)).astype(jnp.bfloat16)


def shards(tokens, w_query, w_output, neighbor_shard, neighbor_block, kv_store):
    gathered = lax.all_gather(tokens, "fsdp", axis=1, tiled=True)
    normed = normalize(gathered)
    row_count = normed.shape[0]
    local_width = w_query.shape[1]
    queries = jnp.dot(
        normed,
        lax.all_gather(w_query, "dp", axis=0, tiled=True),
        preferred_element_type=jnp.float32,
    ).astype(jnp.bfloat16)
    peers = lax.axis_size("dp")
    span_count = neighbor_shard.shape[0]
    capacity = max(2, 3 * span_count * NEIGH // (2 * peers))
    owners = neighbor_shard.reshape(-1)
    wanted = neighbor_block.reshape(-1)
    owned = (owners[:, None] == jnp.arange(peers, dtype=jnp.int32)[None, :]).astype(jnp.int32)
    earlier = jnp.cumsum(owned, axis=0) - owned
    placed = owners * capacity + jnp.sum(earlier * owned, axis=1)
    matches = placed[:, None] == jnp.arange(peers * capacity, dtype=jnp.int32)[None, :]
    table = jnp.sum(jnp.where(matches, wanted[:, None], 0), axis=0).reshape(peers, capacity)
    stored = kv_store[0]
    replies = lax.all_to_all(
        stored[lax.all_to_all(table, "dp", split_axis=0, concat_axis=0, tiled=True)],
        "dp",
        split_axis=0,
        concat_axis=0,
        tiled=True,
    )
    fetched = replies.reshape((peers * capacity,) + replies.shape[2:])[placed]
    block_size = fetched.shape[2]
    head_count = local_width // HEAD_DIM
    grouped = fetched.reshape(span_count, NEIGH, 2, block_size, local_width)
    key_rows = grouped[:, :, 0].reshape(span_count, NEIGH * block_size, head_count, HEAD_DIM)
    value_rows = grouped[:, :, 1].reshape(span_count, NEIGH * block_size, head_count, HEAD_DIM)
    query_grid = queries.reshape(span_count, row_count // span_count, head_count, HEAD_DIM)
    scores = jnp.einsum(
        "cqhd,ckhd->chqk", query_grid, key_rows, preferred_element_type=jnp.float32
    ) * HEAD_DIM ** (-0.5)
    highest = jnp.max(scores, axis=-1, keepdims=True)
    raised = jnp.exp(scores - highest)
    weights = (raised / jnp.sum(raised, axis=-1, keepdims=True)).astype(jnp.bfloat16)
    mixed_heads = jnp.einsum(
        "chqk,ckhd->cqhd", weights, value_rows, preferred_element_type=jnp.float32
    )
    attended = mixed_heads.astype(jnp.bfloat16).reshape(row_count, local_width)
    w_columns = lax.all_gather(w_output, "dp", axis=0, tiled=True)
    summed = jnp.dot(
        lax.all_gather(attended, "fsdp", axis=1, tiled=True),
        w_columns,
        preferred_element_type=jnp.float32,
    )
    return summed.astype(jnp.bfloat16)


def solution(mesh):
    in_specs = (
        P("dp", "fsdp"),
        P("dp", "fsdp"),
        P("dp", "fsdp"),
        P("dp", None),
        P("dp", None),
        P("dp", None, None, None, "fsdp"),
    )
    out_specs = P("dp", "fsdp")
    return jax.shard_map(shards, mesh=mesh, in_specs=in_specs, out_specs=out_specs, check_vma=False)
```

profile of v0, /device:TPU:25, one launch (start us, length us, event | category | flops | bytes accessed | tf_op | source)
XLA Modules:
  0.0 797.7 jit_solution(4837158703240660849)
XLA Ops:
  6.5 0.0 all-gather.5.cloned.1.call-start
  6.5 0.7 all-gather.5.cloned.1.call-update
  7.3 0.0 all-gather.7.cloned.1.call-start
  7.3 0.7 all-gather.7.cloned.1.call-update
  8.0 0.8 copy.38
  8.8 0.1 broadcast_in_dim.14
  8.9 0.8 copy.37
  9.6 0.1 reshape.92
  9.7 0.1 fusion.24
  9.8 0.1 reduce_window_sum.11
  9.8 0.2 select_reduce_fusion.1
  10.0 0.1 select_reduce_fusion
  10.1 0.1 all_to_all.11
  10.2 6.8 all_to_all.17
  17.0 0.1 reshape.99
  17.1 18.1 %gather_fusion = bf16[48,2,128,1024]{3,2,1,0:T(8,128)(2,1)} fusion(bf16[32,2,128,1024]{3,2,1,0:T(8,128)(2,1)} %bitcast.44, s32[1024]{0:T(1024)S(1)} %pad_clamp_fusion.1), kind=kCustom, calls=%fused_computation | custom fusion | bytes 50331840 | tf_op jit(solution)/shard_map/gather | solution.py:41
  35.2 0.0 copy-start.1
  35.2 8.7 %all-to-all-start.1 = ((bf16[4,12,2,128,1024]{4,3,2,1,0:T(8,128)(2,1)}), bf16[4,12,2,128,1024]{4,3,2,1,0:T(8,128)(2,1)}, u32[]{:S(2)}, u32[]{:S(2)}) async-start(bf16[4,12,2,128,1024]{4,3,2,1,0:T(8,128)(2,1)} %bitcast.42), calls=%async_computation.1 | async-start | bytes 50331648 | tf_op jit(solution)/shard_map/all_to_all | solution.py:40
  43.9 0.0 all-gather.11.cloned.1.call-start
  43.9 0.7 all-gather.11.cloned.1.call-update
  44.6 0.0 all-gather.9.cloned.1.call-start
  44.7 0.0 copy-done.1
  44.7 0.1 copy.40
  44.8 0.1 mul.48
  44.9 315.6 %all-to-all-done.1 = bf16[4,12,2,128,1024]{4,3,2,1,0:T(8,128)(2,1)} async-done(((bf16[4,12,2,128,1024]{4,3,2,1,0:T(8,128)(2,1)}), bf16[4,12,2,128,1024]{4,3,2,1,0:T(8,128)(2,1)}, u32[]{:S(2)}, u32[]{:S(2)}) %all-to-all-start.1) | async-done | bytes 25165856 | tf_op jit(solution)/shard_map/all_to_all | solution.py:40
  360.4 16.5 %gather_fusion.1 = bf16[32,2,128,1024]{3,2,1,0:T(8,128)(2,1)} fusion(bf16[48,2,128,1024]{3,2,1,0:T(8,128)(2,1)} %bitcast.4, s32[1024]{0:T(1024)S(1)} %pad_clamp_fusion), kind=kCustom, calls=%fused_computation.1 | custom fusion | bytes 33554560 | tf_op jit(solution)/shard_map/gather | solution.py:47
  377.0 11.9 %fusion.30 = (bf16[16,2,1,128,1024]{4,3,2,1,0:T(8,128)(2,1)}, bf16[16,2,1,128,1024]{4,3,2,1,0:T(8,128)(2,1)}) fusion(bf16[16,2,2,128,1024]{4,3,2,1,0:T(8,128)(2,1)} %bitcast.43), kind=kLoop, calls=%fused_computation.41 | loop fusion | bytes 33554432 | tf_op jit(solution)/shard_map/slice | solution.py:51
  388.9 8.8 %copy.51 = bf16[512,8,8,128]{3,2,1,0:T(8,128)(2,1)} copy(bf16[512,8,8,128]{3,1,2,0:T(8,128)(2,1)} %bitcast.47) | data formatting | bytes 16777216
  397.6 8.8 %copy.50 = bf16[512,8,8,128]{3,2,1,0:T(8,128)(2,1)} copy(bf16[512,8,8,128]{3,1,2,0:T(8,128)(2,1)} %bitcast.46) | data formatting | bytes 16777216
  406.4 0.0 all-gather.5.cloned.1.call-done
  406.4 7.2 fusion.1
  413.6 45.0 %all-gather.7.cloned.1.call-done = bf16[8192,1024]{1,0:T(8,128)(2,1)} async-done(((bf16[2048,1024]{1,0:T(8,128)(2,1)}), bf16[8192,1024]{1,0:T(8,128)(2,1)}) %all-gather.7.cloned.1.call-update) | async-done | bytes 16777232 | tf_op jit(solution)/shard_map/all_gather | solution.py:26
  458.6 0.0 copy-start
  458.6 23.2 %convert_bitcast_fusion.1 = bf16[128,8,8,128]{3,1,2,0:T(8,128)(2,1)S(1)} fusion(bf16[8192,1024]{1,0:T(8,128)(2,1)} %all-gather.7.cloned.1.call-done, bf16[1024,8192]{1,0:T(8,128)(2,1)} %all-gather.5.cloned.1.call-done, f32[1024]{0:T(1024)S(1)} %add_rsqrt_fusion), kind=kOutput, calls=%fused_computation.22 | convolution fusion | flops 17206083584 | bytes 35655680 | tf_op jit(solution)/shard_map/dot_general | solution.py:24
  481.9 0.6 copy.49
  482.5 0.0 copy-done
  482.5 6.2 fusion.8
  488.8 8.9 %fusion.31 = f32[16,8,64]{2,1,0:T(8,128)S(1)} fusion(f32[16,8,64,256]{3,2,1,0:T(8,128)} %fusion.8), kind=kOutput, calls=%fused_computation.42 | output fusion | flops 8388863 | bytes 8421376 | tf_op jit(solution)/shard_map/sub | solution.py:58
  497.7 20.7 %convert_bitcast_fusion = bf16[16,64,8,128]{3,1,2,0:T(8,128)(2,1)S(1)} fusion(bf16[16,256,8,128]{3,2,1,0:T(8,128)(2,1)} %bitcast.49, f32[16,8,64]{2,1,0:T(8,128)S(1)} %fusion.31, f32[16,8,64,256]{3,2,1,0:T(8,128)} %fusion.8), kind=kOutput, calls=%fused_computation.21 | convolution fusion | flops 548413696 | bytes 18907136 | tf_op jit(solution)/shard_map/chqk,ckhd->cqhd/dot_general | solution.py:60
  518.3 1.8 copy.46
  520.1 1.9 copy.62
  522.1 0.0 all-gather.9.cloned.1.call-update
  522.1 95.7 %all-gather.11.cloned.1.call-done = bf16[8192,1024]{1,0:T(8,128)(2,1)} async-done(((bf16[2048,1024]{1,0:T(8,128)(2,1)}), bf16[8192,1024]{1,0:T(8,128)(2,1)}) %all-gather.11.cloned.1.call-update) | async-done | bytes 16777232 | tf_op jit(solution)/shard_map/all_gather | solution.py:64
  617.8 150.1 %all-gather.9.cloned.1.call-done = bf16[1024,8192]{1,0:T(8,128)(2,1)} async-done(((bf16[1024,1024]{1,0:T(8,128)(2,1)}), bf16[1024,8192]{1,0:T(8,128)(2,1)}) %all-gather.9.cloned.1.call-update) | async-done | bytes 16777232 | tf_op jit(solution)/shard_map/all_gather | solution.py:66
  767.9 23.2 %convolution_convert_fusion = bf16[1024,1024]{1,0:T(8,128)(2,1)} fusion(bf16[1024,8192]{1,0:T(8,128)(2,1)} %all-gather.9.cloned.1.call-done, bf16[8192,1024]{1,0:T(8,128)(2,1)} %all-gather.11.cloned.1.call-done), kind=kOutput, calls=%fused_computation.23 | convolution fusion | flops 17180917760 | bytes 35651584 | tf_op jit(solution)/shard_map/dot_general | solution.py:65
  (7 shorter events, 0.0 us)
Async XLA Ops:
  6.5 399.9 %all-gather.5.cloned.1.call-start = ((), (), s32[]{:S(2)}) async-start(), calls=%async_computation.2 | async-start | bytes 18874368 | tf_op jit(solution)/shard_map/all_gather | solution.py:20
  7.3 451.4 %all-gather.7.cloned.1.call-start = ((), (), s32[]{:S(2)}) async-start(), calls=%async_computation.3 | async-start | bytes 20971520 | tf_op jit(solution)/shard_map/all_gather | solution.py:26
  35.2 9.5 %copy-start.1 = (s32[16,2]{0,1:T(2,128)S(1)}, s32[16,2]{0,1:T(2,128)}, u32[]{:S(2)}) copy-start(s32[16,2]{0,1:T(2,128)} %param.9) | copy-start | bytes 388
  35.2 325.2 %all-to-all-start.1 = ((bf16[4,12,2,128,1024]{4,3,2,1,0:T(8,128)(2,1)}), bf16[4,12,2,128,1024]{4,3,2,1,0:T(8,128)(2,1)}, u32[]{:S(2)}, u32[]{:S(2)}) async-start(bf16[4,12,2,128,1024]{4,3,2,1,0:T(8,128)(2,1)} %bitcast.42), calls=%async_computation.1 | async-start | bytes 50331648 | tf_op jit(solution)/shard_map/all_to_all | solution.py:40
  43.9 573.9 %all-gather.11.cloned.1.call-start = ((), (), s32[]{:S(2)}) async-start(), calls=%async_computation.5 | async-start | bytes 20971520 | tf_op jit(solution)/shard_map/all_gather | solution.py:64
  44.6 723.3 %all-gather.9.cloned.1.call-start = ((), (), s32[]{:S(2)}) async-start(), calls=%async_computation.4 | async-start | bytes 18874368 | tf_op jit(solution)/shard_map/all_gather | solution.py:66
  458.6 23.9 %copy-start = (bf16[512,8,8,128]{3,2,1,0:T(8,128)(2,1)S(1)}, bf16[512,8,8,128]{3,2,1,0:T(8,128)(2,1)}, u32[]{:S(2)}) copy-start(bf16[512,8,8,128]{3,2,1,0:T(8,128)(2,1)} %copy.50) | copy-start | bytes 25165828
Sparse Core Ops, SparseCore 0:
  8.9 149.4 all-gather.4
  160.2 298.3 all-gather.6
  460.5 157.2 all-gather.10
  619.3 148.6 all-gather.8
where the time goes:
time: 802 us; the launch traced here: 798 us
  waiting for transfers between devices  609 us (76%)
  matrix products  73.3 us (9%)
  local copies, waits for them, and re-layouts  70.5 us (9%)
  other arithmetic  16.5 us (2%)
  between operations  13.3 us (2%)
  starting transfers between devices  8.79 us (1%)
    all_to_all x1, waiting for transfers between devices, shards(): lax.all_to_all(stored[lax.all_to_all(table, 'dp', split_axis=0, concat_ax...  316 us
    all_gather x1, waiting for transfers between devices, shards(): lax.all_gather(attended, 'fsdp', axis=1, tiled=True)  150 us
    all_gather x1, waiting for transfers between devices, shards(): w_columns = lax.all_gather(w_output, 'dp', axis=0, tiled=True)  95.7 us
    all_gather x1, waiting for transfers between devices, shards(): lax.all_gather(w_query, 'dp', axis=0, tiled=True)  45 us
    dot_general x1, matrix products, shards(): jnp.dot(normed, lax.all_gather(w_query, 'dp', axis=0, tiled=True), prefer...  23.2 us
    dot_general x1, matrix products, shards(): jnp.dot(lax.all_gather(attended, 'fsdp', axis=1, tiled=True), w_columns,...  23.2 us
    unnamed x10, local copies, waits for them, and re-layouts  21.6 us
    dot_general x1, matrix products, shards(): jnp.einsum('chqk,ckhd->cqhd', weights, value_rows, preferred_element_type...  20.7 us
  transfers between devices with their start and end apart: 5, of which 4 were waited for; matrix products, arithmetic and copies ran while one was open for 17% of the time, Pallas kernels for 0%

commit v1 on v0

v1 whole, which is shorter than its diff:
```python
import functools

import jax
import jax.numpy as jnp
from jax import lax
from jax.experimental import pallas as pl
from jax.experimental.pallas import tpu as pltpu
from jax.sharding import PartitionSpec as P

HEAD_DIM = 128
NEIGH = 2
CHUNKS = 2

EPSILON = 1e-05


def normalize(features):
    widened = features.astype(jnp.float32)
    mean_square = jnp.mean(widened * widened, axis=1, keepdims=True)
    return (widened * lax.rsqrt(mean_square + EPSILON)).astype(jnp.bfloat16)


def pieces_over_fsdp(piece):
    members = lax.axis_size("fsdp")
    chips = members // 2
    me = lax.axis_index("fsdp")
    chip, core = me // 2, me % 2
    swap = [(i, i ^ 1) for i in range(members)]
    found = []
    for step in range(chips):
        if step == 0:
            here = piece
        else:
            shift = [(z * 2 + c, (z + step) % chips * 2 + c) for z in range(chips) for c in range(2)]
            here = lax.ppermute(piece, "fsdp", shift)
        there = lax.ppermute(here, "fsdp", swap)
        owner = (chip - step + chips) % chips
        found.append((owner * 2 + core, here))
        found.append((owner * 2 + 1 - core, there))
    return found


def pick_kernel(table_ref, stored_ref, *out_refs):
    width = out_refs[0].shape[-1]
    for number, out_ref in enumerate(out_refs):
        out_ref[...] = stored_ref[..., number * width:(number + 1) * width]


def pick_blocks(stored, table, chunks):
    count = table.shape[0]
    _, two, block_size, width = stored.shape
    part = width // chunks
    return pl.pallas_call(
        pick_kernel,
        grid_spec=pltpu.PrefetchScalarGridSpec(
            num_scalar_prefetch=1,
            grid=(count,),
            in_specs=[pl.BlockSpec((1, two, block_size, width), lambda i, t: (t[i], 0, 0, 0))],
            out_specs=[pl.BlockSpec((1, two, block_size, part), lambda i, t: (i, 0, 0, 0))] * chunks,
        ),
        out_shape=[jax.ShapeDtypeStruct((count, two, block_size, part), stored.dtype)] * chunks,
        cost_estimate=pl.CostEstimate(
            flops=0, transcendentals=0, bytes_accessed=count * two * block_size * width * 4
        ),
        name="pick",
    )(table, stored)


def attend_kernel(placed_ref, query_ref, *refs):
    block_refs, out_ref = refs[:-1], refs[-1]
    for head in range(out_ref.shape[1] // HEAD_DIM):
        columns = slice(head * HEAD_DIM, (head + 1) * HEAD_DIM)
        query = query_ref[:, columns]
        keys = jnp.concatenate([ref[0, 0, :, columns] for ref in block_refs], axis=0)
        values = jnp.concatenate([ref[0, 1, :, columns] for ref in block_refs], axis=0)
        scores = lax.dot_general(
            query, keys, (((1,), (1,)), ((), ())), preferred_element_type=jnp.float32
        ) * HEAD_DIM ** (-0.5)
        highest = jnp.max(scores, axis=-1, keepdims=True)
        raised = jnp.exp(scores - highest)
        weights = (raised / jnp.sum(raised, axis=-1, keepdims=True)).astype(jnp.bfloat16)
        mixed = jnp.dot(weights, values, preferred_element_type=jnp.float32)
        out_ref[:, columns] = mixed.astype(jnp.bfloat16)


def attend(queries, blocks, placed, span_count):
    rows, width = queries.shape
    span = rows // span_count
    _, two, block_size, _ = blocks.shape

    def block_spec(j):
        return pl.BlockSpec((1, two, block_size, width), lambda c, p, j=j: (p[c * NEIGH + j], 0, 0, 0))

    return pl.pallas_call(
        attend_kernel,
        grid_spec=pltpu.PrefetchScalarGridSpec(
            num_scalar_prefetch=1,
            grid=(span_count,),
            in_specs=[pl.BlockSpec((span, width), lambda c, p: (c, 0))] + [block_spec(j) for j in range(NEIGH)],
            out_specs=pl.BlockSpec((span, width), lambda c, p: (c, 0)),
        ),
        out_shape=jax.ShapeDtypeStruct((rows, width), jnp.bfloat16),
        cost_estimate=pl.CostEstimate(
            flops=4 * rows * NEIGH * block_size * width,
            transcendentals=rows * NEIGH * block_size * width // HEAD_DIM,
            bytes_accessed=span_count * NEIGH * two * block_size * width * 2 + rows * width * 4,
        ),
        name="attend",
    )(placed, queries, *[blocks] * NEIGH)


def shards(tokens, w_query, w_output, neighbor_shard, neighbor_block, kv_store):
    local_width = w_query.shape[1]
    row_count = tokens.shape[0]
    peers = lax.axis_size("dp")
    members = lax.axis_size("fsdp")
    chunks = CHUNKS if local_width % (CHUNKS * HEAD_DIM) == 0 else 1
    part = local_width // chunks

    w_query_columns = lax.all_gather(w_query, "dp", axis=0, tiled=True)
    w_output_columns = lax.all_gather(w_output, "dp", axis=0, tiled=True)

    span_count = neighbor_shard.shape[0]
    capacity = max(2, 3 * span_count * NEIGH // (2 * peers))
    owners = neighbor_shard.reshape(-1)
    wanted = neighbor_block.reshape(-1)
    owned = (owners[:, None] == jnp.arange(peers, dtype=jnp.int32)[None, :]).astype(jnp.int32)
    earlier = jnp.cumsum(owned, axis=0) - owned
    placed = owners * capacity + jnp.sum(earlier * owned, axis=1)
    matches = placed[:, None] == jnp.arange(peers * capacity, dtype=jnp.int32)[None, :]
    table = jnp.sum(jnp.where(matches, wanted[:, None], 0), axis=0).reshape(peers, capacity)
    asked = lax.all_to_all(table, "dp", split_axis=0, concat_axis=0, tiled=True)
    picked = pick_blocks(kv_store[0], asked.reshape(-1), chunks)
    replies = [
        lax.all_to_all(
            blocks.reshape((peers, capacity) + blocks.shape[1:]), "dp", split_axis=0, concat_axis=0, tiled=True
        ).reshape(blocks.shape)
        for blocks in picked
    ]

    width = tokens.shape[1]
    gathered = jnp.zeros((row_count, members * width), tokens.dtype)
    for owner, piece in pieces_over_fsdp(tokens):
        gathered = lax.dynamic_update_slice(gathered, piece, (0, owner * width))
    normed = normalize(gathered)
    queries = jnp.dot(normed, w_query_columns, preferred_element_type=jnp.float32).astype(jnp.bfloat16)

    attended = jnp.zeros((row_count, members * local_width), jnp.bfloat16)
    for chunk in range(chunks):
        mixed = attend(queries[:, chunk * part:(chunk + 1) * part], replies[chunk], placed, span_count)
        for owner, piece in pieces_over_fsdp(mixed):
            attended = lax.dynamic_update_slice(attended, piece, (0, owner * local_width + chunk * part))
    summed = jnp.dot(attended, w_output_columns, preferred_element_type=jnp.float32)
    return summed.astype(jnp.bfloat16)


def solution(mesh):
    in_specs = (
        P("dp", "fsdp"),
        P("dp", "fsdp"),
        P("dp", "fsdp"),
        P("dp", None),
        P("dp", None),
        P("dp", None, None, None, "fsdp"),
    )
    out_specs = P("dp", "fsdp")
    return jax.shard_map(shards, mesh=mesh, in_specs=in_specs, out_specs=out_specs, check_vma=False)
```

time: 802 us -> 684 us (0.85)
  waiting for transfers between devices: 609 us -> 399 us
  Pallas kernels: 0 us -> 85.5 us
  starting transfers between devices: 8.79 us -> 66.4 us
  matrix products: 73.3 us -> 46.1 us
  other arithmetic: 16.5 us -> 4.98 us
  local copies, waits for them, and re-layouts: 70.5 us -> 59.3 us
    all_gather x4 -> x2, waiting for transfers between devices: 291 us -> 99.5 us  [the longest x1 99.5 us: shards(): w_query_columns = lax.all_gather(w_query, 'dp', axis=0, tiled=True)]
    all_to_all x1 -> x2, waiting for transfers between devices: 316 us -> 158 us  [shards(): lax.all_to_all(blocks.reshape((peers, capacity) + blocks.shape[1:]), 'dp'...]
    ppermute x0 -> x21, waiting for transfers between devices: none -> 140 us  [the longest x9 140 us: pieces_over_fsdp(): here = lax.ppermute(piece, 'fsdp', shift)]
    pallas_call x0 -> x3, Pallas kernels: none -> 85.5 us  [the longest x2 51.1 us: attend(): pl.pallas_call(attend_kernel, grid_spec=pltpu.PrefetchScalarGridSpec(num_...]
    ppermute x0 -> x21, starting transfers between devices: none -> 53.6 us  [the longest x12 48.9 us: pieces_over_fsdp(): there = lax.ppermute(here, 'fsdp', swap)]
    dynamic_update_slice x0 -> x24, local copies, waits for them, and re-layouts: none -> 41.7 us  [the longest x16 28.4 us: shards(): lax.dynamic_update_slice(attended, piece, (0, owner * local_width + chunk...]
    gather x2 -> x0, local copies, waits for them, and re-layouts: 34.7 us -> none  [the longest x1 18.1 us: shards(): stored[lax.all_to_all(table, 'dp', split_axis=0, concat_axis=0, tiled=True)]]
    dot_general x4 -> x2, matrix products: 73.3 us -> 46.1 us  [the longest x1 23.2 us: shards(): jnp.dot(attended, w_output_columns, preferred_element_type=jnp.float32)]
  transfers between devices with their start and end apart: 5 -> 25, of which waited for: 4 -> 6; matrix products, arithmetic and copies ran while one was open for 17% -> 12% of each run, Pallas kernels for 0% -> 13%
where the time goes in v1:
time: 684 us; the launch traced here: 681 us
  waiting for transfers between devices  399 us (58%)
  Pallas kernels  85.5 us (12%)
  starting transfers between devices  66.4 us (10%)
  local copies, waits for them, and re-layouts  59.3 us (9%)
  matrix products  46.1 us (7%)
  between operations  13.6 us (2%)
    all_to_all x2, waiting for transfers between devices, shards(): lax.all_to_all(blocks.reshape((peers, capacity) + blocks.shape[1:]), 'dp'...  158 us
    ppermute x9, waiting for transfers between devices, pieces_over_fsdp(): here = lax.ppermute(piece, 'fsdp', shift)  140 us
    all_gather x1, waiting for transfers between devices, shards(): w_query_columns = lax.all_gather(w_query, 'dp', axis=0, tiled=True)  99.5 us
    pallas_call x2, Pallas kernels, attend(): pl.pallas_call(attend_kernel, grid_spec=pltpu.PrefetchScalarGridSpec(num_...  51.1 us
    ppermute x12, starting transfers between devices, pieces_over_fsdp(): there = lax.ppermute(here, 'fsdp', swap)  48.9 us
    pallas_call x1, Pallas kernels, pick_blocks(): pl.pallas_call(pick_kernel, grid_spec=pltpu.PrefetchScalarGridSpec(num_sc...  34.4 us
    dynamic_update_slice x16, local copies, waits for them, and re-layouts, shards(): lax.dynamic_update_slice(attended, piece, (0, owner * local_width + chunk...  28.4 us
    dot_general x1, matrix products, shards(): jnp.dot(attended, w_output_columns, preferred_element_type=jnp.float32)  23.2 us
  transfers between devices with their start and end apart: 25, of which 6 were waited for; matrix products, arithmetic and copies ran while one was open for 12% of the time, Pallas kernels for 13%

profile of v1, /device:TPU:25, one launch (start us, length us, event | category | flops | bytes accessed | tf_op | source)
XLA Modules:
  0.0 681.4 jit_solution(3540244764308623483)
XLA Ops:
  6.5 0.7 all-gather.3.cloned.1.call-update
  7.3 0.7 all-gather.5.cloned.1.call-update
  8.0 0.8 copy.14
  8.9 0.8 copy.15
  9.8 0.2 select_reduce_fusion.1
  10.2 6.8 all_to_all.19
  17.0 0.5 broadcast.33
  17.5 0.7 reduce.3
  18.2 0.6 reshape.42.table_ref
  18.8 34.4 %pick.1 = (bf16[48,2,128,512]{3,2,1,0:T(8,128)(2,1)}, bf16[48,2,128,512]{3,2,1,0:T(8,128)(2,1)}) custom-call(s32[48]{0:T(128)} %reshape.42.table_ref, bf16[32,2,128,1024]{3,2,1,0:T(8,128)(2,1)} %bitcast.9), custom_call_target="tpu_custom_call" | custom-call | bytes 50331648 | tf_op jit(solution)/shard_map/pick/pallas_call | solution.py:53
  53.2 6.4 all-to-all-start.1
  59.7 1.3 collective-permute-start.3
  61.1 2.9 collective-permute-start
  64.0 41.0 %collective-permute-done.1 = bf16[1024,1024]{1,0:T(8,128)(2,1)} collective-permute-done((bf16[1024,1024]{1,0:T(8,128)(2,1)S(1)}, bf16[1024,1024]{1,0:T(8,128)(2,1)}, u32[]{:S(2)}, u32[]{:S(2)}) %collective-permute-start.1) | collective-permute-done | bytes 2097184 | tf_op jit(solution)/shard_map/ppermute | solution.py:35
  105.0 3.6 collective-permute-start.2
  108.6 148.4 %all-to-all-done.1 = bf16[4,12,2,128,512]{4,3,2,1,0:T(8,128)(2,1)} async-done(((bf16[4,12,2,128,512]{4,3,2,1,0:T(8,128)(2,1)}), bf16[4,12,2,128,512]{4,3,2,1,0:T(8,128)(2,1)}, u32[]{:S(2)}, u32[]{:S(2)}) %all-to-all-start.1) | async-done | bytes 12582944 | tf_op jit(solution)/shard_map/all_to_all | solution.py:135
  257.0 6.3 all-to-all-start.2
  263.4 2.3 collective-permute-start.4
  265.7 1.6 broadcast.27.clone
  267.4 0.3 constant_dynamic-update-slice_fusion.22
  267.7 1.9 constant_dynamic-update-slice_fusion.21
  269.5 1.9 constant_dynamic-update-slice_fusion.20
  271.4 1.9 constant_dynamic-update-slice_fusion.19
  273.3 1.9 constant_dynamic-update-slice_fusion.18
  275.1 1.9 constant_dynamic-update-slice_fusion.17
  277.0 1.9 constant_dynamic-update-slice_fusion.16
  278.9 1.9 constant_dynamic-update-slice_fusion.15
  280.8 5.7 copy-done
  286.5 3.9 fusion
  290.4 99.5 %all-gather.3.cloned.1.call-done = bf16[8192,1024]{1,0:T(8,128)(2,1)} async-done(((bf16[2048,1024]{1,0:T(8,128)(2,1)}), bf16[8192,1024]{1,0:T(8,128)(2,1)}) %all-gather.3.cloned.1.call-update) | async-done | bytes 16777232 | tf_op jit(solution)/shard_map/all_gather | solution.py:120
  389.9 22.9 %fusion.5 = bf16[1024,1024]{1,0:T(8,128)(2,1)S(1)} fusion(bf16[8192,1024]{1,0:T(8,128)(2,1)} %all-gather.3.cloned.1.call-done, bf16[1024,8192]{1,0:T(8,128)(2,1)} %copy-done, f32[1024]{0:T(1024)S(1)} %add_rsqrt_fusion), kind=kOutput, calls=%fused_computation.6 | convolution fusion | flops 17206083584 | bytes 35655680 | tf_op jit(solution)/shard_map/dot_general | solution.py:146
  412.8 1.5 fusion.9
  414.2 25.5 %attend.2 = bf16[1024,512]{1,0:T(8,128)(2,1)} custom-call(s32[32]{0:T(128)} %copy-done.4, bf16[1024,512]{1,0:T(8,128)(2,1)} %get-tuple-element.10.query_ref, bf16[48,2,128,512]{3,2,1,0:T(8,128)(2,1)} %bitcast.3.refs_0_.refs_1_, bf16[48,2,128,512]{3,2,1,0:T(8,128)(2,1)} %bitcast.3.refs_0_.refs_1_), custom_call_target="tpu_custom_call" | custom-call | flops 536870912 | bytes 10485760 | tf_op jit(solution)/shard_map/attend/pallas_call | solution.py:94
  439.7 0.6 collective-permute-start.7
  440.5 1.3 collective-permute-start.10
  441.8 0.3 collective-permute-start.12
  442.0 9.8 %all-to-all-done.2 = bf16[4,12,2,128,512]{4,3,2,1,0:T(8,128)(2,1)} async-done(((bf16[4,12,2,128,512]{4,3,2,1,0:T(8,128)(2,1)}), bf16[4,12,2,128,512]{4,3,2,1,0:T(8,128)(2,1)}, u32[]{:S(2)}, u32[]{:S(2)}) %all-to-all-start.2) | async-done | bytes 12582944 | tf_op jit(solution)/shard_map/all_to_all | solution.py:135
  451.8 25.6 %attend.3 = bf16[1024,512]{1,0:T(8,128)(2,1)} custom-call(s32[32]{0:T(128)} %copy-done.4, bf16[1024,512]{1,0:T(8,128)(2,1)} %get-tuple-element.9.query_ref, bf16[48,2,128,512]{3,2,1,0:T(8,128)(2,1)} %bitcast.5.refs_0_.refs_1_, bf16[48,2,128,512]{3,2,1,0:T(8,128)(2,1)} %bitcast.5.refs_0_.refs_1_), custom_call_target="tpu_custom_call" | custom-call | flops 536870912 | bytes 10485760 | tf_op jit(solution)/shard_map/attend/pallas_call | solution.py:94
  477.4 0.2 collective-permute-start.15
  477.6 1.2 collective-permute-start.17
  478.9 3.0 collective-permute-start.9
  481.8 50.9 %collective-permute-done.10 = bf16[1024,512]{1,0:T(8,128)(2,1)} collective-permute-done((bf16[1024,512]{1,0:T(8,128)(2,1)}, bf16[1024,512]{1,0:T(8,128)(2,1)}, u32[]{:S(2)}, u32[]{:S(2)}) %collective-permute-start.10) | collective-permute-done | bytes 1048608 | tf_op jit(solution)/shard_map/ppermute | solution.py:35
  532.8 35.0 %collective-permute-start.11 = (bf16[1024,512]{1,0:T(8,128)(2,1)}, bf16[1024,512]{1,0:T(8,128)(2,1)}, u32[]{:S(2)}, u32[]{:S(2)}) collective-permute-start(bf16[1024,512]{1,0:T(8,128)(2,1)} %collective-permute-done.10), channel_id=1, source_target_pairs={{0,1},{1,0},{2,3},{3,2},{4,5},{5,4},{6,7},{7,6},{8,9},{9,8},{10,11... | collective-permute-start | bytes 3145736 | tf_op jit(solution)/shard_map/ppermute | solution.py:36
  567.9 5.9 broadcast.27
  573.9 1.1 constant_dynamic-update-slice_fusion.14
  574.9 47.6 %collective-permute-done.17 = bf16[1024,512]{1,0:T(8,128)(2,1)S(1)} collective-permute-done((bf16[1024,512]{1,0:T(8,128)(2,1)}, bf16[1024,512]{1,0:T(8,128)(2,1)S(1)}, u32[]{:S(2)}, u32[]{:S(2)}) %collective-permute-start.17) | collective-permute-done | bytes 1048608 | tf_op jit(solution)/shard_map/ppermute | solution.py:35
  622.6 0.9 collective-permute-start.14
  623.4 2.3 constant_dynamic-update-slice_fusion.13
  625.7 2.3 constant_dynamic-update-slice_fusion.12
  628.0 2.3 constant_dynamic-update-slice_fusion.11
  630.3 2.3 constant_dynamic-update-slice_fusion.10
  632.6 0.5 collective-permute-start.18
  633.2 2.3 constant_dynamic-update-slice_fusion.9
  635.4 2.3 constant_dynamic-update-slice_fusion.8
  637.8 2.3 constant_dynamic-update-slice_fusion.7
  640.1 1.1 constant_dynamic-update-slice_fusion.6
  641.2 1.1 constant_dynamic-update-slice_fusion.5
  642.3 2.3 constant_dynamic-update-slice_fusion.4
  644.6 1.0 constant_dynamic-update-slice_fusion.3
  645.6 1.1 constant_dynamic-update-slice_fusion.2
  646.8 1.1 constant_dynamic-update-slice_fusion.1
  647.9 2.4 constant_dynamic-update-slice_fusion
  650.2 1.1 constant_dynamic-update-slice_fusion.23
  651.3 23.2 %convolution_convert_fusion = bf16[1024,1024]{1,0:T(8,128)(2,1)} fusion(bf16[1024,8192]{1,0:T(8,128)(2,1)} %constant_dynamic-update-slice_fusion.23, bf16[8192,1024]{1,0:T(8,128)(2,1)} %all-gather.5.cloned.1.call-done), kind=kOutput, calls=%fused_computation.7 | convolution fusion | flops 17180917760 | bytes 35651584 | tf_op jit(solution)/shard_map/dot_general | solution.py:153
  (46 shorter events, 1.2 us)
Async XLA Ops:
  6.5 383.4 %all-gather.3.cloned.1.call-start = ((), (), s32[]{:S(2)}) async-start(), calls=%async_computation.3 | async-start | bytes 20971520 | tf_op jit(solution)/shard_map/all_gather | solution.py:120
  7.3 644.1 %all-gather.5.cloned.1.call-start = ((), (), s32[]{:S(2)}) async-start(), calls=%async_computation.4 | async-start | bytes 20971520 | tf_op jit(solution)/shard_map/all_gather | solution.py:121
  10.0 43.1 %copy-start.4 = (s32[32]{0:T(128)}, s32[32]{0:T(128)S(1)}, u32[]{:S(2)}) copy-start(s32[32]{0:T(128)S(1)} %multiply_add_fusion.placed_ref) | copy-start | bytes 388
  53.2 6.4 copy-start.3
  53.2 203.9 %all-to-all-start.1 = ((bf16[4,12,2,128,512]{4,3,2,1,0:T(8,128)(2,1)}), bf16[4,12,2,128,512]{4,3,2,1,0:T(8,128)(2,1)}, u32[]{:S(2)}, u32[]{:S(2)}) async-start(bf16[4,12,2,128,512]{4,3,2,1,0:T(8,128)(2,1)} %bitcast.11), calls=%async_computation.1 | async-start | bytes 25165824 | tf_op jit(solution)/shard_map/all_to_all | solution.py:135
  59.6 45.4 %collective-permute-start.1 = (bf16[1024,1024]{1,0:T(8,128)(2,1)S(1)}, bf16[1024,1024]{1,0:T(8,128)(2,1)}, u32[]{:S(2)}, u32[]{:S(2)}) collective-permute-start(bf16[1024,1024]{1,0:T(8,128)(2,1)S(1)} %copy-done.3), channel_id=1, source_target_pairs={{0,2},{1,3},{2,4},{3,5},{4,6},{5,7},{6,0},{7,1},{8,10},{9,11},{10,... | collective-permute-start | bytes 6291464 | tf_op jit(solution)/shard_map/ppermute | solution.py:35
  59.7 203.7 %collective-permute-start.3 = (bf16[1024,1024]{1,0:T(8,128)(2,1)S(1)}, bf16[1024,1024]{1,0:T(8,128)(2,1)}, u32[]{:S(2)}, u32[]{:S(2)}) collective-permute-start(bf16[1024,1024]{1,0:T(8,128)(2,1)S(1)} %copy-done.3), channel_id=1, source_target_pairs={{0,4},{1,5},{2,6},{3,7},{4,0},{5,1},{6,2},{7,3},{8,12},{9,13},{10,... | collective-permute-start | bytes 6291464 | tf_op jit(solution)/shard_map/ppermute | solution.py:35
  61.0 204.7 %collective-permute-start.5 = (bf16[1024,1024]{1,0:T(8,128)(2,1)S(1)}, bf16[1024,1024]{1,0:T(8,128)(2,1)}, u32[]{:S(2)}, u32[]{:S(2)}) collective-permute-start(bf16[1024,1024]{1,0:T(8,128)(2,1)S(1)} %copy-done.3), channel_id=1, source_target_pairs={{0,6},{1,7},{2,0},{3,1},{4,2},{5,3},{6,4},{7,5},{8,14},{9,15},{10,... | collective-permute-start | bytes 6291464 | tf_op jit(solution)/shard_map/ppermute | solution.py:35
  61.1 206.5 %collective-permute-start = (bf16[1024,1024]{1,0:T(8,128)(2,1)S(1)}, bf16[1024,1024]{1,0:T(8,128)(2,1)}, u32[]{:S(2)}, u32[]{:S(2)}) collective-permute-start(bf16[1024,1024]{1,0:T(8,128)(2,1)S(1)} %copy-done.3), channel_id=1, source_target_pairs={{0,1},{1,0},{2,3},{3,2},{4,5},{5,4},{6,7},{7,6},{8,9},{9,8},{10,11... | collective-permute-start | bytes 6291464 | tf_op jit(solution)/shard_map/ppermute | solution.py:36
  105.0 166.4 %collective-permute-start.2 = (bf16[1024,1024]{1,0:T(8,128)(2,1)}, bf16[1024,1024]{1,0:T(8,128)(2,1)}, u32[]{:S(2)}, u32[]{:S(2)}) collective-permute-start(bf16[1024,1024]{1,0:T(8,128)(2,1)} %collective-permute-done.1), channel_id=1, source_target_pairs={{0,1},{1,0},{2,3},{3,2},{4,5},{5,4},{6,7},{7,6},{8,9},{9,8},{10,11... | collective-permute-start | bytes 6291464 | tf_op jit(solution)/shard_map/ppermute | solution.py:36
  257.0 194.8 %all-to-all-start.2 = ((bf16[4,12,2,128,512]{4,3,2,1,0:T(8,128)(2,1)}), bf16[4,12,2,128,512]{4,3,2,1,0:T(8,128)(2,1)}, u32[]{:S(2)}, u32[]{:S(2)}) async-start(bf16[4,12,2,128,512]{4,3,2,1,0:T(8,128)(2,1)} %bitcast.10), calls=%async_computation.2 | async-start | bytes 25165824 | tf_op jit(solution)/shard_map/all_to_all | solution.py:135
  263.4 11.8 %collective-permute-start.4 = (bf16[1024,1024]{1,0:T(8,128)(2,1)}, bf16[1024,1024]{1,0:T(8,128)(2,1)}, u32[]{:S(2)}, u32[]{:S(2)}) collective-permute-start(bf16[1024,1024]{1,0:T(8,128)(2,1)} %collective-permute-done.3), channel_id=1, source_target_pairs={{0,1},{1,0},{2,3},{3,2},{4,5},{5,4},{6,7},{7,6},{8,9},{9,8},{10,11... | collective-permute-start | bytes 6291464 | tf_op jit(solution)/shard_map/ppermute | solution.py:36
  265.6 13.2 %collective-permute-start.6 = (bf16[1024,1024]{1,0:T(8,128)(2,1)}, bf16[1024,1024]{1,0:T(8,128)(2,1)}, u32[]{:S(2)}, u32[]{:S(2)}) collective-permute-start(bf16[1024,1024]{1,0:T(8,128)(2,1)} %collective-permute-done.5), channel_id=1, source_target_pairs={{0,1},{1,0},{2,3},{3,2},{4,5},{5,4},{6,7},{7,6},{8,9},{9,8},{10,11... | collective-permute-start | bytes 6291464 | tf_op jit(solution)/shard_map/ppermute | solution.py:36
  280.7 5.7 copy-start
  439.7 37.9 %collective-permute-start.7 = (bf16[1024,512]{1,0:T(8,128)(2,1)}, bf16[1024,512]{1,0:T(8,128)(2,1)}, u32[]{:S(2)}, u32[]{:S(2)}) collective-permute-start(bf16[1024,512]{1,0:T(8,128)(2,1)} %attend.2), channel_id=1, source_target_pairs={{0,1},{1,0},{2,3},{3,2},{4,5},{5,4},{6,7},{7,6},{8,9},{9,8},{10,11... | collective-permute-start | bytes 3145736 | tf_op jit(solution)/shard_map/ppermute | solution.py:36
  440.3 38.6 %collective-permute-start.8 = (bf16[1024,512]{1,0:T(8,128)(2,1)}, bf16[1024,512]{1,0:T(8,128)(2,1)}, u32[]{:S(2)}, u32[]{:S(2)}) collective-permute-start(bf16[1024,512]{1,0:T(8,128)(2,1)} %attend.2), channel_id=1, source_target_pairs={{0,2},{1,3},{2,4},{3,5},{4,6},{5,7},{6,0},{7,1},{8,10},{9,11},{10,... | collective-permute-start | bytes 3145736 | tf_op jit(solution)/shard_map/ppermute | solution.py:35
  440.5 92.3 %collective-permute-start.10 = (bf16[1024,512]{1,0:T(8,128)(2,1)}, bf16[1024,512]{1,0:T(8,128)(2,1)}, u32[]{:S(2)}, u32[]{:S(2)}) collective-permute-start(bf16[1024,512]{1,0:T(8,128)(2,1)} %attend.2), channel_id=1, source_target_pairs={{0,4},{1,5},{2,6},{3,7},{4,0},{5,1},{6,2},{7,3},{8,12},{9,13},{10,... | collective-permute-start | bytes 3145736 | tf_op jit(solution)/shard_map/ppermute | solution.py:35
  441.8 91.0 %collective-permute-start.12 = (bf16[1024,512]{1,0:T(8,128)(2,1)}, bf16[1024,512]{1,0:T(8,128)(2,1)}, u32[]{:S(2)}, u32[]{:S(2)}) collective-permute-start(bf16[1024,512]{1,0:T(8,128)(2,1)} %attend.2), channel_id=1, source_target_pairs={{0,6},{1,7},{2,0},{3,1},{4,2},{5,3},{6,4},{7,5},{8,14},{9,15},{10,... | collective-permute-start | bytes 3145736 | tf_op jit(solution)/shard_map/ppermute | solution.py:35
  451.8 122.1 %copy-start.2 = (bf16[1024,512]{1,0:T(8,128)(2,1)S(1)}, bf16[1024,512]{1,0:T(8,128)(2,1)}, u32[]{:S(2)}) copy-start(bf16[1024,512]{1,0:T(8,128)(2,1)} %attend.2) | copy-start | bytes 3145732
  477.4 145.1 %copy-start.1 = (bf16[1024,512]{1,0:T(8,128)(2,1)S(1)}, bf16[1024,512]{1,0:T(8,128)(2,1)}, u32[]{:S(2)}) copy-start(bf16[1024,512]{1,0:T(8,128)(2,1)} %attend.3) | copy-start | bytes 3145732
  477.4 90.4 %collective-permute-start.15 = (bf16[1024,512]{1,0:T(8,128)(2,1)}, bf16[1024,512]{1,0:T(8,128)(2,1)}, u32[]{:S(2)}, u32[]{:S(2)}) collective-permute-start(bf16[1024,512]{1,0:T(8,128)(2,1)} %attend.3), channel_id=1, source_target_pairs={{0,2},{1,3},{2,4},{3,5},{4,6},{5,7},{6,0},{7,1},{8,10},{9,11},{10,... | collective-permute-start | bytes 3145736 | tf_op jit(solution)/shard_map/ppermute | solution.py:35
  477.6 144.9 %collective-permute-start.17 = (bf16[1024,512]{1,0:T(8,128)(2,1)}, bf16[1024,512]{1,0:T(8,128)(2,1)S(1)}, u32[]{:S(2)}, u32[]{:S(2)}) collective-permute-start(bf16[1024,512]{1,0:T(8,128)(2,1)} %attend.3), channel_id=1, source_target_pairs={{0,4},{1,5},{2,6},{3,7},{4,0},{5,1},{6,2},{7,3},{8,12},{9,13},{10,... | collective-permute-start | bytes 3145736 | tf_op jit(solution)/shard_map/ppermute | solution.py:35
  478.9 149.1 %collective-permute-start.9 = (bf16[1024,512]{1,0:T(8,128)(2,1)}, bf16[1024,512]{1,0:T(8,128)(2,1)}, u32[]{:S(2)}, u32[]{:S(2)}) collective-permute-start(bf16[1024,512]{1,0:T(8,128)(2,1)} %collective-permute-done.8), channel_id=1, source_target_pairs={{0,1},{1,0},{2,3},{3,2},{4,5},{5,4},{6,7},{7,6},{8,9},{9,8},{10,11... | collective-permute-start | bytes 3145736 | tf_op jit(solution)/shard_map/ppermute | solution.py:36
  532.8 99.8 %collective-permute-start.19 = (bf16[1024,512]{1,0:T(8,128)(2,1)}, bf16[1024,512]{1,0:T(8,128)(2,1)}, u32[]{:S(2)}, u32[]{:S(2)}) collective-permute-start(bf16[1024,512]{1,0:T(8,128)(2,1)} %attend.3), channel_id=1, source_target_pairs={{0,6},{1,7},{2,0},{3,1},{4,2},{5,3},{6,4},{7,5},{8,14},{9,15},{10,... | collective-permute-start | bytes 3145736 | tf_op jit(solution)/shard_map/ppermute | solution.py:35
  532.8 100.3 %collective-permute-start.11 = (bf16[1024,512]{1,0:T(8,128)(2,1)}, bf16[1024,512]{1,0:T(8,128)(2,1)}, u32[]{:S(2)}, u32[]{:S(2)}) collective-permute-start(bf16[1024,512]{1,0:T(8,128)(2,1)} %collective-permute-done.10), channel_id=1, source_target_pairs={{0,1},{1,0},{2,3},{3,2},{4,5},{5,4},{6,7},{7,6},{8,9},{9,8},{10,11... | collective-permute-start | bytes 3145736 | tf_op jit(solution)/shard_map/ppermute | solution.py:36
  567.8 70.0 %collective-permute-start.13 = (bf16[1024,512]{1,0:T(8,128)(2,1)}, bf16[1024,512]{1,0:T(8,128)(2,1)}, u32[]{:S(2)}, u32[]{:S(2)}) collective-permute-start(bf16[1024,512]{1,0:T(8,128)(2,1)} %collective-permute-done.12), channel_id=1, source_target_pairs={{0,1},{1,0},{2,3},{3,2},{4,5},{5,4},{6,7},{7,6},{8,9},{9,8},{10,11... | collective-permute-start | bytes 3145736 | tf_op jit(solution)/shard_map/ppermute | solution.py:36
  622.6 18.7 %collective-permute-start.14 = (bf16[1024,512]{1,0:T(8,128)(2,1)S(1)}, bf16[1024,512]{1,0:T(8,128)(2,1)S(1)}, u32[]{:S(2)}, u32[]{:S(2)}) collective-permute-start(bf16[1024,512]{1,0:T(8,128)(2,1)S(1)} %copy-done.1), channel_id=1, source_target_pairs={{0,1},{1,0},{2,3},{3,2},{4,5},{5,4},{6,7},{7,6},{8,9},{9,8},{10,11... | collective-permute-start | bytes 3145736 | tf_op jit(solution)/shard_map/ppermute | solution.py:36
  628.0 16.6 %collective-permute-start.16 = (bf16[1024,512]{1,0:T(8,128)(2,1)}, bf16[1024,512]{1,0:T(8,128)(2,1)S(1)}, u32[]{:S(2)}, u32[]{:S(2)}) collective-permute-start(bf16[1024,512]{1,0:T(8,128)(2,1)} %collective-permute-done.15), channel_id=1, source_target_pairs={{0,1},{1,0},{2,3},{3,2},{4,5},{5,4},{6,7},{7,6},{8,9},{9,8},{10,11... | collective-permute-start | bytes 3145736 | tf_op jit(solution)/shard_map/ppermute | solution.py:36
  632.6 14.2 %collective-permute-start.18 = (bf16[1024,512]{1,0:T(8,128)(2,1)S(1)}, bf16[1024,512]{1,0:T(8,128)(2,1)S(1)}, u32[]{:S(2)}, u32[]{:S(2)}) collective-permute-start(bf16[1024,512]{1,0:T(8,128)(2,1)S(1)} %collective-permute-done.17), channel_id=1, source_target_pairs={{0,1},{1,0},{2,3},{3,2},{4,5},{5,4},{6,7},{7,6},{8,9},{9,8},{10,11... | collective-permute-start | bytes 3145736 | tf_op jit(solution)/shard_map/ppermute | solution.py:36
  633.1 17.1 %collective-permute-start.20 = (bf16[1024,512]{1,0:T(8,128)(2,1)}, bf16[1024,512]{1,0:T(8,128)(2,1)S(1)}, u32[]{:S(2)}, u32[]{:S(2)}) collective-permute-start(bf16[1024,512]{1,0:T(8,128)(2,1)} %collective-permute-done.19), channel_id=1, source_target_pairs={{0,1},{1,0},{2,3},{3,2},{4,5},{5,4},{6,7},{7,6},{8,9},{9,8},{10,11... | collective-permute-start | bytes 3145736 | tf_op jit(solution)/shard_map/ppermute | solution.py:36
Sparse Core Ops, SparseCore 0:
  9.2 380.6 all-gather.2
  391.7 180.1 all-gather.4

commit v2 on v1

v2 whole, which is shorter than its diff:
```python
import functools

import jax
import jax.numpy as jnp
from jax import lax
from jax.experimental import pallas as pl
from jax.experimental.pallas import tpu as pltpu
from jax.sharding import PartitionSpec as P

HEAD_DIM = 128
NEIGH = 2
AXES = 2
LANES = 128
ABSENT = -1e30

EPSILON = 1e-05


def normalize(features):
    widened = features.astype(jnp.float32)
    mean_square = jnp.mean(widened * widened, axis=1, keepdims=True)
    return (widened * lax.rsqrt(mean_square + EPSILON)).astype(jnp.bfloat16)


def over_dp(value, bit):
    return lax.ppermute(value, "dp", [(i, i ^ bit) for i in range(lax.axis_size("dp"))])


def pieces_over_fsdp(piece):
    members = lax.axis_size("fsdp")
    chips = members // 2
    if chips != 4:
        whole = lax.all_gather(piece, "fsdp", axis=0)
        return [(i, whole[i]) for i in range(members)]
    me = lax.axis_index("fsdp")
    chip, core = me // 2, me % 2

    def chip_pairs(pairs):
        return [(a * 2 + c, b * 2 + c) for a, b in pairs for c in range(2)]

    back1 = lax.ppermute(piece, "fsdp", chip_pairs([(0, 1), (1, 2), (2, 3)]))
    back3 = lax.ppermute(piece, "fsdp", chip_pairs([(1, 0), (2, 1), (3, 2)]))
    back2 = lax.ppermute(piece, "fsdp", chip_pairs([(0, 2), (1, 3), (2, 0), (3, 1)]))
    ends = lax.ppermute(back2, "fsdp", chip_pairs([(2, 3), (1, 0)]))
    back1 = jnp.where(chip == 0, ends, back1)
    back3 = jnp.where(chip == 3, ends, back3)
    found = []
    for step, here in enumerate((piece, back1, back2, back3)):
        there = lax.ppermute(here, "fsdp", [(i, i ^ 1) for i in range(members)])
        owner = (chip + 4 - step) % 4
        found.append((owner * 2 + core, here))
        found.append((owner * 2 + 1 - core, there))
    return found


def pick_kernel(first_ref, second_ref, *refs):
    for axis in range(AXES):
        refs[AXES + axis][...] = refs[axis][...]


def pick_blocks(stored, tables, step, part):
    count = tables[0].shape[0]
    _, two, block_size, _ = stored.shape
    shape = (1, two, block_size, part)
    return pl.pallas_call(
        pick_kernel,
        grid_spec=pltpu.PrefetchScalarGridSpec(
            num_scalar_prefetch=AXES,
            grid=(count,),
            in_specs=[
                pl.BlockSpec(shape, lambda i, *t, axis=axis: (t[axis][i], 0, 0, step * AXES + axis))
                for axis in range(AXES)
            ],
            out_specs=[pl.BlockSpec(shape, lambda i, *t: (i, 0, 0, 0))] * AXES,
        ),
        out_shape=[jax.ShapeDtypeStruct((count,) + shape[1:], stored.dtype)] * AXES,
        cost_estimate=pl.CostEstimate(
            flops=0, transcendentals=0, bytes_accessed=count * two * block_size * part * 4 * AXES
        ),
        name="pick",
    )(*tables, *[stored] * AXES)


def scores_of(query, keys, present):
    scores = lax.dot_general(
        query, keys, (((1,), (1,)), ((), ())), preferred_element_type=jnp.float32
    ) * HEAD_DIM ** (-0.5)
    return jnp.where(present == 1, scores, ABSENT)


def head_columns(head):
    return slice(head * HEAD_DIM, (head + 1) * HEAD_DIM)


def presence(index_refs, axis):
    entry = pl.program_id(0) * pl.num_programs(1) + pl.program_id(1)
    here_at, far_at = index_refs[axis * 2], index_refs[axis * 2 + 1]
    return here_at[entry] >= 0, far_at[entry] >= 0


def all_scores(index_refs, query_refs, here_refs, far_refs):
    found = []
    for axis in range(AXES):
        has_here, has_far = presence(index_refs, axis)
        for head in range(query_refs[axis].shape[1] // HEAD_DIM):
            columns = head_columns(head)
            query = query_refs[axis][:, columns]
            found.append((
                axis,
                head,
                scores_of(query, here_refs[axis][0, 0, :, columns], has_here.astype(jnp.int32)),
                scores_of(query, far_refs[axis][0, 0, :, columns], has_far.astype(jnp.int32)),
            ))
    return found


def stats_kernel(*refs):
    index_refs, refs = refs[:2 * AXES], refs[2 * AXES:]
    query_refs, here_refs, far_refs, out_refs = (refs[i * AXES:(i + 1) * AXES] for i in range(4))
    span = pl.program_id(1)

    @pl.when(span == 0)
    def _():
        for out_ref in out_refs:
            out_ref[...] = jnp.zeros_like(out_ref)

    found = all_scores(index_refs, query_refs, here_refs, far_refs)
    highest = [jnp.max(jnp.maximum(here, far), axis=-1, keepdims=True) for _, _, here, far in found]
    totals = [
        jnp.sum(jnp.exp(here - top) + jnp.exp(far - top), axis=-1, keepdims=True)
        for (_, _, here, far), top in zip(found, highest)
    ]
    heads = len(found) // AXES
    lane = lax.broadcasted_iota(jnp.int32, out_refs[0].shape[1:], 1)
    for axis in range(AXES):
        kept = out_refs[axis][0]
        for head in range(heads):
            at = (span * heads + head) * 2
            kept = jnp.where(lane == at, highest[axis * heads + head], kept)
            kept = jnp.where(lane == at + 1, totals[axis * heads + head], kept)
        out_refs[axis][0] = kept


def mix_kernel(*refs):
    index_refs, refs = refs[:2 * AXES], refs[2 * AXES:]
    query_refs, here_refs, far_refs, mine_refs, their_refs, out_refs = (
        refs[i * AXES:(i + 1) * AXES] for i in range(6)
    )
    span = pl.program_id(1)
    found = all_scores(index_refs, query_refs, here_refs, far_refs)
    heads = len(found) // AXES
    lane = lax.broadcasted_iota(jnp.int32, mine_refs[0].shape[1:], 1)

    def column(stats, at):
        return jnp.sum(jnp.where(lane == at, stats, 0.0), axis=-1, keepdims=True)

    scales = []
    for axis in range(AXES):
        mine, theirs = mine_refs[axis][0], their_refs[axis][0]
        for head in range(heads):
            at = (span * heads + head) * 2
            my_top, their_top = column(mine, at), column(theirs, at)
            top = jnp.maximum(my_top, their_top)
            total = column(mine, at + 1) * jnp.exp(my_top - top) + column(theirs, at + 1) * jnp.exp(their_top - top)
            scales.append((top, 1.0 / total))
    weights = [
        jnp.concatenate([jnp.exp(here - top) * scale, jnp.exp(far - top) * scale], axis=1).astype(jnp.bfloat16)
        for (_, _, here, far), (top, scale) in zip(found, scales)
    ]
    for (axis, head, _, _), weight in zip(found, weights):
        columns = head_columns(head)
        values = jnp.concatenate([here_refs[axis][0, 1, :, columns], far_refs[axis][0, 1, :, columns]], axis=0)
        out_refs[axis][0, :, columns] = jnp.dot(weight, values, preferred_element_type=jnp.float32)


def span_call(kernel, indices, queries, stored, received, stats, step, part, spans, planes, out_block, out_index, out_shape, name):
    rows = queries[0].shape[0]
    span = rows // (2 * spans)
    block_size = stored.shape[2]

    def at(c, i):
        return c * spans + i

    in_specs = [pl.BlockSpec((span, part), lambda c, i, *t: (at(c, i), 0))] * AXES
    in_specs += [
        pl.BlockSpec(
            (1, planes, block_size, part),
            lambda c, i, *t, axis=axis: (jnp.maximum(t[axis * 2][at(c, i)], 0), 0, 0, step * AXES + axis),
        )
        for axis in range(AXES)
    ]
    in_specs += [
        pl.BlockSpec(
            (1, planes, block_size, part),
            lambda c, i, *t, axis=axis: (jnp.maximum(t[axis * 2 + 1][at(c, i)], 0), 0, 0, 0),
        )
        for axis in range(AXES)
    ]
    if stats:
        in_specs += [pl.BlockSpec((1, span, LANES), lambda c, i, *t: (c, 0, 0))] * AXES
        in_specs += [pl.BlockSpec((1, span, LANES), lambda c, i, *t: (1 - c, 0, 0))] * AXES
    return pl.pallas_call(
        kernel,
        grid_spec=pltpu.PrefetchScalarGridSpec(
            num_scalar_prefetch=2 * AXES,
            grid=(2, spans),
            in_specs=in_specs,
            out_specs=[pl.BlockSpec(out_block, out_index)] * AXES,
        ),
        out_shape=[jax.ShapeDtypeStruct(out_shape, jnp.float32)] * AXES,
        cost_estimate=pl.CostEstimate(
            flops=4 * rows * NEIGH * block_size * part * AXES * planes,
            transcendentals=rows * NEIGH * block_size * part * AXES // HEAD_DIM,
            bytes_accessed=2 * spans * NEIGH * planes * block_size * part * 2 * AXES,
        ),
        name=name,
    )(*indices, *queries, *[stored] * AXES, *received, *stats)


def exchange_tables(neighbor_shard, neighbor_block, capacity):
    me = lax.axis_index("dp")
    both = jnp.concatenate([neighbor_shard, neighbor_block], axis=1)
    groups = jnp.stack([both] + [over_dp(both, bit) for bit in (1, 2, 3)])
    spans = both.shape[0]
    owners = groups[:, :, :NEIGH].reshape(4, spans * NEIGH)
    wanted = groups[:, :, NEIGH:].reshape(4, spans * NEIGH)
    order = jnp.arange(spans * NEIGH, dtype=jnp.int32)
    same = (owners[:, :, None] == owners[:, None, :]) & (order[None, None, :] < order[None, :, None])
    rank = jnp.sum(same.astype(jnp.int32), axis=2)
    slots = jnp.arange(capacity, dtype=jnp.int32)
    hit = (owners == me)[:, :, None] & (rank[:, :, None] == slots[None, None, :])
    table = jnp.sum(jnp.where(hit, wanted[:, :, None], 0), axis=1)
    sends, places = [], []
    for axis in range(AXES):
        near = 1 << axis
        partner = 3 ^ near
        sends.append(jnp.concatenate([table[near], table[3]]))
        here, far = [], []
        for position, group in enumerate((0, partner)):
            mine = (owners[group] == me).reshape(spans, NEIGH)
            other = (owners[group] == me ^ near).reshape(spans, NEIGH)
            block = wanted[group].reshape(spans, NEIGH)
            slot = rank[group].reshape(spans, NEIGH) + position * capacity
            here.append(jnp.max(jnp.where(mine, block, -1), axis=1))
            far.append(jnp.max(jnp.where(other, slot, -1), axis=1))
        places += [jnp.concatenate(here), jnp.concatenate(far)]
    return sends, places


def shards(tokens, w_query, w_output, neighbor_shard, neighbor_block, kv_store):
    local_width = w_query.shape[1]
    row_count, width = tokens.shape
    peers = lax.axis_size("dp")
    members = lax.axis_size("fsdp")
    passes = 2 if local_width % (2 * AXES * HEAD_DIM) == 0 else 1
    part = local_width // (passes * AXES)
    span_count = neighbor_shard.shape[0]
    span = row_count // span_count
    capacity = max(2, 3 * span_count * NEIGH // (2 * peers))

    w_query_columns = lax.all_gather(w_query, "dp", axis=0, tiled=True)

    sends, places = exchange_tables(neighbor_shard, neighbor_block, capacity)
    stored = kv_store[0]
    received = []
    for step in range(passes):
        picked = pick_blocks(stored, sends, step, part)
        received.append([over_dp(picked[axis], 1 << axis) for axis in range(AXES)])

    w_output, _ = lax.optimization_barrier((w_output, received[-1]))
    w_output_columns = lax.all_gather(w_output, "dp", axis=0, tiled=True)

    gathered = jnp.zeros((row_count, members * width), tokens.dtype)
    for owner, piece in pieces_over_fsdp(tokens):
        gathered = lax.dynamic_update_slice(gathered, piece, (0, owner * width))
    normed = normalize(gathered)
    queries = jnp.dot(normed, w_query_columns, preferred_element_type=jnp.float32).astype(jnp.bfloat16)

    attended = jnp.zeros((row_count, members * local_width), jnp.bfloat16)
    for step in range(passes):
        asked = []
        for axis in range(AXES):
            start = (step * AXES + axis) * part
            own = queries[:, start:start + part]
            asked.append(jnp.concatenate([own, over_dp(own, 3 ^ (1 << axis))], axis=0))
        common = dict(step=step, part=part, spans=span_count)
        mine = span_call(
            stats_kernel, places, asked, stored, received[step], [], planes=1,
            out_block=(1, span, LANES), out_index=lambda c, i, *t: (c, 0, 0),
            out_shape=(2, span, LANES), name="stats", **common,
        )
        theirs = [over_dp(mine[axis], 3 ^ (1 << axis)) for axis in range(AXES)]
        partial = span_call(
            mix_kernel, places, asked, stored, received[step], list(mine) + theirs, planes=2,
            out_block=(1, span, part), out_index=lambda c, i, *t: (c, i, 0),
            out_shape=(2, row_count, part), name="mix", **common,
        )
        mixed = jnp.concatenate(
            [
                (partial[axis][0] + over_dp(partial[axis][1], 3 ^ (1 << axis))).astype(jnp.bfloat16)
                for axis in range(AXES)
            ],
            axis=1,
        )
        for owner, piece in pieces_over_fsdp(mixed):
            start = owner * local_width + step * AXES * part
            attended = lax.dynamic_update_slice(attended, piece, (0, start))
    summed = jnp.dot(attended, w_output_columns, preferred_element_type=jnp.float32)
    return summed.astype(jnp.bfloat16)


def solution(mesh):
    in_specs = (
        P("dp", "fsdp"),
        P("dp", "fsdp"),
        P("dp", "fsdp"),
        P("dp", None),
        P("dp", None),
        P("dp", None, None, None, "fsdp"),
    )
    out_specs = P("dp", "fsdp")
    return jax.shard_map(shards, mesh=mesh, in_specs=in_specs, out_specs=out_specs, check_vma=False)
```

time: 684 us -> 832 us (1.22)
  waiting for transfers between devices: 399 us -> 484 us
  Pallas kernels: 85.5 us -> 133 us
  other arithmetic: 4.98 us -> 40 us
  starting transfers between devices: 66.4 us -> 42.1 us
    ppermute x21 -> x43, waiting for transfers between devices: 140 us -> 484 us  [the longest x19 242 us: over_dp(): lax.ppermute(value, 'dp', [(i, i ^ bit) for i in range(lax.axis_size('dp'...]
    all_to_all x2 -> x0, waiting for transfers between devices: 158 us -> none  [shards(): lax.all_to_all(blocks.reshape((peers, capacity) + blocks.shape[1:]), 'dp'...]
    all_gather x1, waiting for transfers between devices: 99.5 us -> 0.02 us  [shards(): w_query_columns = lax.all_gather(w_query, 'dp', axis=0, tiled=True)]
    pallas_call x2 -> x4, Pallas kernels: 51.1 us -> 103 us  [span_call(): pl.pallas_call(kernel, grid_spec=pltpu.PrefetchScalarGridSpec(num_scalar_...]
    dynamic_update_slice x0 -> x6, other arithmetic: none -> 16.5 us  [the longest x2 10.3 us: shards(): gathered = lax.dynamic_update_slice(gathered, piece, (0, owner * width))]
    all_to_all x2 -> x0, starting transfers between devices: 12.7 us -> none  [shards(): lax.all_to_all(blocks.reshape((peers, capacity) + blocks.shape[1:]), 'dp'...]
    ppermute x21 -> x43, starting transfers between devices: 53.6 us -> 42.1 us  [the longest x19 15.5 us: over_dp(): lax.ppermute(value, 'dp', [(i, i ^ bit) for i in range(lax.axis_size('dp'...]
    concatenate x0 -> x9, other arithmetic: none -> 9.33 us  [the longest x4 4.22 us: shards(): asked.append(jnp.concatenate([own, over_dp(own, 3 ^ 1 << axis)], axis=0))]
  transfers between devices with their start and end apart: 25 -> 45, of which waited for: 6 -> 21; matrix products, arithmetic and copies ran while one was open for 12% -> 15% of each run, Pallas kernels for 13% -> 16%
where the time goes in v2:
time: 832 us; the launch traced here: 823 us
  waiting for transfers between devices  484 us (58%)
  Pallas kernels  133 us (16%)
  local copies, waits for them, and re-layouts  64.7 us (8%)
  matrix products  45.3 us (5%)
  starting transfers between devices  42.1 us (5%)
  other arithmetic  40 us (5%)
  between operations  13.8 us (2%)
    ppermute x19, waiting for transfers between devices, over_dp(): lax.ppermute(value, 'dp', [(i, i ^ bit) for i in range(lax.axis_size('dp'...  242 us
    ppermute x3, waiting for transfers between devices, pieces_over_fsdp(): lax.ppermute(piece, 'fsdp', chip_pairs([(0, 2), (1, 3), (2, 0), (3, 1)]))  174 us
    pallas_call x4, Pallas kernels, span_call(): pl.pallas_call(kernel, grid_spec=pltpu.PrefetchScalarGridSpec(num_scalar_...  103 us
    ppermute x3, waiting for transfers between devices, pieces_over_fsdp(): ends = lax.ppermute(back2, 'fsdp', chip_pairs([(2, 3), (1, 0)]))  49.5 us
    pallas_call x2, Pallas kernels, pick_blocks(): pl.pallas_call(pick_kernel, grid_spec=pltpu.PrefetchScalarGridSpec(num_sc...  29.6 us
    dot_general x1, matrix products, shards(): jnp.dot(attended, w_output_columns, preferred_element_type=jnp.float32)  23.2 us
    dot_general x1, matrix products, shards(): jnp.dot(normed, w_query_columns, preferred_element_type=jnp.float32)  22.1 us
    dynamic_update_slice x6, local copies, waits for them, and re-layouts, shards(): gathered = lax.dynamic_update_slice(gathered, piece, (0, owner * width))  20.1 us
  transfers between devices with their start and end apart: 45, of which 21 were waited for; matrix products, arithmetic and copies ran while one was open for 15% of the time, Pallas kernels for 16%

profile of v2, /device:TPU:25, one launch (start us, length us, event | category | flops | bytes accessed | tf_op | source)
XLA Modules:
  0.0 822.8 jit_solution(11514106429887852328)
XLA Ops:
  13.1 1.8 collective-permute-done.2
  15.9 85.1 %collective-permute-done.4 = bf16[1024,1024]{1,0:T(8,128)(2,1)} collective-permute-done((bf16[1024,1024]{1,0:T(8,128)(2,1)}, bf16[1024,1024]{1,0:T(8,128)(2,1)}, u32[]{:S(2)}, u32[]{:S(2)}) %collective-permute-start.4) | collective-permute-done | bytes 2097184 | tf_op jit(solution)/shard_map/ppermute | solution.py:43
  103.2 14.8 %pick.3 = (bf16[24,2,128,256]{3,2,1,0:T(8,128)(2,1)}, bf16[24,2,128,256]{3,2,1,0:T(8,128)(2,1)}) custom-call(s32[24]{0:T(128)} %get-tuple-element.64.first_ref, s32[24]{0:T(128)} %get-tuple-element.63.second_ref, bf16[32,2,128,1024]{3,2,1,0:T(8,128)(2,1)} %bitcast.51, bf16[32,2,128,1024]{3,2,1,0:T(8,128)(2,1)} %bitcast.52), custom_call_target="tpu_custom_call" | custom-call | bytes 12582912 | tf_op jit(solution)/shard_map/pick/pallas_call | solution.py:65
  118.7 2.6 collective-permute-start.30
  121.3 5.9 broadcast.77.clone
  127.2 3.1 constant_dynamic-update-slice_fusion.23
  130.3 3.1 constant_dynamic-update-slice_fusion.22
  133.4 17.4 %collective-permute-done.5 = bf16[1024,1024]{1,0:T(8,128)(2,1)} collective-permute-done((bf16[1024,1024]{1,0:T(8,128)(2,1)}, bf16[1024,1024]{1,0:T(8,128)(2,1)}, u32[]{:S(2)}, u32[]{:S(2)}) %collective-permute-start.5) | collective-permute-done | bytes 2097184 | tf_op jit(solution)/shard_map/ppermute | solution.py:44
  150.9 4.7 constant_dynamic-update-slice_fusion.21
  156.6 2.6 collective-permute-start.9
  159.2 75.5 %collective-permute-done.29.refs_8_ = bf16[24,2,128,256]{3,2,1,0:T(8,128)(2,1)S(1)} collective-permute-done((bf16[24,2,128,256]{3,2,1,0:T(8,128)(2,1)}, bf16[24,2,128,256]{3,2,1,0:T(8,128)(2,1)S(1)}, u32[]{:S(2)}, u32[]{:S(2)}) %collective-permute-start.29) | collective-permute-done | bytes 3145760 | tf_op jit(solution)/shard_map/ppermute | solution.py:26
  234.8 4.1 constant_dynamic-update-slice_fusion.20
  238.9 3.1 constant_dynamic-update-slice_fusion.19
  242.0 3.6 constant_dynamic-update-slice_fusion.18
  245.5 5.6 constant_dynamic-update-slice_fusion.17
  251.7 14.8 %pick.2 = (bf16[24,2,128,256]{3,2,1,0:T(8,128)(2,1)}, bf16[24,2,128,256]{3,2,1,0:T(8,128)(2,1)}) custom-call(s32[24]{0:T(128)} %get-tuple-element.64.first_ref, s32[24]{0:T(128)} %get-tuple-element.63.second_ref, bf16[32,2,128,1024]{3,2,1,0:T(8,128)(2,1)} %bitcast.53, bf16[32,2,128,1024]{3,2,1,0:T(8,128)(2,1)} %bitcast.54), custom_call_target="tpu_custom_call" | custom-call | bytes 12582912 | tf_op jit(solution)/shard_map/pick/pallas_call | solution.py:65
  266.5 2.3 collective-permute-start.14
  269.4 3.1 constant_dynamic-update-slice_fusion.16
  272.5 7.2 fusion
  279.7 22.1 %fusion.5 = bf16[1024,1024]{1,0:T(8,128)(2,1)S(1)} fusion(bf16[8192,1024]{1,0:T(8,128)(2,1)} %all-gather.3.cloned.1.call-done, bf16[1024,8192]{1,0:T(8,128)(2,1)} %constant_dynamic-update-slice_fusion.16, f32[1024]{0:T(1024)S(1)} %add_rsqrt_fusion), kind=kOutput, calls=%fused_computation.8 | convolution fusion | flops 17206083584 | bytes 35655680 | tf_op jit(solution)/shard_map/dot_general | solution.py:277
  304.9 113.5 %collective-permute-done.12 = bf16[1024,256]{1,0:T(8,128)(2,1)S(1)} collective-permute-done((bf16[1024,256]{1,0:T(8,128)(2,1)S(1)}, bf16[1024,256]{1,0:T(8,128)(2,1)S(1)}, u32[]{:S(2)}, u32[]{:S(2)}) %collective-permute-start.12) | collective-permute-done | bytes 524320 | tf_op jit(solution)/shard_map/ppermute | solution.py:26
  420.5 1.6 copy-done.1
  422.2 24.5 %stats.2 = (f32[2,64,128]{2,1,0:T(8,128)}, f32[2,64,128]{2,1,0:T(8,128)}) custom-call(s32[32]{0:T(128)} %get-tuple-element.66.refs_0_, s32[32]{0:T(128)} %get-tuple-element.67.refs_1_, s32[32]{0:T(128)} %get-tuple-element.65.refs_2_, s32[32]{0:T(128)} %pad_add_fusion.5.refs_3_, bf16[2048,256]{1,0:T(8,128)(2,1)} %pad_maximum_fusion.refs_4_, ...), custom_call_target="tpu_custom_call" | custom-call | flops 1073741824 | bytes 8388608 | tf_op jit(solution)/shard_map/stats/pallas_call | solution.py:202
  446.7 1.5 collective-permute-start.15
  448.3 4.0 collective-permute-done.15.refs_12_
  452.4 1.4 collective-permute-done.16.refs_13_
  454.4 27.0 %mix.2 = (f32[2,1024,256]{2,1,0:T(8,128)}, f32[2,1024,256]{2,1,0:T(8,128)}) custom-call(s32[32]{0:T(128)} %get-tuple-element.66.refs_0_, s32[32]{0:T(128)} %get-tuple-element.67.refs_1_, s32[32]{0:T(128)} %get-tuple-element.65.refs_2_, s32[32]{0:T(128)} %pad_add_fusion.5.refs_3_, bf16[2048,256]{1,0:T(8,128)(2,1)} %pad_maximum_fusion.refs_4_, ...), custom_call_target="tpu_custom_call" | custom-call | flops 2147483648 | bytes 16777216 | tf_op jit(solution)/shard_map/mix/pallas_call | solution.py:202
  481.4 1.4 slice_bitcast_fusion.3
  485.3 20.9 %collective-permute-done.17 = f32[1024,256]{1,0:T(8,128)S(1)} collective-permute-done((f32[1024,256]{1,0:T(8,128)S(1)}, f32[1024,256]{1,0:T(8,128)S(1)}, u32[]{:S(2)}, u32[]{:S(2)}) %collective-permute-start.17) | collective-permute-done | bytes 1048608 | tf_op jit(solution)/shard_map/ppermute | solution.py:26
  509.9 6.0 broadcast.77
  515.9 1.6 pad_maximum_fusion.2
  517.5 2.5 collective-permute-start.19
  521.3 44.8 %collective-permute-done.20 = bf16[1024,512]{1,0:T(8,128)(2,1)} collective-permute-done((bf16[1024,512]{1,0:T(8,128)(2,1)}, bf16[1024,512]{1,0:T(8,128)(2,1)}, u32[]{:S(2)}, u32[]{:S(2)}) %collective-permute-start.20) | collective-permute-done | bytes 1048608 | tf_op jit(solution)/shard_map/ppermute | solution.py:43
  568.1 12.3 %collective-permute-done.28 = bf16[1024,256]{1,0:T(8,128)(2,1)S(1)} collective-permute-done((bf16[1024,256]{1,0:T(8,128)(2,1)S(1)}, bf16[1024,256]{1,0:T(8,128)(2,1)S(1)}, u32[]{:S(2)}, u32[]{:S(2)}) %collective-permute-start.28) | collective-permute-done | bytes 524320 | tf_op jit(solution)/shard_map/ppermute | solution.py:26
  582.6 9.8 %collective-permute-done.21 = bf16[1024,512]{1,0:T(8,128)(2,1)S(1)} collective-permute-done((bf16[1024,512]{1,0:T(8,128)(2,1)}, bf16[1024,512]{1,0:T(8,128)(2,1)S(1)}, u32[]{:S(2)}, u32[]{:S(2)}) %collective-permute-start.21) | collective-permute-done | bytes 1048608 | tf_op jit(solution)/shard_map/ppermute | solution.py:44
  592.3 1.7 constant_dynamic-update-slice_fusion.13
  594.1 1.5 collective-permute-start.23
  596.6 24.5 %stats.3 = (f32[2,64,128]{2,1,0:T(8,128)}, f32[2,64,128]{2,1,0:T(8,128)}) custom-call(s32[32]{0:T(128)} %get-tuple-element.66.refs_0_, s32[32]{0:T(128)} %get-tuple-element.67.refs_1_, s32[32]{0:T(128)} %get-tuple-element.65.refs_2_, s32[32]{0:T(128)} %pad_add_fusion.5.refs_3_, bf16[2048,256]{1,0:T(8,128)(2,1)} %pad_maximum_fusion.3.refs_4_, ...), custom_call_target="tpu_custom_call" | custom-call | flops 1073741824 | bytes 8388608 | tf_op jit(solution)/shard_map/stats/pallas_call | solution.py:202
  622.5 2.2 collective-permute-start.25
  626.2 26.9 %mix.3 = (f32[2,1024,256]{2,1,0:T(8,128)}, f32[2,1024,256]{2,1,0:T(8,128)}) custom-call(s32[32]{0:T(128)} %get-tuple-element.66.refs_0_, s32[32]{0:T(128)} %get-tuple-element.67.refs_1_, s32[32]{0:T(128)} %get-tuple-element.65.refs_2_, s32[32]{0:T(128)} %pad_add_fusion.5.refs_3_, bf16[2048,256]{1,0:T(8,128)(2,1)} %pad_maximum_fusion.3.refs_4_, ...), custom_call_target="tpu_custom_call" | custom-call | flops 2147483648 | bytes 16777216 | tf_op jit(solution)/shard_map/mix/pallas_call | solution.py:202
  653.1 2.4 slice_bitcast_fusion.1
  656.2 2.3 slice_bitcast_fusion
  658.4 1.5 collective-permute-start.34
  659.9 2.4 constant_dynamic-update-slice_fusion.12
  662.3 2.3 constant_dynamic-update-slice_fusion.11
  664.6 2.3 constant_dynamic-update-slice_fusion.10
  666.9 1.7 constant_dynamic-update-slice_fusion.9
  669.4 10.3 %collective-permute-done.33 = f32[1024,256]{1,0:T(8,128)} collective-permute-done((f32[1024,256]{1,0:T(8,128)}, f32[1024,256]{1,0:T(8,128)}, u32[]{:S(2)}, u32[]{:S(2)}) %collective-permute-start.33) | collective-permute-done | bytes 1048608 | tf_op jit(solution)/shard_map/ppermute | solution.py:26
  679.7 1.6 fusion.9
  684.7 1.6 pad_maximum_fusion.5
  686.5 1.9 collective-permute-start.35
  689.7 44.5 %collective-permute-done.36 = bf16[1024,512]{1,0:T(8,128)(2,1)S(1)} collective-permute-done((bf16[1024,512]{1,0:T(8,128)(2,1)}, bf16[1024,512]{1,0:T(8,128)(2,1)S(1)}, u32[]{:S(2)}, u32[]{:S(2)}) %collective-permute-start.36) | collective-permute-done | bytes 1048608 | tf_op jit(solution)/shard_map/ppermute | solution.py:43
  735.5 2.4 constant_dynamic-update-slice_fusion.6
  737.9 22.3 %collective-permute-done.37 = bf16[1024,512]{1,0:T(8,128)(2,1)S(1)} collective-permute-done((bf16[1024,512]{1,0:T(8,128)(2,1)S(1)}, bf16[1024,512]{1,0:T(8,128)(2,1)S(1)}, u32[]{:S(2)}, u32[]{:S(2)}) %collective-permute-start.37) | collective-permute-done | bytes 1048608 | tf_op jit(solution)/shard_map/ppermute | solution.py:44
  760.2 1.4 constant_dynamic-update-slice_fusion.5
  761.6 1.4 collective-permute-start.39
  763.0 1.3 collective-permute-start.41
  765.4 2.3 constant_dynamic-update-slice_fusion.4
  767.7 2.3 constant_dynamic-update-slice_fusion.3
  770.1 2.3 constant_dynamic-update-slice_fusion.2
  772.4 14.4 %collective-permute-done.41 = bf16[1024,512]{1,0:T(8,128)(2,1)S(1)} collective-permute-done((bf16[1024,512]{1,0:T(8,128)(2,1)}, bf16[1024,512]{1,0:T(8,128)(2,1)S(1)}, u32[]{:S(2)}, u32[]{:S(2)}) %collective-permute-start.41) | collective-permute-done | bytes 1048608 | tf_op jit(solution)/shard_map/ppermute | solution.py:42
  786.7 1.4 constant_dynamic-update-slice_fusion.1
  789.3 2.3 collective-permute-done.42
  792.7 23.2 %convolution_convert_fusion = bf16[1024,1024]{1,0:T(8,128)(2,1)} fusion(bf16[1024,8192]{1,0:T(8,128)(2,1)} %constant_dynamic-update-slice_fusion, bf16[8192,1024]{1,0:T(8,128)(2,1)} %all-gather.5.cloned.1.call-done), kind=kOutput, calls=%fused_computation.9 | convolution fusion | flops 17180917760 | bytes 35651584 | tf_op jit(solution)/shard_map/dot_general | solution.py:308
  (126 shorter events, 44.9 us)
Async XLA Ops:
  6.5 273.1 %all-gather.3.cloned.1.call-start = ((), (), s32[]{:S(2)}) async-start(), calls=%async_computation | async-start | bytes 20971520 | tf_op jit(solution)/shard_map/all_gather | solution.py:261
  7.3 785.5 %all-gather.5.cloned.1.call-start = ((), (), s32[]{:S(2)}) async-start(), calls=%async_computation.1 | async-start | bytes 20971520 | tf_op jit(solution)/shard_map/all_gather | solution.py:271
  7.3 93.7 %collective-permute-start.4 = (bf16[1024,1024]{1,0:T(8,128)(2,1)}, bf16[1024,1024]{1,0:T(8,128)(2,1)}, u32[]{:S(2)}, u32[]{:S(2)}) collective-permute-start(bf16[1024,1024]{1,0:T(8,128)(2,1)} %param.6), channel_id=1, source_target_pairs={{0,4},{1,5},{2,6},{3,7},{4,0},{5,1},{6,2},{7,3},{8,12},{9,13},{10,... | collective-permute-start | bytes 6291464 | tf_op jit(solution)/shard_map/ppermute | solution.py:43
  7.4 122.9 %collective-permute-start.3 = (bf16[1024,1024]{1,0:T(8,128)(2,1)}, bf16[1024,1024]{1,0:T(8,128)(2,1)}, u32[]{:S(2)}, u32[]{:S(2)}) collective-permute-start(bf16[1024,1024]{1,0:T(8,128)(2,1)} %param.6), channel_id=1, source_target_pairs={{0,1},{1,0},{2,3},{3,2},{4,5},{5,4},{6,7},{7,6},{8,9},{9,8},{10,11... | collective-permute-start | bytes 6291464 | tf_op jit(solution)/shard_map/ppermute | solution.py:49
  9.1 2.7 collective-permute-start
  10.3 2.7 collective-permute-start.1
  11.5 3.3 collective-permute-start.2
  11.7 121.7 %collective-permute-start.6 = (bf16[1024,1024]{1,0:T(8,128)(2,1)}, bf16[1024,1024]{1,0:T(8,128)(2,1)}, u32[]{:S(2)}, u32[]{:S(2)}) collective-permute-start(bf16[1024,1024]{1,0:T(8,128)(2,1)} %param.6), channel_id=1, source_target_pairs={{0,2},{1,3},{2,4},{3,5},{4,6},{5,7},{8,10},{9,11},{10,12},{11,13},... | collective-permute-start | bytes 6291464 | tf_op jit(solution)/shard_map/ppermute | solution.py:41
  101.0 49.8 %collective-permute-start.5 = (bf16[1024,1024]{1,0:T(8,128)(2,1)}, bf16[1024,1024]{1,0:T(8,128)(2,1)}, u32[]{:S(2)}, u32[]{:S(2)}) collective-permute-start(bf16[1024,1024]{1,0:T(8,128)(2,1)} %collective-permute-done.4), channel_id=1, source_target_pairs={{4,6},{5,7},{2,0},{3,1},{12,14},{13,15},{10,8},{11,9},{20,22},{21,... | collective-permute-start | bytes 6291464 | tf_op jit(solution)/shard_map/ppermute | solution.py:44
  118.0 116.7 %collective-permute-start.29 = (bf16[24,2,128,256]{3,2,1,0:T(8,128)(2,1)}, bf16[24,2,128,256]{3,2,1,0:T(8,128)(2,1)S(1)}, u32[]{:S(2)}, u32[]{:S(2)}) collective-permute-start(bf16[24,2,128,256]{3,2,1,0:T(8,128)(2,1)} %get-tuple-element.24), channel_id=1, source_target_pairs={{0,8},{8,0},{16,24},{24,16},{1,9},{9,1},{17,25},{25,17},{2,10},{10... | collective-permute-start | bytes 9437192 | tf_op jit(solution)/shard_map/ppermute | solution.py:26
  118.7 116.0 %collective-permute-start.30 = (bf16[24,2,128,256]{3,2,1,0:T(8,128)(2,1)}, bf16[24,2,128,256]{3,2,1,0:T(8,128)(2,1)}, u32[]{:S(2)}, u32[]{:S(2)}) collective-permute-start(bf16[24,2,128,256]{3,2,1,0:T(8,128)(2,1)} %get-tuple-element.25), channel_id=1, source_target_pairs={{0,16},{8,24},{16,0},{24,8},{1,17},{9,25},{17,1},{25,9},{2,18},{10... | collective-permute-start | bytes 9437192 | tf_op jit(solution)/shard_map/ppermute | solution.py:26
  155.6 79.2 %collective-permute-start.7 = (bf16[1024,1024]{1,0:T(8,128)(2,1)}, bf16[1024,1024]{1,0:T(8,128)(2,1)}, u32[]{:S(2)}, u32[]{:S(2)}) collective-permute-start(bf16[1024,1024]{1,0:T(8,128)(2,1)} %get-tuple-element.50), channel_id=1, source_target_pairs={{0,1},{1,0},{2,3},{3,2},{4,5},{5,4},{6,7},{7,6},{8,9},{9,8},{10,11... | collective-permute-start | bytes 6291464 | tf_op jit(solution)/shard_map/ppermute | solution.py:49
  156.6 85.4 %collective-permute-start.8 = (bf16[1024,1024]{1,0:T(8,128)(2,1)}, bf16[1024,1024]{1,0:T(8,128)(2,1)}, u32[]{:S(2)}, u32[]{:S(2)}) collective-permute-start(bf16[1024,1024]{1,0:T(8,128)(2,1)} %collective-permute-done.4), channel_id=1, source_target_pairs={{0,1},{1,0},{2,3},{3,2},{4,5},{5,4},{6,7},{7,6},{8,9},{9,8},{10,11... | collective-permute-start | bytes 6291464 | tf_op jit(solution)/shard_map/ppermute | solution.py:49
  156.6 89.0 %collective-permute-start.9 = (bf16[1024,1024]{1,0:T(8,128)(2,1)}, bf16[1024,1024]{1,0:T(8,128)(2,1)}, u32[]{:S(2)}, u32[]{:S(2)}) collective-permute-start(bf16[1024,1024]{1,0:T(8,128)(2,1)} %param.6), channel_id=1, source_target_pairs={{2,0},{3,1},{4,2},{5,3},{6,4},{7,5},{10,8},{11,9},{12,10},{13,11},... | collective-permute-start | bytes 6291464 | tf_op jit(solution)/shard_map/ppermute | solution.py:42
  234.7 31.8 %copy-start = (bf16[24,2,128,256]{3,2,1,0:T(8,128)(2,1)}, bf16[24,2,128,256]{3,2,1,0:T(8,128)(2,1)S(1)}, u32[]{:S(2)}) copy-start(bf16[24,2,128,256]{3,2,1,0:T(8,128)(2,1)S(1)} %collective-permute-done.29.refs_8_) | copy-start | bytes 9437188
  251.1 18.2 %collective-permute-start.10 = (bf16[1024,1024]{1,0:T(8,128)(2,1)}, bf16[1024,1024]{1,0:T(8,128)(2,1)}, u32[]{:S(2)}, u32[]{:S(2)}) collective-permute-start(bf16[1024,1024]{1,0:T(8,128)(2,1)} %get-tuple-element.48), channel_id=1, source_target_pairs={{0,1},{1,0},{2,3},{3,2},{4,5},{5,4},{6,7},{7,6},{8,9},{9,8},{10,11... | collective-permute-start | bytes 6291464 | tf_op jit(solution)/shard_map/ppermute | solution.py:49
  266.5 154.0 %collective-permute-start.13 = (bf16[24,2,128,256]{3,2,1,0:T(8,128)(2,1)}, bf16[24,2,128,256]{3,2,1,0:T(8,128)(2,1)S(1)}, u32[]{:S(2)}, u32[]{:S(2)}) collective-permute-start(bf16[24,2,128,256]{3,2,1,0:T(8,128)(2,1)} %get-tuple-element.18), channel_id=1, source_target_pairs={{0,8},{8,0},{16,24},{24,16},{1,9},{9,1},{17,25},{25,17},{2,10},{10... | collective-permute-start | bytes 9437192 | tf_op jit(solution)/shard_map/ppermute | solution.py:26
  266.5 154.0 %collective-permute-start.14 = (bf16[24,2,128,256]{3,2,1,0:T(8,128)(2,1)}, bf16[24,2,128,256]{3,2,1,0:T(8,128)(2,1)}, u32[]{:S(2)}, u32[]{:S(2)}) collective-permute-start(bf16[24,2,128,256]{3,2,1,0:T(8,128)(2,1)} %get-tuple-element.19), channel_id=1, source_target_pairs={{0,16},{8,24},{16,0},{24,8},{1,17},{9,25},{17,1},{25,9},{2,18},{10... | collective-permute-start | bytes 9437192 | tf_op jit(solution)/shard_map/ppermute | solution.py:26
  302.9 115.5 %collective-permute-start.12 = (bf16[1024,256]{1,0:T(8,128)(2,1)S(1)}, bf16[1024,256]{1,0:T(8,128)(2,1)S(1)}, u32[]{:S(2)}, u32[]{:S(2)}) collective-permute-start(bf16[1024,256]{1,0:T(8,128)(2,1)S(1)} %get-tuple-element.53), channel_id=1, source_target_pairs={{0,8},{8,0},{16,24},{24,16},{1,9},{9,1},{17,25},{25,17},{2,10},{10... | collective-permute-start | bytes 1572872 | tf_op jit(solution)/shard_map/ppermute | solution.py:26
  303.0 116.4 %collective-permute-start.11 = (bf16[1024,256]{1,0:T(8,128)(2,1)S(1)}, bf16[1024,256]{1,0:T(8,128)(2,1)S(1)}, u32[]{:S(2)}, u32[]{:S(2)}) collective-permute-start(bf16[1024,256]{1,0:T(8,128)(2,1)S(1)} %get-tuple-element.54), channel_id=1, source_target_pairs={{0,16},{8,24},{16,0},{24,8},{1,17},{9,25},{17,1},{25,9},{2,18},{10... | collective-permute-start | bytes 1572872 | tf_op jit(solution)/shard_map/ppermute | solution.py:26
  420.5 1.7 copy-start.1
  446.7 5.7 collective-permute-start.15
  448.2 5.6 collective-permute-start.16
  452.4 1.4 copy-start.8
  453.8 0.6 copy-start.9
  481.4 86.0 %copy-start.4 = (bf16[1024,256]{1,0:T(8,128)(2,1)S(1)}, bf16[1024,256]{1,0:T(8,128)(2,1)}, u32[]{:S(2)}) copy-start(bf16[1024,256]{1,0:T(8,128)(2,1)} %get-tuple-element.51) | copy-start | bytes 1572868
  481.4 86.1 %copy-start.3 = (bf16[1024,256]{1,0:T(8,128)(2,1)S(1)}, bf16[1024,256]{1,0:T(8,128)(2,1)}, u32[]{:S(2)}) copy-start(bf16[1024,256]{1,0:T(8,128)(2,1)} %get-tuple-element.52) | copy-start | bytes 1572868
  482.8 23.5 %collective-permute-start.17 = (f32[1024,256]{1,0:T(8,128)S(1)}, f32[1024,256]{1,0:T(8,128)S(1)}, u32[]{:S(2)}, u32[]{:S(2)}) collective-permute-start(f32[1024,256]{1,0:T(8,128)S(1)} %slice_bitcast_fusion.3), channel_id=1, source_target_pairs={{0,16},{8,24},{16,0},{24,8},{1,17},{9,25},{17,1},{25,9},{2,18},{10... | collective-permute-start | bytes 3145736 | tf_op jit(solution)/shard_map/ppermute | solution.py:26
  485.1 23.5 %collective-permute-start.18 = (f32[1024,256]{1,0:T(8,128)S(1)}, f32[1024,256]{1,0:T(8,128)S(1)}, u32[]{:S(2)}, u32[]{:S(2)}) collective-permute-start(f32[1024,256]{1,0:T(8,128)S(1)} %slice_bitcast_fusion.2), channel_id=1, source_target_pairs={{0,8},{8,0},{16,24},{24,16},{1,9},{9,1},{17,25},{25,17},{2,10},{10... | collective-permute-start | bytes 3145736 | tf_op jit(solution)/shard_map/ppermute | solution.py:26
  517.4 48.7 %collective-permute-start.20 = (bf16[1024,512]{1,0:T(8,128)(2,1)}, bf16[1024,512]{1,0:T(8,128)(2,1)}, u32[]{:S(2)}, u32[]{:S(2)}) collective-permute-start(bf16[1024,512]{1,0:T(8,128)(2,1)} %get-tuple-element.57), channel_id=1, source_target_pairs={{0,4},{1,5},{2,6},{3,7},{4,0},{5,1},{6,2},{7,3},{8,12},{9,13},{10,... | collective-permute-start | bytes 3145736 | tf_op jit(solution)/shard_map/ppermute | solution.py:43
  517.5 63.9 %collective-permute-start.19 = (bf16[1024,512]{1,0:T(8,128)(2,1)}, bf16[1024,512]{1,0:T(8,128)(2,1)S(1)}, u32[]{:S(2)}, u32[]{:S(2)}) collective-permute-start(bf16[1024,512]{1,0:T(8,128)(2,1)} %get-tuple-element.57), channel_id=1, source_target_pairs={{0,1},{1,0},{2,3},{3,2},{4,5},{5,4},{6,7},{7,6},{8,9},{9,8},{10,11... | collective-permute-start | bytes 3145736 | tf_op jit(solution)/shard_map/ppermute | solution.py:49
  520.0 62.6 %collective-permute-start.22 = (bf16[1024,512]{1,0:T(8,128)(2,1)}, bf16[1024,512]{1,0:T(8,128)(2,1)S(1)}, u32[]{:S(2)}, u32[]{:S(2)}) collective-permute-start(bf16[1024,512]{1,0:T(8,128)(2,1)} %get-tuple-element.57), channel_id=1, source_target_pairs={{0,2},{1,3},{2,4},{3,5},{4,6},{5,7},{8,10},{9,11},{10,12},{11,13},... | collective-permute-start | bytes 3145736 | tf_op jit(solution)/shard_map/ppermute | solution.py:41
  566.1 26.2 %collective-permute-start.21 = (bf16[1024,512]{1,0:T(8,128)(2,1)}, bf16[1024,512]{1,0:T(8,128)(2,1)S(1)}, u32[]{:S(2)}, u32[]{:S(2)}) collective-permute-start(bf16[1024,512]{1,0:T(8,128)(2,1)} %collective-permute-done.20), channel_id=1, source_target_pairs={{4,6},{5,7},{2,0},{3,1},{12,14},{13,15},{10,8},{11,9},{20,22},{21,... | collective-permute-start | bytes 3145736 | tf_op jit(solution)/shard_map/ppermute | solution.py:44
  567.4 13.0 %collective-permute-start.28 = (bf16[1024,256]{1,0:T(8,128)(2,1)S(1)}, bf16[1024,256]{1,0:T(8,128)(2,1)S(1)}, u32[]{:S(2)}, u32[]{:S(2)}) collective-permute-start(bf16[1024,256]{1,0:T(8,128)(2,1)S(1)} %copy-done.4), channel_id=1, source_target_pairs={{0,8},{8,0},{16,24},{24,16},{1,9},{9,1},{17,25},{25,17},{2,10},{10... | collective-permute-start | bytes 1572872 | tf_op jit(solution)/shard_map/ppermute | solution.py:26
  567.5 28.0 %collective-permute-start.27 = (bf16[1024,256]{1,0:T(8,128)(2,1)S(1)}, bf16[1024,256]{1,0:T(8,128)(2,1)S(1)}, u32[]{:S(2)}, u32[]{:S(2)}) collective-permute-start(bf16[1024,256]{1,0:T(8,128)(2,1)S(1)} %copy-done.3), channel_id=1, source_target_pairs={{0,16},{8,24},{16,0},{24,8},{1,17},{9,25},{17,1},{25,9},{2,18},{10... | collective-permute-start | bytes 1572872 | tf_op jit(solution)/shard_map/ppermute | solution.py:26
  594.1 65.9 %collective-permute-start.23 = (bf16[1024,512]{1,0:T(8,128)(2,1)}, bf16[1024,512]{1,0:T(8,128)(2,1)}, u32[]{:S(2)}, u32[]{:S(2)}) collective-permute-start(bf16[1024,512]{1,0:T(8,128)(2,1)} %get-tuple-element.46), channel_id=1, source_target_pairs={{0,1},{1,0},{2,3},{3,2},{4,5},{5,4},{6,7},{7,6},{8,9},{9,8},{10,11... | collective-permute-start | bytes 3145736 | tf_op jit(solution)/shard_map/ppermute | solution.py:49
  621.1 3.9 collective-permute-start.31
  621.5 3.6 collective-permute-start.32
  621.9 42.7 %collective-permute-start.24 = (bf16[1024,512]{1,0:T(8,128)(2,1)}, bf16[1024,512]{1,0:T(8,128)(2,1)}, u32[]{:S(2)}, u32[]{:S(2)}) collective-permute-start(bf16[1024,512]{1,0:T(8,128)(2,1)} %collective-permute-done.20), channel_id=1, source_target_pairs={{0,1},{1,0},{2,3},{3,2},{4,5},{5,4},{6,7},{7,6},{8,9},{9,8},{10,11... | collective-permute-start | bytes 3145736 | tf_op jit(solution)/shard_map/ppermute | solution.py:49
  622.5 44.4 %collective-permute-start.25 = (bf16[1024,512]{1,0:T(8,128)(2,1)}, bf16[1024,512]{1,0:T(8,128)(2,1)}, u32[]{:S(2)}, u32[]{:S(2)}) collective-permute-start(bf16[1024,512]{1,0:T(8,128)(2,1)} %get-tuple-element.57), channel_id=1, source_target_pairs={{2,0},{3,1},{4,2},{5,3},{6,4},{7,5},{10,8},{11,9},{12,10},{13,11},... | collective-permute-start | bytes 3145736 | tf_op jit(solution)/shard_map/ppermute | solution.py:42
  624.9 0.6 copy-start.6
  625.5 0.6 copy-start.7
  653.1 29.1 %copy-start.2 = (f32[2,1024,256]{2,1,0:T(8,128)S(1)}, f32[2,1024,256]{2,1,0:T(8,128)}, u32[]{:S(2)}) copy-start(f32[2,1024,256]{2,1,0:T(8,128)} %get-tuple-element.29) | copy-start | bytes 6291460
  655.5 24.2 %collective-permute-start.33 = (f32[1024,256]{1,0:T(8,128)}, f32[1024,256]{1,0:T(8,128)}, u32[]{:S(2)}, u32[]{:S(2)}) collective-permute-start(f32[1024,256]{1,0:T(8,128)} %slice_bitcast_fusion.1), channel_id=1, source_target_pairs={{0,16},{8,24},{16,0},{24,8},{1,17},{9,25},{17,1},{25,9},{2,18},{10... | collective-permute-start | bytes 3145736 | tf_op jit(solution)/shard_map/ppermute | solution.py:26
  658.4 23.7 %collective-permute-start.34 = (f32[1024,256]{1,0:T(8,128)}, f32[1024,256]{1,0:T(8,128)}, u32[]{:S(2)}, u32[]{:S(2)}) collective-permute-start(f32[1024,256]{1,0:T(8,128)} %slice_bitcast_fusion), channel_id=1, source_target_pairs={{0,8},{8,0},{16,24},{24,16},{1,9},{9,1},{17,25},{25,17},{2,10},{10... | collective-permute-start | bytes 3145736 | tf_op jit(solution)/shard_map/ppermute | solution.py:26
  668.6 14.9 %collective-permute-start.26 = (bf16[1024,512]{1,0:T(8,128)(2,1)}, bf16[1024,512]{1,0:T(8,128)(2,1)S(1)}, u32[]{:S(2)}, u32[]{:S(2)}) collective-permute-start(bf16[1024,512]{1,0:T(8,128)(2,1)} %get-tuple-element.44), channel_id=1, source_target_pairs={{0,1},{1,0},{2,3},{3,2},{4,5},{5,4},{6,7},{7,6},{8,9},{9,8},{10,11... | collective-permute-start | bytes 3145736 | tf_op jit(solution)/shard_map/ppermute | solution.py:49
  686.3 47.9 %collective-permute-start.36 = (bf16[1024,512]{1,0:T(8,128)(2,1)}, bf16[1024,512]{1,0:T(8,128)(2,1)S(1)}, u32[]{:S(2)}, u32[]{:S(2)}) collective-permute-start(bf16[1024,512]{1,0:T(8,128)(2,1)} %get-tuple-element.55), channel_id=1, source_target_pairs={{0,4},{1,5},{2,6},{3,7},{4,0},{5,1},{6,2},{7,3},{8,12},{9,13},{10,... | collective-permute-start | bytes 3145736 | tf_op jit(solution)/shard_map/ppermute | solution.py:43
  686.5 49.0 %collective-permute-start.35 = (bf16[1024,512]{1,0:T(8,128)(2,1)}, bf16[1024,512]{1,0:T(8,128)(2,1)}, u32[]{:S(2)}, u32[]{:S(2)}) collective-permute-start(bf16[1024,512]{1,0:T(8,128)(2,1)} %get-tuple-element.55), channel_id=1, source_target_pairs={{0,1},{1,0},{2,3},{3,2},{4,5},{5,4},{6,7},{7,6},{8,9},{9,8},{10,11... | collective-permute-start | bytes 3145736 | tf_op jit(solution)/shard_map/ppermute | solution.py:49
  688.4 49.5 %collective-permute-start.38 = (bf16[1024,512]{1,0:T(8,128)(2,1)}, bf16[1024,512]{1,0:T(8,128)(2,1)S(1)}, u32[]{:S(2)}, u32[]{:S(2)}) collective-permute-start(bf16[1024,512]{1,0:T(8,128)(2,1)} %get-tuple-element.55), channel_id=1, source_target_pairs={{0,2},{1,3},{2,4},{3,5},{4,6},{5,7},{8,10},{9,11},{10,12},{11,13},... | collective-permute-start | bytes 3145736 | tf_op jit(solution)/shard_map/ppermute | solution.py:41
  734.2 3.7 copy-start.5
  734.2 26.0 %collective-permute-start.37 = (bf16[1024,512]{1,0:T(8,128)(2,1)S(1)}, bf16[1024,512]{1,0:T(8,128)(2,1)S(1)}, u32[]{:S(2)}, u32[]{:S(2)}) collective-permute-start(bf16[1024,512]{1,0:T(8,128)(2,1)S(1)} %collective-permute-done.36), channel_id=1, source_target_pairs={{4,6},{5,7},{2,0},{3,1},{12,14},{13,15},{10,8},{11,9},{20,22},{21,... | collective-permute-start | bytes 3145736 | tf_op jit(solution)/shard_map/ppermute | solution.py:44
  761.6 3.8 collective-permute-start.39
  763.0 7.1 collective-permute-start.40
  763.0 23.7 %collective-permute-start.41 = (bf16[1024,512]{1,0:T(8,128)(2,1)}, bf16[1024,512]{1,0:T(8,128)(2,1)S(1)}, u32[]{:S(2)}, u32[]{:S(2)}) collective-permute-start(bf16[1024,512]{1,0:T(8,128)(2,1)} %get-tuple-element.55), channel_id=1, source_target_pairs={{2,0},{3,1},{4,2},{5,3},{6,4},{7,5},{10,8},{11,9},{12,10},{13,11},... | collective-permute-start | bytes 3145736 | tf_op jit(solution)/shard_map/ppermute | solution.py:42
  788.1 3.5 collective-permute-start.42
Sparse Core Ops, SparseCore 0:
  9.2 203.8 all-gather.2
  234.8 229.8 all-gather.4

commit v3 on v2

v3 whole, which is shorter than its diff:
```python
import functools

import jax
import jax.numpy as jnp
from jax import lax
from jax.experimental import pallas as pl
from jax.experimental.pallas import tpu as pltpu
from jax.sharding import PartitionSpec as P


HEAD_DIM = 128
NEIGH = 2
AXES = 2
LANES = 128
ABSENT = -1e30

EPSILON = 1e-05


def normalize(features):
    widened = features.astype(jnp.float32)
    mean_square = jnp.mean(widened * widened, axis=1, keepdims=True)
    return (widened * lax.rsqrt(mean_square + EPSILON)).astype(jnp.bfloat16)


def over_dp(value, bit):
    return lax.ppermute(value, "dp", [(i, i ^ bit) for i in range(lax.axis_size("dp"))])


def pieces_over_fsdp(piece):
    members = lax.axis_size("fsdp")
    chips = members // 2
    if chips != 4:
        whole = lax.all_gather(piece, "fsdp", axis=0)
        return [(i, whole[i]) for i in range(members)]
    me = lax.axis_index("fsdp")
    chip, core = me // 2, me % 2

    def chip_pairs(pairs):
        return [(a * 2 + c, b * 2 + c) for a, b in pairs for c in range(2)]

    back1 = lax.ppermute(piece, "fsdp", chip_pairs([(0, 1), (1, 2), (2, 3)]))
    back3 = lax.ppermute(piece, "fsdp", chip_pairs([(1, 0), (2, 1), (3, 2)]))
    back2 = lax.ppermute(piece, "fsdp", chip_pairs([(0, 2), (1, 3), (2, 0), (3, 1)]))
    ends = lax.ppermute(back2, "fsdp", chip_pairs([(2, 3), (1, 0)]))
    back1 = jnp.where(chip == 0, ends, back1)
    back3 = jnp.where(chip == 3, ends, back3)
    found = []
    for step, here in enumerate((piece, back1, back2, back3)):
        there = lax.ppermute(here, "fsdp", [(i, i ^ 1) for i in range(members)])
        owner = (chip + 4 - step) % 4
        found.append((owner * 2 + core, here))
        found.append((owner * 2 + 1 - core, there))
    return found


def pick_kernel(first_ref, second_ref, *refs):
    for axis in range(AXES):
        refs[AXES + axis][...] = refs[axis][...]


def pick_blocks(stored, tables, step, part):
    count = tables[0].shape[0]
    _, two, block_size, _ = stored.shape
    shape = (1, two, block_size, part)
    return pl.pallas_call(
        pick_kernel,
        grid_spec=pltpu.PrefetchScalarGridSpec(
            num_scalar_prefetch=AXES,
            grid=(count,),
            in_specs=[
                pl.BlockSpec(shape, lambda i, *t, axis=axis: (t[axis][i], 0, 0, step * AXES + axis))
                for axis in range(AXES)
            ],
            out_specs=[pl.BlockSpec(shape, lambda i, *t: (i, 0, 0, 0))] * AXES,
        ),
        out_shape=[jax.ShapeDtypeStruct((count,) + shape[1:], stored.dtype)] * AXES,
        cost_estimate=pl.CostEstimate(
            flops=0, transcendentals=0, bytes_accessed=count * two * block_size * part * 4 * AXES
        ),
        name="pick",
    )(*tables, *[stored] * AXES)


def send_blocks(picked, after):
    picked, _ = lax.optimization_barrier((picked, after))
    return [over_dp(picked[axis], 1 << axis) for axis in range(AXES)]


def scores_of(query, keys, present):
    scores = lax.dot_general(
        query, keys, (((1,), (1,)), ((), ())), preferred_element_type=jnp.float32
    ) * HEAD_DIM ** (-0.5)
    return jnp.where(present, scores, ABSENT)


def head_columns(head):
    return slice(head * HEAD_DIM, (head + 1) * HEAD_DIM)


def span_units(index_refs, query_refs, here_ref, far_refs, spans, span, first, together):
    per_step = query_refs[0].shape[0] // span
    part = query_refs[0].shape[1]
    units = []
    for local in (first + number for number in range(together)):
        in_group = pl.program_id(1) * per_step + local
        entry = pl.program_id(0) * spans + in_group
        rows = pl.ds(pl.multiple_of(local * span, span), span)
        for axis in range(AXES):
            here_at, far_at = index_refs[axis * 2][entry], index_refs[axis * 2 + 1][entry]
            here_block, far_block = jnp.maximum(here_at, 0), jnp.maximum(far_at, 0)
            for head in range(part // HEAD_DIM):
                columns = head_columns(head)
                here_columns = head_columns(axis * (part // HEAD_DIM) + head)
                query = query_refs[axis][rows, columns]
                here = scores_of(query, here_ref[here_block, 0, :, here_columns], here_at >= 0)
                far = scores_of(query, far_refs[axis][far_block, 0, :, columns], far_at >= 0)
                lane = (in_group * (part // HEAD_DIM) + head) * 2
                units.append((axis, rows, columns, here_block, here_columns, far_block, lane, here, far))
    return units


def stats_kernel(spans, span, together, *refs):
    index_refs, refs = refs[:2 * AXES], refs[2 * AXES:]
    query_refs, here_ref, far_refs, out_refs = refs[:AXES], refs[AXES], refs[AXES + 1:2 * AXES + 1], refs[2 * AXES + 1:]
    per_step = query_refs[0].shape[0] // span

    @pl.when(pl.program_id(1) == 0)
    def _():
        for out_ref in out_refs:
            out_ref[...] = jnp.zeros_like(out_ref)

    lanes = lax.broadcasted_iota(jnp.int32, out_refs[0].shape[1:], 1)

    def some(turn, carry):
        units = span_units(index_refs, query_refs, here_ref, far_refs, spans, span, turn * together, together)
        tops = [jnp.max(jnp.maximum(unit[-2], unit[-1]), axis=-1, keepdims=True) for unit in units]
        totals = [
            jnp.sum(jnp.exp(unit[-2] - top) + jnp.exp(unit[-1] - top), axis=-1, keepdims=True)
            for unit, top in zip(units, tops)
        ]
        for axis in range(AXES):
            kept = out_refs[axis][0]
            for unit, top, total in zip(units, tops, totals):
                if unit[0] == axis:
                    kept = jnp.where(lanes == unit[6], top, kept)
                    kept = jnp.where(lanes == unit[6] + 1, total, kept)
            out_refs[axis][0] = kept
        return carry

    lax.fori_loop(0, per_step // together, some, 0)


def mix_kernel(spans, span, together, *refs):
    index_refs, refs = refs[:2 * AXES], refs[2 * AXES:]
    query_refs, here_ref, far_refs, refs = refs[:AXES], refs[AXES], refs[AXES + 1:2 * AXES + 1], refs[2 * AXES + 1:]
    mine_refs, their_refs, keep_refs, send_refs = (refs[i * AXES:(i + 1) * AXES] for i in range(4))
    per_step = query_refs[0].shape[0] // span
    lanes = lax.broadcasted_iota(jnp.int32, mine_refs[0].shape[1:], 1)

    def column(stats, at):
        return jnp.sum(jnp.where(lanes == at, stats, 0.0), axis=-1, keepdims=True)

    def some(out_refs, turn, carry):
        units = span_units(index_refs, query_refs, here_ref, far_refs, spans, span, turn * together, together)
        scales = []
        for unit in units:
            mine, theirs, at = mine_refs[unit[0]][0], their_refs[unit[0]][0], unit[6]
            my_top, their_top = column(mine, at), column(theirs, at)
            top = jnp.maximum(my_top, their_top)
            total = column(mine, at + 1) * jnp.exp(my_top - top) + column(theirs, at + 1) * jnp.exp(their_top - top)
            scales.append((top, 1.0 / total))
        weights = [
            jnp.concatenate(
                [jnp.exp(unit[-2] - top) * scale, jnp.exp(unit[-1] - top) * scale], axis=1
            ).astype(jnp.bfloat16)
            for unit, (top, scale) in zip(units, scales)
        ]
        for (axis, rows, columns, here_block, here_columns, far_block, _, _, _), weight in zip(units, weights):
            values = jnp.concatenate(
                [here_ref[here_block, 1, :, here_columns], far_refs[axis][far_block, 1, :, columns]], axis=0
            )
            out_refs[axis][rows, columns] = jnp.dot(weight, values, preferred_element_type=jnp.float32)
        return carry

    for group, out_refs in enumerate((keep_refs, send_refs)):
        @pl.when(pl.program_id(0) == group)
        def _(out_refs=out_refs):
            lax.fori_loop(0, per_step // together, functools.partial(some, out_refs), 0)


def span_call(kernel, indices, queries, stored, received, stats, step, part, spans, planes):
    rows = queries[0].shape[0] // 2
    span = rows // spans
    count, _, block_size, _ = stored.shape
    per_step = 8 if spans % 8 == 0 else spans
    steps = spans // per_step
    together = 2 if per_step % 2 == 0 else 1
    step_rows = per_step * span

    in_specs = [pl.BlockSpec((step_rows, part), lambda c, i, *t: (c * steps + i, step))] * AXES
    in_specs += [pl.BlockSpec((count, planes, block_size, AXES * part), lambda c, i, *t: (0, 0, 0, step))]
    in_specs += [
        pl.BlockSpec((received[0].shape[0], planes, block_size, part), lambda c, i, *t: (0, 0, 0, 0))
    ] * AXES
    if stats:
        in_specs += [pl.BlockSpec((1, span, LANES), lambda c, i, *t: (c, 0, 0))] * AXES
        in_specs += [pl.BlockSpec((1, span, LANES), lambda c, i, *t: (1 - c, 0, 0))] * AXES
        out_specs = [pl.BlockSpec((step_rows, part), lambda c, i, *t: (jnp.where(c == 0, i, steps - 1), 0))] * AXES
        out_specs += [pl.BlockSpec((step_rows, part), lambda c, i, *t: (jnp.where(c == 0, 0, i), 0))] * AXES
        out_shape = [jax.ShapeDtypeStruct((rows, part), jnp.float32)] * (2 * AXES)
    else:
        out_specs = [pl.BlockSpec((1, span, LANES), lambda c, i, *t: (c, 0, 0))] * AXES
        out_shape = [jax.ShapeDtypeStruct((2, span, LANES), jnp.float32)] * AXES
    return pl.pallas_call(
        functools.partial(kernel, spans, span, together),
        grid_spec=pltpu.PrefetchScalarGridSpec(
            num_scalar_prefetch=2 * AXES,
            grid=(2, steps),
            in_specs=in_specs,
            out_specs=out_specs,
        ),
        out_shape=out_shape,
        cost_estimate=pl.CostEstimate(
            flops=8 * rows * NEIGH * block_size * part * AXES * planes,
            transcendentals=2 * rows * NEIGH * block_size * part * AXES // HEAD_DIM,
            bytes_accessed=(count + received[0].shape[0]) * planes * block_size * part * 2 * AXES,
        ),
        name="mix" if stats else "stats",
    )(*indices, *queries, stored, *received, *stats)


def exchange_tables(neighbor_shard, neighbor_block, capacity):
    me = lax.axis_index("dp")
    both = jnp.concatenate([neighbor_shard, neighbor_block], axis=1)
    groups = jnp.stack([both] + [over_dp(both, bit) for bit in (1, 2, 3)])
    spans = both.shape[0]
    owners = groups[:, :, :NEIGH].reshape(4, spans * NEIGH)
    wanted = groups[:, :, NEIGH:].reshape(4, spans * NEIGH)
    order = jnp.arange(spans * NEIGH, dtype=jnp.int32)
    same = (owners[:, :, None] == owners[:, None, :]) & (order[None, None, :] < order[None, :, None])
    rank = jnp.sum(same.astype(jnp.int32), axis=2)
    slots = jnp.arange(capacity, dtype=jnp.int32)
    hit = (owners == me)[:, :, None] & (rank[:, :, None] == slots[None, None, :])
    table = jnp.sum(jnp.where(hit, wanted[:, :, None], 0), axis=1)
    sends, places = [], []
    for axis in range(AXES):
        near = 1 << axis
        partner = 3 ^ near
        sends.append(jnp.concatenate([table[near], table[3]]))
        here, far = [], []
        for position, group in enumerate((0, partner)):
            mine = (owners[group] == me).reshape(spans, NEIGH)
            other = (owners[group] == me ^ near).reshape(spans, NEIGH)
            block = wanted[group].reshape(spans, NEIGH)
            slot = rank[group].reshape(spans, NEIGH) + position * capacity
            here.append(jnp.max(jnp.where(mine, block, -1), axis=1))
            far.append(jnp.max(jnp.where(other, slot, -1), axis=1))
        places += [jnp.concatenate(here), jnp.concatenate(far)]
    return sends, places


def work(tokens, w_query, w_output, neighbor_shard, neighbor_block, kv_store):
    local_width = w_query.shape[1]
    row_count, width = tokens.shape
    peers = lax.axis_size("dp")
    members = lax.axis_size("fsdp")
    passes = 2 if local_width % (2 * AXES * HEAD_DIM) == 0 else 1
    part = local_width // (passes * AXES)
    span_count = neighbor_shard.shape[0]
    capacity = max(2, 3 * span_count * NEIGH // (2 * peers))

    w_query_columns = lax.all_gather(w_query, "dp", axis=0, tiled=True)

    sends, places = exchange_tables(neighbor_shard, neighbor_block, capacity)
    stored = kv_store[0]
    picked = [pick_blocks(stored, sends, step, part) for step in range(passes)]

    pieces = pieces_over_fsdp(tokens)
    received = [send_blocks(picked[0], pieces[-1][1])]

    gathered = jnp.zeros((row_count, members * width), tokens.dtype)
    for owner, piece in pieces:
        gathered = lax.dynamic_update_slice(gathered, piece, (0, owner * width))
    normed = normalize(gathered)
    queries = jnp.dot(normed, w_query_columns, preferred_element_type=jnp.float32).astype(jnp.bfloat16)

    asked = []
    for axis in range(AXES):
        starts = [(step * AXES + axis) * part for step in range(passes)]
        own = jnp.concatenate([queries[:, start:start + part] for start in starts], axis=1)
        asked.append(jnp.concatenate([own, over_dp(own, 3 ^ (1 << axis))], axis=0))
    for step in range(1, passes):
        received.append(send_blocks(picked[step], asked[0]))

    attended = jnp.zeros((row_count, members * local_width), jnp.bfloat16)
    for step in range(passes):
        common = dict(step=step, part=part, spans=span_count)
        mine = span_call(
            stats_kernel, places, asked, stored, received[step], [], planes=1, **common
        )
        theirs = [over_dp(mine[axis], 3 ^ (1 << axis)) for axis in range(AXES)]
        partial = span_call(mix_kernel, places, asked, stored, received[step], list(mine) + theirs, planes=2, **common)
        if step == 0:
            w_output, _ = lax.optimization_barrier((w_output, partial))
            w_output_columns = lax.all_gather(w_output, "dp", axis=0, tiled=True)
        others = [over_dp(partial[AXES + axis], 3 ^ (1 << axis)) for axis in range(AXES)]
        mixed = jnp.concatenate(
            [(partial[axis] + others[axis]).astype(jnp.bfloat16) for axis in range(AXES)], axis=1
        )
        pieces = pieces_over_fsdp(mixed)
        for owner, piece in pieces:
            start = owner * local_width + step * AXES * part
            attended = lax.dynamic_update_slice(attended, piece, (0, start))
    summed = jnp.dot(attended, w_output_columns, preferred_element_type=jnp.float32)
    return summed.astype(jnp.bfloat16)


def solution(mesh):
    in_specs = (
        P("dp", "fsdp"),
        P("dp", "fsdp"),
        P("dp", "fsdp"),
        P("dp", None),
        P("dp", None),
        P("dp", None, None, None, "fsdp"),
    )
    out_specs = P("dp", "fsdp")
    return jax.shard_map(work, mesh=mesh, in_specs=in_specs, out_specs=out_specs, check_vma=False)
```

time: 832 us -> 758 us (0.911)
  waiting for transfers between devices: 484 us -> 396 us
  starting transfers between devices: 42.1 us -> 104 us
  Pallas kernels: 133 us -> 95.6 us
    ppermute x19 -> x17, waiting for transfers between devices: 242 us -> 104 us  [over_dp(): lax.ppermute(value, 'dp', [(i, i ^ bit) for i in range(lax.axis_size('dp'...]
    ppermute x3, waiting for transfers between devices: 174 us -> 123 us  [pieces_over_fsdp(): lax.ppermute(piece, 'fsdp', chip_pairs([(0, 2), (1, 3), (2, 0), (3, 1)]))]
    ppermute x12, starting transfers between devices: 12.3 us -> 61 us  [pieces_over_fsdp(): there = lax.ppermute(here, 'fsdp', [(i, i ^ 1) for i in range(members)])]
    ppermute x3, waiting for transfers between devices: 0.01 us -> 38.8 us  [pieces_over_fsdp(): back1 = lax.ppermute(piece, 'fsdp', chip_pairs([(0, 1), (1, 2), (2, 3)]))]
    pallas_call x4, Pallas kernels: 103 us -> 66.6 us  [span_call(): pl.pallas_call(functools.partial(kernel, spans, span, together), grid_spe...]
    ppermute x3, waiting for transfers between devices: 14.4 us -> 47 us  [pieces_over_fsdp(): back3 = lax.ppermute(piece, 'fsdp', chip_pairs([(1, 0), (2, 1), (3, 2)]))]
    ppermute x3, waiting for transfers between devices: 49.5 us -> 78.1 us  [pieces_over_fsdp(): ends = lax.ppermute(back2, 'fsdp', chip_pairs([(2, 3), (1, 0)]))]
    ppermute x3, starting transfers between devices: 0.37 us -> 13.4 us  [pieces_over_fsdp(): lax.ppermute(piece, 'fsdp', chip_pairs([(0, 2), (1, 3), (2, 0), (3, 1)]))]
  transfers between devices with their start and end apart: 45 -> 43, of which waited for: 21 -> 24; matrix products, arithmetic and copies ran while one was open for 15% -> 15% of each run, Pallas kernels for 16% -> 8%
where the time goes in v3:
time: 758 us; the launch traced here: 754 us
  waiting for transfers between devices  396 us (52%)
  starting transfers between devices  104 us (14%)
  Pallas kernels  95.6 us (13%)
  local copies, waits for them, and re-layouts  57.7 us (8%)
  matrix products  45.3 us (6%)
  other arithmetic  41.2 us (5%)
  between operations  13.8 us (2%)
    ppermute x3, waiting for transfers between devices, pieces_over_fsdp(): lax.ppermute(piece, 'fsdp', chip_pairs([(0, 2), (1, 3), (2, 0), (3, 1)]))  123 us
    ppermute x17, waiting for transfers between devices, over_dp(): lax.ppermute(value, 'dp', [(i, i ^ bit) for i in range(lax.axis_size('dp'...  104 us
    ppermute x3, waiting for transfers between devices, pieces_over_fsdp(): ends = lax.ppermute(back2, 'fsdp', chip_pairs([(2, 3), (1, 0)]))  78.1 us
    pallas_call x4, Pallas kernels, span_call(): pl.pallas_call(functools.partial(kernel, spans, span, together), grid_spe...  66.6 us
    ppermute x12, starting transfers between devices, pieces_over_fsdp(): there = lax.ppermute(here, 'fsdp', [(i, i ^ 1) for i in range(members)])  61 us
    ppermute x3, waiting for transfers between devices, pieces_over_fsdp(): back3 = lax.ppermute(piece, 'fsdp', chip_pairs([(1, 0), (2, 1), (3, 2)]))  47 us
    ppermute x3, waiting for transfers between devices, pieces_over_fsdp(): back1 = lax.ppermute(piece, 'fsdp', chip_pairs([(0, 1), (1, 2), (2, 3)]))  38.8 us
    pallas_call x2, Pallas kernels, pick_blocks(): pl.pallas_call(pick_kernel, grid_spec=pltpu.PrefetchScalarGridSpec(num_sc...  29 us
  transfers between devices with their start and end apart: 43, of which 24 were waited for; matrix products, arithmetic and copies ran while one was open for 15% of the time, Pallas kernels for 8%

profile of v3, /device:TPU:25, one launch (start us, length us, event | category | flops | bytes accessed | tf_op | source)
XLA Modules:
  0.0 754.0 jit_solution(8037828841795650557)
XLA Ops:
  9.7 91.3 %collective-permute-done.4 = bf16[1024,1024]{1,0:T(8,128)(2,1)} collective-permute-done((bf16[1024,1024]{1,0:T(8,128)(2,1)}, bf16[1024,1024]{1,0:T(8,128)(2,1)}, u32[]{:S(2)}, u32[]{:S(2)}) %collective-permute-start.4) | collective-permute-done | bytes 2097184 | tf_op jit(solution)/shard_map/ppermute | solution.py:44
  102.4 5.9 broadcast.77.clone
  108.3 3.1 constant_dynamic-update-slice_fusion.23
  111.4 3.1 constant_dynamic-update-slice_fusion.22
  114.5 35.3 %collective-permute-done.5 = bf16[1024,1024]{1,0:T(8,128)(2,1)S(1)} collective-permute-done((bf16[1024,1024]{1,0:T(8,128)(2,1)}, bf16[1024,1024]{1,0:T(8,128)(2,1)S(1)}, u32[]{:S(2)}, u32[]{:S(2)}) %collective-permute-start.5) | collective-permute-done | bytes 2097184 | tf_op jit(solution)/shard_map/ppermute | solution.py:45
  149.8 4.8 constant_dynamic-update-slice_fusion.21
  156.0 2.6 collective-permute-start.9
  158.6 1.5 collective-permute-done.7
  160.1 3.2 constant_dynamic-update-slice_fusion.20
  163.2 3.1 constant_dynamic-update-slice_fusion.19
  166.4 3.1 constant_dynamic-update-slice_fusion.18
  169.5 32.6 %collective-permute-done.9 = bf16[1024,1024]{1,0:T(8,128)(2,1)} collective-permute-done((bf16[1024,1024]{1,0:T(8,128)(2,1)}, bf16[1024,1024]{1,0:T(8,128)(2,1)}, u32[]{:S(2)}, u32[]{:S(2)}) %collective-permute-start.9) | collective-permute-done | bytes 2097184 | tf_op jit(solution)/shard_map/ppermute | solution.py:43
  202.1 3.1 constant_dynamic-update-slice_fusion.17
  210.3 2.1 collective-permute-done.2
  214.3 14.4 %pick.2 = (bf16[24,2,128,256]{3,2,1,0:T(8,128)(2,1)}, bf16[24,2,128,256]{3,2,1,0:T(8,128)(2,1)}) custom-call(s32[24]{0:T(128)} %get-tuple-element.80.first_ref, s32[24]{0:T(128)} %get-tuple-element.79.second_ref, bf16[32,2,128,1024]{3,2,1,0:T(8,128)(2,1)} %bitcast.27, bf16[32,2,128,1024]{3,2,1,0:T(8,128)(2,1)} %bitcast.28), custom_call_target="tpu_custom_call" | custom-call | bytes 12582912 | tf_op jit(solution)/shard_map/pick/pallas_call | solution.py:66
  231.4 3.1 constant_dynamic-update-slice_fusion.16
  234.5 7.2 fusion
  241.7 22.1 %fusion.5 = bf16[1024,1024]{1,0:T(8,128)(2,1)S(1)} fusion(bf16[8192,1024]{1,0:T(8,128)(2,1)} %all-gather.3.cloned.1.call-done, bf16[1024,8192]{1,0:T(8,128)(2,1)} %constant_dynamic-update-slice_fusion.16, f32[1024]{0:T(1024)S(1)} %add_rsqrt_fusion), kind=kOutput, calls=%fused_computation.10 | convolution fusion | flops 17206083584 | bytes 35655680 | tf_op jit(solution)/shard_map/dot_general | solution.py:286
  271.7 49.8 %collective-permute-done.11 = bf16[1024,512]{1,0:T(8,128)(2,1)} collective-permute-done((bf16[1024,512]{1,0:T(8,128)(2,1)}, bf16[1024,512]{1,0:T(8,128)(2,1)}, u32[]{:S(2)}, u32[]{:S(2)}) %collective-permute-start.11) | collective-permute-done | bytes 1048608 | tf_op jit(solution)/shard_map/ppermute | solution.py:27
  321.5 3.0 pad_maximum_fusion.refs_4_
  324.5 2.6 pad_maximum_fusion.1.refs_5_
  327.1 1.6 copy-done
  328.7 14.9 %stats.2 = (f32[2,64,128]{2,1,0:T(8,128)}, f32[2,64,128]{2,1,0:T(8,128)}) custom-call(s32[32]{0:T(128)} %get-tuple-element.82.refs_0_, s32[32]{0:T(128)} %get-tuple-element.83.refs_1_, s32[32]{0:T(128)} %get-tuple-element.81.refs_2_, s32[32]{0:T(128)} %pad_add_fusion.5.refs_3_, bf16[2048,512]{1,0:T(8,128)(2,1)} %pad_maximum_fusion.refs_4_, ...), custom_call_target="tpu_custom_call" | custom-call | flops 1073741824 | bytes 7340032 | tf_op jit(solution)/shard_map/stats/pallas_call | solution.py:215
  345.5 1.5 collective-permute-done.15.refs_11_
  348.3 18.4 %mix.2 = (f32[1024,256]{1,0:T(8,128)}, f32[1024,256]{1,0:T(8,128)}, f32[1024,256]{1,0:T(8,128)}, f32[1024,256]{1,0:T(8,128)}) custom-call(s32[32]{0:T(128)} %get-tuple-element.82.refs_0_, s32[32]{0:T(128)} %get-tuple-element.83.refs_1_, s32[32]{0:T(128)} %get-tuple-element.81.refs_2_, s32[32]{0:T(128)} %pad_add_fusion.5.refs_3_, ...), custom_call_target="tpu_custom_call" | custom-call | flops 2147483648 | bytes 14680064 | tf_op jit(solution)/shard_map/mix/pallas_call | solution.py:215
  368.5 14.6 %pick.3 = (bf16[24,2,128,256]{3,2,1,0:T(8,128)(2,1)}, bf16[24,2,128,256]{3,2,1,0:T(8,128)(2,1)}) custom-call(s32[24]{0:T(128)} %get-tuple-element.80.first_ref, s32[24]{0:T(128)} %get-tuple-element.79.second_ref, bf16[32,2,128,1024]{3,2,1,0:T(8,128)(2,1)} %bitcast.31, bf16[32,2,128,1024]{3,2,1,0:T(8,128)(2,1)} %bitcast.32), custom_call_target="tpu_custom_call" | custom-call | bytes 12582912 | tf_op jit(solution)/shard_map/pick/pallas_call | solution.py:66
  385.4 2.5 collective-permute-done.18
  387.8 2.1 add_convert_fusion.2
  389.9 1.6 add_convert_fusion.3
  391.6 5.9 broadcast.77
  397.5 1.5 pad_maximum_fusion.4
  399.0 6.4 collective-permute-start.20
  405.4 19.9 %collective-permute-start.19 = (bf16[1024,512]{1,0:T(8,128)(2,1)}, bf16[1024,512]{1,0:T(8,128)(2,1)S(1)}, u32[]{:S(2)}, u32[]{:S(2)}) collective-permute-start(bf16[1024,512]{1,0:T(8,128)(2,1)} %get-tuple-element.73), channel_id=1, source_target_pairs={{0,1},{1,0},{2,3},{3,2},{4,5},{5,4},{6,7},{7,6},{8,9},{9,8},{10,11... | collective-permute-start | bytes 3145736 | tf_op jit(solution)/shard_map/ppermute | solution.py:50
  426.6 8.8 %collective-permute-done.20 = bf16[1024,512]{1,0:T(8,128)(2,1)} collective-permute-done((bf16[1024,512]{1,0:T(8,128)(2,1)}, bf16[1024,512]{1,0:T(8,128)(2,1)}, u32[]{:S(2)}, u32[]{:S(2)}) %collective-permute-start.20) | collective-permute-done | bytes 1048608 | tf_op jit(solution)/shard_map/ppermute | solution.py:44
  437.8 25.3 %collective-permute-done.22 = bf16[1024,512]{1,0:T(8,128)(2,1)S(1)} collective-permute-done((bf16[1024,512]{1,0:T(8,128)(2,1)}, bf16[1024,512]{1,0:T(8,128)(2,1)S(1)}, u32[]{:S(2)}, u32[]{:S(2)}) %collective-permute-start.22) | collective-permute-done | bytes 1048608 | tf_op jit(solution)/shard_map/ppermute | solution.py:42
  463.1 20.3 %collective-permute-done.21 = bf16[1024,512]{1,0:T(8,128)(2,1)S(1)} collective-permute-done((bf16[1024,512]{1,0:T(8,128)(2,1)}, bf16[1024,512]{1,0:T(8,128)(2,1)S(1)}, u32[]{:S(2)}, u32[]{:S(2)}) %collective-permute-start.21) | collective-permute-done | bytes 1048608 | tf_op jit(solution)/shard_map/ppermute | solution.py:45
  483.4 1.7 constant_dynamic-update-slice_fusion.13
  485.1 3.0 collective-permute-start.23
  488.1 2.2 collective-permute-start.25
  490.4 24.2 %collective-permute-done.27.refs_7_ = bf16[24,2,128,256]{3,2,1,0:T(8,128)(2,1)S(1)} collective-permute-done((bf16[24,2,128,256]{3,2,1,0:T(8,128)(2,1)}, bf16[24,2,128,256]{3,2,1,0:T(8,128)(2,1)S(1)}, u32[]{:S(2)}, u32[]{:S(2)}) %collective-permute-start.27) | collective-permute-done | bytes 3145760 | tf_op jit(solution)/shard_map/ppermute | solution.py:27
  516.2 14.9 %stats.3 = (f32[2,64,128]{2,1,0:T(8,128)}, f32[2,64,128]{2,1,0:T(8,128)}) custom-call(s32[32]{0:T(128)} %get-tuple-element.82.refs_0_, s32[32]{0:T(128)} %get-tuple-element.83.refs_1_, s32[32]{0:T(128)} %get-tuple-element.81.refs_2_, s32[32]{0:T(128)} %pad_add_fusion.5.refs_3_, bf16[2048,512]{1,0:T(8,128)(2,1)} %pad_maximum_fusion.refs_4_, ...), custom_call_target="tpu_custom_call" | custom-call | flops 1073741824 | bytes 7340032 | tf_op jit(solution)/shard_map/stats/pallas_call | solution.py:215
  533.3 3.1 collective-permute-done.29.refs_11_
  538.1 18.3 %mix.3 = (f32[1024,256]{1,0:T(8,128)}, f32[1024,256]{1,0:T(8,128)}, f32[1024,256]{1,0:T(8,128)}, f32[1024,256]{1,0:T(8,128)}) custom-call(s32[32]{0:T(128)} %get-tuple-element.82.refs_0_, s32[32]{0:T(128)} %get-tuple-element.83.refs_1_, s32[32]{0:T(128)} %get-tuple-element.81.refs_2_, s32[32]{0:T(128)} %pad_add_fusion.5.refs_3_, ...), custom_call_target="tpu_custom_call" | custom-call | flops 2147483648 | bytes 14680064 | tf_op jit(solution)/shard_map/mix/pallas_call | solution.py:215
  558.4 2.4 constant_dynamic-update-slice_fusion.12
  560.8 2.3 constant_dynamic-update-slice_fusion.11
  563.1 2.3 constant_dynamic-update-slice_fusion.10
  566.7 16.1 %collective-permute-start.26 = (bf16[1024,512]{1,0:T(8,128)(2,1)S(1)}, bf16[1024,512]{1,0:T(8,128)(2,1)S(1)}, u32[]{:S(2)}, u32[]{:S(2)}) collective-permute-start(bf16[1024,512]{1,0:T(8,128)(2,1)S(1)} %get-tuple-element.60), channel_id=1, source_target_pairs={{0,1},{1,0},{2,3},{3,2},{4,5},{5,4},{6,7},{7,6},{8,9},{9,8},{10,11... | collective-permute-start | bytes 3145736 | tf_op jit(solution)/shard_map/ppermute | solution.py:50
  582.8 16.4 %collective-permute-done.32 = f32[1024,256]{1,0:T(8,128)} collective-permute-done((f32[1024,256]{1,0:T(8,128)}, f32[1024,256]{1,0:T(8,128)}, u32[]{:S(2)}, u32[]{:S(2)}) %collective-permute-start.32) | collective-permute-done | bytes 1048608 | tf_op jit(solution)/shard_map/ppermute | solution.py:27
  599.3 1.6 add_convert_fusion
  603.3 1.5 pad_maximum_fusion.5
  604.9 6.9 collective-permute-start.34
  611.8 16.4 %collective-permute-start.33 = (bf16[1024,512]{1,0:T(8,128)(2,1)}, bf16[1024,512]{1,0:T(8,128)(2,1)}, u32[]{:S(2)}, u32[]{:S(2)}) collective-permute-start(bf16[1024,512]{1,0:T(8,128)(2,1)} %get-tuple-element.71), channel_id=1, source_target_pairs={{0,1},{1,0},{2,3},{3,2},{4,5},{5,4},{6,7},{7,6},{8,9},{9,8},{10,11... | collective-permute-start | bytes 3145736 | tf_op jit(solution)/shard_map/ppermute | solution.py:50
  629.4 23.1 %collective-permute-done.34 = bf16[1024,512]{1,0:T(8,128)(2,1)S(1)} collective-permute-done((bf16[1024,512]{1,0:T(8,128)(2,1)}, bf16[1024,512]{1,0:T(8,128)(2,1)S(1)}, u32[]{:S(2)}, u32[]{:S(2)}) %collective-permute-start.34) | collective-permute-done | bytes 1048608 | tf_op jit(solution)/shard_map/ppermute | solution.py:44
  653.9 2.3 constant_dynamic-update-slice_fusion.6
  656.2 13.5 %collective-permute-done.36 = bf16[1024,512]{1,0:T(8,128)(2,1)S(1)} collective-permute-done((bf16[1024,512]{1,0:T(8,128)(2,1)}, bf16[1024,512]{1,0:T(8,128)(2,1)S(1)}, u32[]{:S(2)}, u32[]{:S(2)}) %collective-permute-start.36) | collective-permute-done | bytes 1048608 | tf_op jit(solution)/shard_map/ppermute | solution.py:42
  669.7 22.5 %collective-permute-done.35 = bf16[1024,512]{1,0:T(8,128)(2,1)S(1)} collective-permute-done((bf16[1024,512]{1,0:T(8,128)(2,1)S(1)}, bf16[1024,512]{1,0:T(8,128)(2,1)S(1)}, u32[]{:S(2)}, u32[]{:S(2)}) %collective-permute-start.35) | collective-permute-done | bytes 1048608 | tf_op jit(solution)/shard_map/ppermute | solution.py:45
  692.1 1.4 constant_dynamic-update-slice_fusion.5
  694.3 1.3 collective-permute-start.39
  696.8 2.3 constant_dynamic-update-slice_fusion.4
  699.1 2.3 constant_dynamic-update-slice_fusion.3
  701.4 2.3 constant_dynamic-update-slice_fusion.2
  703.7 14.4 %collective-permute-done.39 = bf16[1024,512]{1,0:T(8,128)(2,1)S(1)} collective-permute-done((bf16[1024,512]{1,0:T(8,128)(2,1)}, bf16[1024,512]{1,0:T(8,128)(2,1)S(1)}, u32[]{:S(2)}, u32[]{:S(2)}) %collective-permute-start.39) | collective-permute-done | bytes 1048608 | tf_op jit(solution)/shard_map/ppermute | solution.py:43
  720.6 2.3 collective-permute-done.40
  723.9 23.2 %convolution_convert_fusion = bf16[1024,1024]{1,0:T(8,128)(2,1)} fusion(bf16[1024,8192]{1,0:T(8,128)(2,1)} %constant_dynamic-update-slice_fusion, bf16[8192,1024]{1,0:T(8,128)(2,1)} %all-gather.5.cloned.1.call-done), kind=kOutput, calls=%fused_computation.11 | convolution fusion | flops 17180917760 | bytes 35651584 | tf_op jit(solution)/shard_map/dot_general | solution.py:315
  (126 shorter events, 53.2 us)
Async XLA Ops:
  6.5 235.2 %all-gather.3.cloned.1.call-start = ((), (), s32[]{:S(2)}) async-start(), calls=%async_computation | async-start | bytes 20971520 | tf_op jit(solution)/shard_map/all_gather | solution.py:273
  7.3 716.7 %all-gather.5.cloned.1.call-start = ((), (), s32[]{:S(2)}) async-start(), calls=%async_computation.1 | async-start | bytes 20971520 | tf_op jit(solution)/shard_map/all_gather | solution.py:306
  7.3 93.7 %collective-permute-start.4 = (bf16[1024,1024]{1,0:T(8,128)(2,1)}, bf16[1024,1024]{1,0:T(8,128)(2,1)}, u32[]{:S(2)}, u32[]{:S(2)}) collective-permute-start(bf16[1024,1024]{1,0:T(8,128)(2,1)} %param.6), channel_id=1, source_target_pairs={{0,4},{1,5},{2,6},{3,7},{4,0},{5,1},{6,2},{7,3},{8,12},{9,13},{10,... | collective-permute-start | bytes 6291464 | tf_op jit(solution)/shard_map/ppermute | solution.py:44
  7.4 104.0 %collective-permute-start.3 = (bf16[1024,1024]{1,0:T(8,128)(2,1)}, bf16[1024,1024]{1,0:T(8,128)(2,1)}, u32[]{:S(2)}, u32[]{:S(2)}) collective-permute-start(bf16[1024,1024]{1,0:T(8,128)(2,1)} %param.6), channel_id=1, source_target_pairs={{0,1},{1,0},{2,3},{3,2},{4,5},{5,4},{6,7},{7,6},{8,9},{9,8},{10,11... | collective-permute-start | bytes 6291464 | tf_op jit(solution)/shard_map/ppermute | solution.py:50
  8.4 106.1 %collective-permute-start.6 = (bf16[1024,1024]{1,0:T(8,128)(2,1)}, bf16[1024,1024]{1,0:T(8,128)(2,1)}, u32[]{:S(2)}, u32[]{:S(2)}) collective-permute-start(bf16[1024,1024]{1,0:T(8,128)(2,1)} %param.6), channel_id=1, source_target_pairs={{0,2},{1,3},{2,4},{3,5},{4,6},{5,7},{8,10},{9,11},{10,12},{11,13},... | collective-permute-start | bytes 6291464 | tf_op jit(solution)/shard_map/ppermute | solution.py:42
  101.0 48.8 %collective-permute-start.5 = (bf16[1024,1024]{1,0:T(8,128)(2,1)}, bf16[1024,1024]{1,0:T(8,128)(2,1)S(1)}, u32[]{:S(2)}, u32[]{:S(2)}) collective-permute-start(bf16[1024,1024]{1,0:T(8,128)(2,1)} %collective-permute-done.4), channel_id=1, source_target_pairs={{4,6},{5,7},{2,0},{3,1},{12,14},{13,15},{10,8},{11,9},{20,22},{21,... | collective-permute-start | bytes 6291464 | tf_op jit(solution)/shard_map/ppermute | solution.py:45
  111.4 95.2 %copy-start.12 = (s32[16,2]{0,1:T(2,128)S(1)}, s32[16,2]{0,1:T(2,128)}, u32[]{:S(2)}) copy-start(s32[16,2]{0,1:T(2,128)} %param.10) | copy-start | bytes 388
  111.4 95.2 %copy-start.13 = (s32[16,2]{0,1:T(2,128)S(1)}, s32[16,2]{0,1:T(2,128)}, u32[]{:S(2)}) copy-start(s32[16,2]{0,1:T(2,128)} %param.9) | copy-start | bytes 388
  154.6 5.5 collective-permute-start.7
  156.0 10.4 %collective-permute-start.8 = (bf16[1024,1024]{1,0:T(8,128)(2,1)}, bf16[1024,1024]{1,0:T(8,128)(2,1)}, u32[]{:S(2)}, u32[]{:S(2)}) collective-permute-start(bf16[1024,1024]{1,0:T(8,128)(2,1)} %collective-permute-done.4), channel_id=1, source_target_pairs={{0,1},{1,0},{2,3},{3,2},{4,5},{5,4},{6,7},{7,6},{8,9},{9,8},{10,11... | collective-permute-start | bytes 6291464 | tf_op jit(solution)/shard_map/ppermute | solution.py:50
  156.0 46.1 %collective-permute-start.9 = (bf16[1024,1024]{1,0:T(8,128)(2,1)}, bf16[1024,1024]{1,0:T(8,128)(2,1)}, u32[]{:S(2)}, u32[]{:S(2)}) collective-permute-start(bf16[1024,1024]{1,0:T(8,128)(2,1)} %param.6), channel_id=1, source_target_pairs={{2,0},{3,1},{4,2},{5,3},{6,4},{7,5},{10,8},{11,9},{12,10},{13,11},... | collective-permute-start | bytes 6291464 | tf_op jit(solution)/shard_map/ppermute | solution.py:43
  205.2 23.5 %collective-permute-start.10 = (bf16[1024,1024]{1,0:T(8,128)(2,1)}, bf16[1024,1024]{1,0:T(8,128)(2,1)S(1)}, u32[]{:S(2)}, u32[]{:S(2)}) collective-permute-start(bf16[1024,1024]{1,0:T(8,128)(2,1)} %get-tuple-element.64), channel_id=1, source_target_pairs={{0,1},{1,0},{2,3},{3,2},{4,5},{5,4},{6,7},{7,6},{8,9},{9,8},{10,11... | collective-permute-start | bytes 6291464 | tf_op jit(solution)/shard_map/ppermute | solution.py:50
  206.6 2.7 collective-permute-start.1
  207.8 2.4 collective-permute-start
  209.1 3.3 collective-permute-start.2
  228.7 1.3 copy-start.6
  230.0 97.1 %collective-permute-start.13 = (bf16[24,2,128,256]{3,2,1,0:T(8,128)(2,1)}, bf16[24,2,128,256]{3,2,1,0:T(8,128)(2,1)S(1)}, u32[]{:S(2)}, u32[]{:S(2)}) collective-permute-start(bf16[24,2,128,256]{3,2,1,0:T(8,128)(2,1)} %get-tuple-element.28), channel_id=1, source_target_pairs={{0,8},{8,0},{16,24},{24,16},{1,9},{9,1},{17,25},{25,17},{2,10},{10... | collective-permute-start | bytes 9437192 | tf_op jit(solution)/shard_map/ppermute | solution.py:27
  231.0 96.0 %collective-permute-start.14 = (bf16[24,2,128,256]{3,2,1,0:T(8,128)(2,1)}, bf16[24,2,128,256]{3,2,1,0:T(8,128)(2,1)}, u32[]{:S(2)}, u32[]{:S(2)}) collective-permute-start(bf16[24,2,128,256]{3,2,1,0:T(8,128)(2,1)} %get-tuple-element.29), channel_id=1, source_target_pairs={{0,16},{8,24},{16,0},{24,8},{1,17},{9,25},{17,1},{25,9},{2,18},{10... | collective-permute-start | bytes 9437192 | tf_op jit(solution)/shard_map/ppermute | solution.py:27
  264.9 0.8 copy-start.2
  264.9 1.9 copy-start.3
  266.8 54.7 %collective-permute-start.11 = (bf16[1024,512]{1,0:T(8,128)(2,1)}, bf16[1024,512]{1,0:T(8,128)(2,1)}, u32[]{:S(2)}, u32[]{:S(2)}) collective-permute-start(bf16[1024,512]{1,0:T(8,128)(2,1)} %pad_maximum_fusion.2), channel_id=1, source_target_pairs={{0,16},{8,24},{16,0},{24,8},{1,17},{9,25},{17,1},{25,9},{2,18},{10... | collective-permute-start | bytes 3145736 | tf_op jit(solution)/shard_map/ppermute | solution.py:27
  269.7 54.7 %collective-permute-start.12 = (bf16[1024,512]{1,0:T(8,128)(2,1)S(1)}, bf16[1024,512]{1,0:T(8,128)(2,1)S(1)}, u32[]{:S(2)}, u32[]{:S(2)}) collective-permute-start(bf16[1024,512]{1,0:T(8,128)(2,1)S(1)} %pad_maximum_fusion.3), channel_id=1, source_target_pairs={{0,8},{8,0},{16,24},{24,16},{1,9},{9,1},{17,25},{25,17},{2,10},{10... | collective-permute-start | bytes 3145736 | tf_op jit(solution)/shard_map/ppermute | solution.py:27
  327.1 1.6 copy-start
  343.6 3.3 collective-permute-start.15
  344.3 3.3 collective-permute-start.16
  347.0 0.7 copy-start.10
  347.6 0.6 copy-start.11
  366.7 21.2 %collective-permute-start.18 = (f32[1024,256]{1,0:T(8,128)}, f32[1024,256]{1,0:T(8,128)}, u32[]{:S(2)}, u32[]{:S(2)}) collective-permute-start(f32[1024,256]{1,0:T(8,128)} %get-tuple-element.35), channel_id=1, source_target_pairs={{0,8},{8,0},{16,24},{24,16},{1,9},{9,1},{17,25},{25,17},{2,10},{10... | collective-permute-start | bytes 3145736 | tf_op jit(solution)/shard_map/ppermute | solution.py:27
  367.9 22.0 %collective-permute-start.17 = (f32[1024,256]{1,0:T(8,128)}, f32[1024,256]{1,0:T(8,128)}, u32[]{:S(2)}, u32[]{:S(2)}) collective-permute-start(f32[1024,256]{1,0:T(8,128)} %get-tuple-element.33), channel_id=1, source_target_pairs={{0,16},{8,24},{16,0},{24,8},{1,17},{9,25},{17,1},{25,9},{2,18},{10... | collective-permute-start | bytes 3145736 | tf_op jit(solution)/shard_map/ppermute | solution.py:27
  383.1 131.5 %collective-permute-start.27 = (bf16[24,2,128,256]{3,2,1,0:T(8,128)(2,1)}, bf16[24,2,128,256]{3,2,1,0:T(8,128)(2,1)S(1)}, u32[]{:S(2)}, u32[]{:S(2)}) collective-permute-start(bf16[24,2,128,256]{3,2,1,0:T(8,128)(2,1)} %get-tuple-element.38), channel_id=1, source_target_pairs={{0,8},{8,0},{16,24},{24,16},{1,9},{9,1},{17,25},{25,17},{2,10},{10... | collective-permute-start | bytes 9437192 | tf_op jit(solution)/shard_map/ppermute | solution.py:27
  384.4 131.4 %collective-permute-start.28 = (bf16[24,2,128,256]{3,2,1,0:T(8,128)(2,1)}, bf16[24,2,128,256]{3,2,1,0:T(8,128)(2,1)}, u32[]{:S(2)}, u32[]{:S(2)}) collective-permute-start(bf16[24,2,128,256]{3,2,1,0:T(8,128)(2,1)} %get-tuple-element.39), channel_id=1, source_target_pairs={{0,16},{8,24},{16,0},{24,8},{1,17},{9,25},{17,1},{25,9},{2,18},{10... | collective-permute-start | bytes 9437192 | tf_op jit(solution)/shard_map/ppermute | solution.py:27
  399.0 36.4 %collective-permute-start.20 = (bf16[1024,512]{1,0:T(8,128)(2,1)}, bf16[1024,512]{1,0:T(8,128)(2,1)}, u32[]{:S(2)}, u32[]{:S(2)}) collective-permute-start(bf16[1024,512]{1,0:T(8,128)(2,1)} %get-tuple-element.73), channel_id=1, source_target_pairs={{0,4},{1,5},{2,6},{3,7},{4,0},{5,1},{6,2},{7,3},{8,12},{9,13},{10,... | collective-permute-start | bytes 3145736 | tf_op jit(solution)/shard_map/ppermute | solution.py:44
  405.4 31.3 %collective-permute-start.19 = (bf16[1024,512]{1,0:T(8,128)(2,1)}, bf16[1024,512]{1,0:T(8,128)(2,1)S(1)}, u32[]{:S(2)}, u32[]{:S(2)}) collective-permute-start(bf16[1024,512]{1,0:T(8,128)(2,1)} %get-tuple-element.73), channel_id=1, source_target_pairs={{0,1},{1,0},{2,3},{3,2},{4,5},{5,4},{6,7},{7,6},{8,9},{9,8},{10,11... | collective-permute-start | bytes 3145736 | tf_op jit(solution)/shard_map/ppermute | solution.py:50
  425.3 37.8 %collective-permute-start.22 = (bf16[1024,512]{1,0:T(8,128)(2,1)}, bf16[1024,512]{1,0:T(8,128)(2,1)S(1)}, u32[]{:S(2)}, u32[]{:S(2)}) collective-permute-start(bf16[1024,512]{1,0:T(8,128)(2,1)} %get-tuple-element.73), channel_id=1, source_target_pairs={{0,2},{1,3},{2,4},{3,5},{4,6},{5,7},{8,10},{9,11},{10,12},{11,13},... | collective-permute-start | bytes 3145736 | tf_op jit(solution)/shard_map/ppermute | solution.py:42
  435.5 47.9 %collective-permute-start.21 = (bf16[1024,512]{1,0:T(8,128)(2,1)}, bf16[1024,512]{1,0:T(8,128)(2,1)S(1)}, u32[]{:S(2)}, u32[]{:S(2)}) collective-permute-start(bf16[1024,512]{1,0:T(8,128)(2,1)} %collective-permute-done.20), channel_id=1, source_target_pairs={{4,6},{5,7},{2,0},{3,1},{12,14},{13,15},{10,8},{11,9},{20,22},{21,... | collective-permute-start | bytes 3145736 | tf_op jit(solution)/shard_map/ppermute | solution.py:45
  483.4 31.2 %copy-start.4 = (bf16[1024,512]{1,0:T(8,128)(2,1)}, bf16[1024,512]{1,0:T(8,128)(2,1)S(1)}, u32[]{:S(2)}) copy-start(bf16[1024,512]{1,0:T(8,128)(2,1)S(1)} %collective-permute-done.21) | copy-start | bytes 3145732
  485.1 73.2 %collective-permute-start.23 = (bf16[1024,512]{1,0:T(8,128)(2,1)}, bf16[1024,512]{1,0:T(8,128)(2,1)}, u32[]{:S(2)}, u32[]{:S(2)}) collective-permute-start(bf16[1024,512]{1,0:T(8,128)(2,1)} %get-tuple-element.62), channel_id=1, source_target_pairs={{0,1},{1,0},{2,3},{3,2},{4,5},{5,4},{6,7},{7,6},{8,9},{9,8},{10,11... | collective-permute-start | bytes 3145736 | tf_op jit(solution)/shard_map/ppermute | solution.py:50
  488.1 75.0 %collective-permute-start.24 = (bf16[1024,512]{1,0:T(8,128)(2,1)}, bf16[1024,512]{1,0:T(8,128)(2,1)}, u32[]{:S(2)}, u32[]{:S(2)}) collective-permute-start(bf16[1024,512]{1,0:T(8,128)(2,1)} %collective-permute-done.20), channel_id=1, source_target_pairs={{0,1},{1,0},{2,3},{3,2},{4,5},{5,4},{6,7},{7,6},{8,9},{9,8},{10,11... | collective-permute-start | bytes 3145736 | tf_op jit(solution)/shard_map/ppermute | solution.py:50
  488.1 77.3 %collective-permute-start.25 = (bf16[1024,512]{1,0:T(8,128)(2,1)}, bf16[1024,512]{1,0:T(8,128)(2,1)}, u32[]{:S(2)}, u32[]{:S(2)}) collective-permute-start(bf16[1024,512]{1,0:T(8,128)(2,1)} %get-tuple-element.73), channel_id=1, source_target_pairs={{2,0},{3,1},{4,2},{5,3},{6,4},{7,5},{10,8},{11,9},{12,10},{13,11},... | collective-permute-start | bytes 3145736 | tf_op jit(solution)/shard_map/ppermute | solution.py:43
  514.6 1.7 copy-start.1
  531.2 5.3 collective-permute-start.29
  532.2 33.1 %copy-start.5 = (bf16[1024,512]{1,0:T(8,128)(2,1)S(1)}, bf16[1024,512]{1,0:T(8,128)(2,1)}, u32[]{:S(2)}) copy-start(bf16[1024,512]{1,0:T(8,128)(2,1)} %copy-done.4) | copy-start | bytes 3145732
  532.2 5.3 collective-permute-start.30
  536.4 1.1 copy-start.8
  537.5 0.6 copy-start.9
  556.4 42.8 %collective-permute-start.32 = (f32[1024,256]{1,0:T(8,128)}, f32[1024,256]{1,0:T(8,128)}, u32[]{:S(2)}, u32[]{:S(2)}) collective-permute-start(f32[1024,256]{1,0:T(8,128)} %get-tuple-element.45), channel_id=1, source_target_pairs={{0,8},{8,0},{16,24},{24,16},{1,9},{9,1},{17,25},{25,17},{2,10},{10... | collective-permute-start | bytes 3145736 | tf_op jit(solution)/shard_map/ppermute | solution.py:27
  557.5 43.4 %collective-permute-start.31 = (f32[1024,256]{1,0:T(8,128)}, f32[1024,256]{1,0:T(8,128)S(1)}, u32[]{:S(2)}, u32[]{:S(2)}) collective-permute-start(f32[1024,256]{1,0:T(8,128)} %get-tuple-element.43), channel_id=1, source_target_pairs={{0,16},{8,24},{16,0},{24,8},{1,17},{9,25},{17,1},{25,9},{2,18},{10... | collective-permute-start | bytes 3145736 | tf_op jit(solution)/shard_map/ppermute | solution.py:27
  566.7 35.6 %collective-permute-start.26 = (bf16[1024,512]{1,0:T(8,128)(2,1)S(1)}, bf16[1024,512]{1,0:T(8,128)(2,1)S(1)}, u32[]{:S(2)}, u32[]{:S(2)}) collective-permute-start(bf16[1024,512]{1,0:T(8,128)(2,1)S(1)} %get-tuple-element.60), channel_id=1, source_target_pairs={{0,1},{1,0},{2,3},{3,2},{4,5},{5,4},{6,7},{7,6},{8,9},{9,8},{10,11... | collective-permute-start | bytes 3145736 | tf_op jit(solution)/shard_map/ppermute | solution.py:50
  604.9 47.7 %collective-permute-start.34 = (bf16[1024,512]{1,0:T(8,128)(2,1)}, bf16[1024,512]{1,0:T(8,128)(2,1)S(1)}, u32[]{:S(2)}, u32[]{:S(2)}) collective-permute-start(bf16[1024,512]{1,0:T(8,128)(2,1)} %get-tuple-element.71), channel_id=1, source_target_pairs={{0,4},{1,5},{2,6},{3,7},{4,0},{5,1},{6,2},{7,3},{8,12},{9,13},{10,... | collective-permute-start | bytes 3145736 | tf_op jit(solution)/shard_map/ppermute | solution.py:44
  611.8 42.1 %collective-permute-start.33 = (bf16[1024,512]{1,0:T(8,128)(2,1)}, bf16[1024,512]{1,0:T(8,128)(2,1)}, u32[]{:S(2)}, u32[]{:S(2)}) collective-permute-start(bf16[1024,512]{1,0:T(8,128)(2,1)} %get-tuple-element.71), channel_id=1, source_target_pairs={{0,1},{1,0},{2,3},{3,2},{4,5},{5,4},{6,7},{7,6},{8,9},{9,8},{10,11... | collective-permute-start | bytes 3145736 | tf_op jit(solution)/shard_map/ppermute | solution.py:50
  628.2 41.5 %collective-permute-start.36 = (bf16[1024,512]{1,0:T(8,128)(2,1)}, bf16[1024,512]{1,0:T(8,128)(2,1)S(1)}, u32[]{:S(2)}, u32[]{:S(2)}) collective-permute-start(bf16[1024,512]{1,0:T(8,128)(2,1)} %get-tuple-element.71), channel_id=1, source_target_pairs={{0,2},{1,3},{2,4},{3,5},{4,6},{5,7},{8,10},{9,11},{10,12},{11,13},... | collective-permute-start | bytes 3145736 | tf_op jit(solution)/shard_map/ppermute | solution.py:42
  652.6 17.1 %copy-start.7 = (bf16[1024,512]{1,0:T(8,128)(2,1)}, bf16[1024,512]{1,0:T(8,128)(2,1)S(1)}, u32[]{:S(2)}) copy-start(bf16[1024,512]{1,0:T(8,128)(2,1)S(1)} %collective-permute-done.34) | copy-start | bytes 3145732
  652.6 39.6 %collective-permute-start.35 = (bf16[1024,512]{1,0:T(8,128)(2,1)S(1)}, bf16[1024,512]{1,0:T(8,128)(2,1)S(1)}, u32[]{:S(2)}, u32[]{:S(2)}) collective-permute-start(bf16[1024,512]{1,0:T(8,128)(2,1)S(1)} %collective-permute-done.34), channel_id=1, source_target_pairs={{4,6},{5,7},{2,0},{3,1},{12,14},{13,15},{10,8},{11,9},{20,22},{21,... | collective-permute-start | bytes 3145736 | tf_op jit(solution)/shard_map/ppermute | solution.py:45
  693.5 3.2 collective-permute-start.37
  694.3 7.1 collective-permute-start.38
  694.3 23.8 %collective-permute-start.39 = (bf16[1024,512]{1,0:T(8,128)(2,1)}, bf16[1024,512]{1,0:T(8,128)(2,1)S(1)}, u32[]{:S(2)}, u32[]{:S(2)}) collective-permute-start(bf16[1024,512]{1,0:T(8,128)(2,1)} %get-tuple-element.71), channel_id=1, source_target_pairs={{2,0},{3,1},{4,2},{5,3},{6,4},{7,5},{10,8},{11,9},{12,10},{13,11},... | collective-permute-start | bytes 3145736 | tf_op jit(solution)/shard_map/ppermute | solution.py:43
  719.5 3.4 collective-permute-start.40
Sparse Core Ops, SparseCore 0:
  9.2 158.0 all-gather.2
  366.8 252.7 all-gather.4

commit v4 on v3

--- a/solution.py
+++ b/solution.py
@@ -39,15 +39,23 @@
     def chip_pairs(pairs):
         return [(a * 2 + c, b * 2 + c) for a, b in pairs for c in range(2)]
 
+    def swap(value):
+        return lax.ppermute(value, "fsdp", [(i, i ^ 1) for i in range(members)])
+
+    back2 = lax.ppermute(piece, "fsdp", chip_pairs([(0, 2), (1, 3), (2, 0), (3, 1)]))
     back1 = lax.ppermute(piece, "fsdp", chip_pairs([(0, 1), (1, 2), (2, 3)]))
     back3 = lax.ppermute(piece, "fsdp", chip_pairs([(1, 0), (2, 1), (3, 2)]))
-    back2 = lax.ppermute(piece, "fsdp", chip_pairs([(0, 2), (1, 3), (2, 0), (3, 1)]))
+    own_there = swap(piece)
     ends = lax.ppermute(back2, "fsdp", chip_pairs([(2, 3), (1, 0)]))
-    back1 = jnp.where(chip == 0, ends, back1)
-    back3 = jnp.where(chip == 3, ends, back3)
+    there1, there2, there3 = swap(back1), swap(back2), swap(back3)
+    ends_there = lax.ppermute(ends, "fsdp", [(0, 1), (1, 0), (6, 7), (7, 6)])
     found = []
-    for step, here in enumerate((piece, back1, back2, back3)):
-        there = lax.ppermute(here, "fsdp", [(i, i ^ 1) for i in range(members)])
+    for step, (here, there) in enumerate((
+        (piece, own_there),
+        (jnp.where(chip == 0, ends, back1), jnp.where(chip == 0, ends_there, there1)),
+        (back2, there2),
+        (jnp.where(chip == 3, ends, back3), jnp.where(chip == 3, ends_there, there3)),
+    )):
         owner = (chip + 4 - step) % 4
         found.append((owner * 2 + core, here))
         found.append((owner * 2 + 1 - core, there))
@@ -56,35 +64,32 @@
 
 def pick_kernel(first_ref, second_ref, *refs):
     for axis in range(AXES):
-        refs[AXES + axis][...] = refs[axis][...]
+        for plane in range(2):
+            refs[AXES + axis * 2 + plane][...] = refs[axis][:, plane]
 
 
 def pick_blocks(stored, tables, step, part):
     count = tables[0].shape[0]
     _, two, block_size, _ = stored.shape
-    shape = (1, two, block_size, part)
     return pl.pallas_call(
         pick_kernel,
         grid_spec=pltpu.PrefetchScalarGridSpec(
             num_scalar_prefetch=AXES,
             grid=(count,),
             in_specs=[
-                pl.BlockSpec(shape, lambda i, *t, axis=axis: (t[axis][i], 0, 0, step * AXES + axis))
+                pl.BlockSpec(
+                    (1, two, block_size, part), lambda i, *t, axis=axis: (t[axis][i], 0, 0, step * AXES + axis)
+                )
                 for axis in range(AXES)
             ],
-            out_specs=[pl.BlockSpec(shape, lambda i, *t: (i, 0, 0, 0))] * AXES,
+            out_specs=[pl.BlockSpec((1, block_size, part), lambda i, *t: (i, 0, 0))] * (2 * AXES),
         ),
-        out_shape=[jax.ShapeDtypeStruct((count,) + shape[1:], stored.dtype)] * AXES,
+        out_shape=[jax.ShapeDtypeStruct((count, block_size, part), stored.dtype)] * (2 * AXES),
         cost_estimate=pl.CostEstimate(
             flops=0, transcendentals=0, bytes_accessed=count * two * block_size * part * 4 * AXES
         ),
         name="pick",
     )(*tables, *[stored] * AXES)
-
-
-def send_blocks(picked, after):
-    picked, _ = lax.optimization_barrier((picked, after))
-    return [over_dp(picked[axis], 1 << axis) for axis in range(AXES)]
 
 
 def scores_of(query, keys, present):
@@ -114,7 +119,7 @@
                 here_columns = head_columns(axis * (part // HEAD_DIM) + head)
                 query = query_refs[axis][rows, columns]
                 here = scores_of(query, here_ref[here_block, 0, :, here_columns], here_at >= 0)
-                far = scores_of(query, far_refs[axis][far_block, 0, :, columns], far_at >= 0)
+                far = scores_of(query, far_refs[axis][far_block, :, columns], far_at >= 0)
                 lane = (in_group * (part // HEAD_DIM) + head) * 2
                 units.append((axis, rows, columns, here_block, here_columns, far_block, lane, here, far))
     return units
@@ -123,7 +128,7 @@
 def stats_kernel(spans, span, together, *refs):
     index_refs, refs = refs[:2 * AXES], refs[2 * AXES:]
     query_refs, here_ref, far_refs, out_refs = refs[:AXES], refs[AXES], refs[AXES + 1:2 * AXES + 1], refs[2 * AXES + 1:]
-    per_step = query_refs[0].shape[0] // span
+    turns = query_refs[0].shape[0] // span // together
 
     @pl.when(pl.program_id(1) == 0)
     def _():
@@ -148,14 +153,16 @@
             out_refs[axis][0] = kept
         return carry
 
-    lax.fori_loop(0, per_step // together, some, 0)
+    lax.fori_loop(0, turns, some, 0)
 
 
 def mix_kernel(spans, span, together, *refs):
     index_refs, refs = refs[:2 * AXES], refs[2 * AXES:]
-    query_refs, here_ref, far_refs, refs = refs[:AXES], refs[AXES], refs[AXES + 1:2 * AXES + 1], refs[2 * AXES + 1:]
-    mine_refs, their_refs, keep_refs, send_refs = (refs[i * AXES:(i + 1) * AXES] for i in range(4))
-    per_step = query_refs[0].shape[0] // span
+    query_refs, here_ref, refs = refs[:AXES], refs[AXES], refs[AXES + 1:]
+    far_refs, value_refs, mine_refs, their_refs, keep_refs, send_refs = (
+        refs[i * AXES:(i + 1) * AXES] for i in range(6)
+    )
+    turns = query_refs[0].shape[0] // span // together
     lanes = lax.broadcasted_iota(jnp.int32, mine_refs[0].shape[1:], 1)
 
     def column(stats, at):
@@ -178,7 +185,7 @@
         ]
         for (axis, rows, columns, here_block, here_columns, far_block, _, _, _), weight in zip(units, weights):
             values = jnp.concatenate(
-                [here_ref[here_block, 1, :, here_columns], far_refs[axis][far_block, 1, :, columns]], axis=0
+                [here_ref[here_block, 1, :, here_columns], value_refs[axis][far_block, :, columns]], axis=0
             )
             out_refs[axis][rows, columns] = jnp.dot(weight, values, preferred_element_type=jnp.float32)
         return carry
@@ -186,23 +193,22 @@
     for group, out_refs in enumerate((keep_refs, send_refs)):
         @pl.when(pl.program_id(0) == group)
         def _(out_refs=out_refs):
-            lax.fori_loop(0, per_step // together, functools.partial(some, out_refs), 0)
+            lax.fori_loop(0, turns, functools.partial(some, out_refs), 0)
 
 
 def span_call(kernel, indices, queries, stored, received, stats, step, part, spans, planes):
     rows = queries[0].shape[0] // 2
     span = rows // spans
     count, _, block_size, _ = stored.shape
+    slots = received[0].shape[0]
     per_step = 8 if spans % 8 == 0 else spans
     steps = spans // per_step
     together = 2 if per_step % 2 == 0 else 1
     step_rows = per_step * span
 
-    in_specs = [pl.BlockSpec((step_rows, part), lambda c, i, *t: (c * steps + i, step))] * AXES
+    in_specs = [pl.BlockSpec((step_rows, part), lambda c, i, *t: (c * steps + i, 0))] * AXES
     in_specs += [pl.BlockSpec((count, planes, block_size, AXES * part), lambda c, i, *t: (0, 0, 0, step))]
-    in_specs += [
-        pl.BlockSpec((received[0].shape[0], planes, block_size, part), lambda c, i, *t: (0, 0, 0, 0))
-    ] * AXES
+    in_specs += [pl.BlockSpec((slots, block_size, part), lambda c, i, *t: (0, 0, 0))] * (planes * AXES)
     if stats:
         in_specs += [pl.BlockSpec((1, span, LANES), lambda c, i, *t: (c, 0, 0))] * AXES
         in_specs += [pl.BlockSpec((1, span, LANES), lambda c, i, *t: (1 - c, 0, 0))] * AXES
@@ -224,7 +230,7 @@
         cost_estimate=pl.CostEstimate(
             flops=8 * rows * NEIGH * block_size * part * AXES * planes,
             transcendentals=2 * rows * NEIGH * block_size * part * AXES // HEAD_DIM,
-            bytes_accessed=(count + received[0].shape[0]) * planes * block_size * part * 2 * AXES,
+            bytes_accessed=(count + slots) * planes * block_size * part * 2 * AXES,
         ),
         name="mix" if stats else "stats",
     )(*indices, *queries, stored, *received, *stats)
@@ -260,6 +266,10 @@
     return sends, places
 
 
+def after(values, marker):
+    return lax.optimization_barrier((values, marker))[0]
+
+
 def work(tokens, w_query, w_output, neighbor_shard, neighbor_block, kv_store):
     local_width = w_query.shape[1]
     row_count, width = tokens.shape
@@ -267,50 +277,67 @@
     members = lax.axis_size("fsdp")
     passes = 2 if local_width % (2 * AXES * HEAD_DIM) == 0 else 1
     part = local_width // (passes * AXES)
+    share = AXES * part
     span_count = neighbor_shard.shape[0]
     capacity = max(2, 3 * span_count * NEIGH // (2 * peers))
 
-    w_query_columns = lax.all_gather(w_query, "dp", axis=0, tiled=True)
-
     sends, places = exchange_tables(neighbor_shard, neighbor_block, capacity)
     stored = kv_store[0]
-    picked = [pick_blocks(stored, sends, step, part) for step in range(passes)]
+    picked = []
+    for step in range(passes):
+        picked.append(pick_blocks(stored, sends, step, part))
+
+    def query_columns(step):
+        columns = w_query[:, step * share:(step + 1) * share]
+        if step > 0:
+            columns = after(columns, picked[0])
+        return lax.all_gather(columns, "dp", axis=0, tiled=True)
+
+    def send_blocks(step, plane, marker):
+        blocks = [picked[step][axis * 2 + plane] for axis in range(AXES)]
+        if marker is not None:
+            blocks = after(blocks, marker)
+        return [over_dp(blocks[axis], 1 << axis) for axis in range(AXES)]
 
     pieces = pieces_over_fsdp(tokens)
-    received = [send_blocks(picked[0], pieces[-1][1])]
-
     gathered = jnp.zeros((row_count, members * width), tokens.dtype)
     for owner, piece in pieces:
         gathered = lax.dynamic_update_slice(gathered, piece, (0, owner * width))
     normed = normalize(gathered)
-    queries = jnp.dot(normed, w_query_columns, preferred_element_type=jnp.float32).astype(jnp.bfloat16)
-
-    asked = []
-    for axis in range(AXES):
-        starts = [(step * AXES + axis) * part for step in range(passes)]
-        own = jnp.concatenate([queries[:, start:start + part] for start in starts], axis=1)
-        asked.append(jnp.concatenate([own, over_dp(own, 3 ^ (1 << axis))], axis=0))
-    for step in range(1, passes):
-        received.append(send_blocks(picked[step], asked[0]))
+
+    columns = [query_columns(step) for step in range(passes)]
+    received = [[send_blocks(0, plane, None) for plane in range(2)]]
+    asked, own_queries = [], []
+    for step in range(passes):
+        queries = jnp.dot(normed, columns[step], preferred_element_type=jnp.float32).astype(jnp.bfloat16)
+        own_queries.append(queries)
+        parts = [queries[:, axis * part:(axis + 1) * part] for axis in range(AXES)]
+        asked.append([
+            jnp.concatenate([parts[axis], over_dp(parts[axis], 3 ^ (1 << axis))], axis=0) for axis in range(AXES)
+        ])
+        if step > 0:
+            received.append([send_blocks(step, 0, own_queries[0]), send_blocks(step, 1, queries)])
+    w_output = after(w_output, own_queries[-1])
+    w_output_columns = lax.all_gather(w_output, "dp", axis=0, tiled=True)
 
     attended = jnp.zeros((row_count, members * local_width), jnp.bfloat16)
     for step in range(passes):
         common = dict(step=step, part=part, spans=span_count)
         mine = span_call(
-            stats_kernel, places, asked, stored, received[step], [], planes=1, **common
+            stats_kernel, places, asked[step], stored, received[step][0], [], planes=1, **common
         )
         theirs = [over_dp(mine[axis], 3 ^ (1 << axis)) for axis in range(AXES)]
-        partial = span_call(mix_kernel, places, asked, stored, received[step], list(mine) + theirs, planes=2, **common)
-        if step == 0:
-            w_output, _ = lax.optimization_barrier((w_output, partial))
-            w_output_columns = lax.all_gather(w_output, "dp", axis=0, tiled=True)
+        partial = span_call(
+            mix_kernel, places, asked[step], stored, received[step][0] + received[step][1], list(mine) + theirs,
+            planes=2, **common
+        )
         others = [over_dp(partial[AXES + axis], 3 ^ (1 << axis)) for axis in range(AXES)]
         mixed = jnp.concatenate(
             [(partial[axis] + others[axis]).astype(jnp.bfloat16) for axis in range(AXES)], axis=1
         )
         pieces = pieces_over_fsdp(mixed)
         for owner, piece in pieces:
-            start = owner * local_width + step * AXES * part
+            start = owner * local_width + step * share
             attended = lax.dynamic_update_slice(attended, piece, (0, start))
     summed = jnp.dot(attended, w_output_columns, preferred_element_type=jnp.float32)
     return summed.astype(jnp.bfloat16)

time: 758 us -> 836 us (1.10)
  the two profiles are of different devices: /device:TPU:25 before, /device:TPU:0 now
where the time goes in v4:
time: 836 us; the launch traced here: 834 us
  waiting for transfers between devices  516 us (62%)
  Pallas kernels  95.3 us (11%)
  starting transfers between devices  61.4 us (7%)
  matrix products  57.1 us (7%)
  other arithmetic  46.9 us (6%)
  local copies, waits for them, and re-layouts  44.2 us (5%)
  between operations  13.5 us (2%)
    ppermute x23, waiting for transfers between devices, over_dp(): lax.ppermute(value, 'dp', [(i, i ^ bit) for i in range(lax.axis_size('dp'...  231 us
    ppermute x3, waiting for transfers between devices, pieces_over_fsdp(): lax.ppermute(piece, 'fsdp', chip_pairs([(0, 2), (1, 3), (2, 0), (3, 1)]))  128 us
    ppermute x3, waiting for transfers between devices, pieces_over_fsdp(): ends = lax.ppermute(back2, 'fsdp', chip_pairs([(2, 3), (1, 0)]))  82.2 us
    ppermute x3, waiting for transfers between devices, pieces_over_fsdp(): back3 = lax.ppermute(piece, 'fsdp', chip_pairs([(1, 0), (2, 1), (3, 2)]))  73.9 us
    pallas_call x4, Pallas kernels, span_call(): pl.pallas_call(functools.partial(kernel, spans, span, together), grid_spe...  66.8 us
    dot_general x2, matrix products, work(): jnp.dot(normed, columns[step], preferred_element_type=jnp.float32)  33.9 us
    pallas_call x2, Pallas kernels, pick_blocks(): pl.pallas_call(pick_kernel, grid_spec=pltpu.PrefetchScalarGridSpec(num_sc...  28.6 us
    ppermute x23, starting transfers between devices, over_dp(): lax.ppermute(value, 'dp', [(i, i ^ bit) for i in range(lax.axis_size('dp'...  26.1 us
  transfers between devices with their start and end apart: 53, of which 18 were waited for; matrix products, arithmetic and copies ran while one was open for 13% of the time, Pallas kernels for 10%

profile of v4, /device:TPU:0, one launch (start us, length us, event | category | flops | bytes accessed | tf_op | source)
XLA Modules:
  0.0 834.3 jit_solution(8870814117927486655)
XLA Ops:
  7.2 3.0 collective-permute-start.1
  10.2 1.5 collective-permute-start
  11.8 4.6 fusion.21
  18.2 14.3 %pick.2 = (bf16[24,128,256]{2,1,0:T(8,128)(2,1)}, bf16[24,128,256]{2,1,0:T(8,128)(2,1)}, bf16[24,128,256]{2,1,0:T(8,128)(2,1)}, bf16[24,128,256]{2,1,0:T(8,128)(2,1)}) custom-call(s32[24]{0:T(128)} %get-tuple-element.80.first_ref, s32[24]{0:T(128)} %get-tuple-element.79.second_ref, bf16[32,2,128,1024]{3,2,1,0:T(8,128)(2,1)} %bitcast.28, ...), custom_call_target="tpu_custom_call" | custom-call | bytes 12582912 | tf_op jit(solution)/shard_map/pick/pallas_call | solution.py:74
  33.3 3.1 collective-permute-start.4
  36.4 4.8 collective-permute-start.6
  41.2 85.3 %collective-permute-done.4 = bf16[1024,1024]{1,0:T(8,128)(2,1)} collective-permute-done((bf16[1024,1024]{1,0:T(8,128)(2,1)}, bf16[1024,1024]{1,0:T(8,128)(2,1)}, u32[]{:S(2)}, u32[]{:S(2)}) %collective-permute-start.4) | collective-permute-done | bytes 2097184 | tf_op jit(solution)/shard_map/ppermute | solution.py:45
  129.6 47.4 %collective-permute-done.5 = bf16[1024,1024]{1,0:T(8,128)(2,1)S(1)} collective-permute-done((bf16[1024,1024]{1,0:T(8,128)(2,1)}, bf16[1024,1024]{1,0:T(8,128)(2,1)S(1)}, u32[]{:S(2)}, u32[]{:S(2)}) %collective-permute-start.5) | collective-permute-done | bytes 2097184 | tf_op jit(solution)/shard_map/ppermute | solution.py:49
  177.0 1.9 collective-permute-start.7
  179.5 40.6 %collective-permute-done.10 = bf16[1024,1024]{1,0:T(8,128)(2,1)} collective-permute-done((bf16[1024,1024]{1,0:T(8,128)(2,1)}, bf16[1024,1024]{1,0:T(8,128)(2,1)}, u32[]{:S(2)}, u32[]{:S(2)}) %collective-permute-start.10) | collective-permute-done | bytes 2097184 | tf_op jit(solution)/shard_map/ppermute | solution.py:47
  220.1 1.6 broadcast.77.clone
  221.7 1.9 constant_dynamic-update-slice_fusion.11
  223.6 1.9 constant_dynamic-update-slice_fusion.10
  226.7 2.8 select_dynamic-update-slice_fusion.2
  229.5 1.9 constant_dynamic-update-slice_fusion.9
  231.4 1.9 constant_dynamic-update-slice_fusion.8
  233.3 2.8 select_dynamic-update-slice_fusion.1
  236.0 2.8 select_dynamic-update-slice_fusion
  238.8 5.8 copy-done
  244.6 3.9 fusion
  248.6 15.8 %fusion.9 = bf16[1024,512]{1,0:T(8,128)(2,1)} fusion(bf16[8192,512]{1,0:T(8,128)(2,1)} %all-gather.6.cloned.1.call-done, bf16[1024,8192]{1,0:T(8,128)(2,1)} %copy-done, f32[1024]{0:T(1024)S(1)} %add_rsqrt_fusion), kind=kOutput, calls=%fused_computation.12 | convolution fusion | flops 8615624704 | bytes 26218496 | tf_op jit(solution)/shard_map/dot_general | solution.py:312
  264.5 2.5 collective-permute-start.14
  267.4 1.9 collective-permute-start.16
  269.3 18.1 %fusion.6 = bf16[1024,512]{1,0:T(8,128)(2,1)S(1)} fusion(bf16[8192,512]{1,0:T(8,128)(2,1)} %all-gather.4.cloned.1.call-done, bf16[1024,8192]{1,0:T(8,128)(2,1)} %copy-done, f32[1024]{0:T(1024)S(1)} %add_rsqrt_fusion), kind=kOutput, calls=%fused_computation.11 | convolution fusion | flops 8615624704 | bytes 26218496 | tf_op jit(solution)/shard_map/dot_general | solution.py:312
  288.5 2.0 collective-permute-start.12
  291.2 122.5 %collective-permute-done.12 = bf16[1024,256]{1,0:T(8,128)(2,1)} collective-permute-done((bf16[1024,256]{1,0:T(8,128)(2,1)}, bf16[1024,256]{1,0:T(8,128)(2,1)}, u32[]{:S(2)}, u32[]{:S(2)}) %collective-permute-start.12) | collective-permute-done | bytes 524320 | tf_op jit(solution)/shard_map/ppermute | solution.py:27
  415.2 2.3 pad_maximum_fusion.refs_4_
  417.5 21.3 %collective-permute-done.13 = bf16[1024,256]{1,0:T(8,128)(2,1)S(1)} collective-permute-done((bf16[1024,256]{1,0:T(8,128)(2,1)}, bf16[1024,256]{1,0:T(8,128)(2,1)S(1)}, u32[]{:S(2)}, u32[]{:S(2)}) %collective-permute-start.13) | collective-permute-done | bytes 524320 | tf_op jit(solution)/shard_map/ppermute | solution.py:27
  438.9 2.1 pad_maximum_fusion.1.refs_5_
  442.7 14.9 %stats.2 = (f32[2,64,128]{2,1,0:T(8,128)}, f32[2,64,128]{2,1,0:T(8,128)}) custom-call(s32[32]{0:T(128)} %get-tuple-element.82.refs_0_, s32[32]{0:T(128)} %get-tuple-element.83.refs_1_, s32[32]{0:T(128)} %get-tuple-element.81.refs_2_, s32[32]{0:T(128)} %pad_add_fusion.5.refs_3_, bf16[2048,256]{1,0:T(8,128)(2,1)} %pad_maximum_fusion.refs_4_, ...), custom_call_target="tpu_custom_call" | custom-call | flops 1073741824 | bytes 7340032 | tf_op jit(solution)/shard_map/stats/pallas_call | solution.py:221
  458.9 1.6 collective-permute-start.19
  460.5 3.1 collective-permute-done.18.refs_13_
  465.5 18.5 %mix.2 = (f32[1024,256]{1,0:T(8,128)}, f32[1024,256]{1,0:T(8,128)}, f32[1024,256]{1,0:T(8,128)}, f32[1024,256]{1,0:T(8,128)}) custom-call(s32[32]{0:T(128)} %get-tuple-element.82.refs_0_, s32[32]{0:T(128)} %get-tuple-element.83.refs_1_, s32[32]{0:T(128)} %get-tuple-element.81.refs_2_, s32[32]{0:T(128)} %pad_add_fusion.5.refs_3_, ...), custom_call_target="tpu_custom_call" | custom-call | flops 2147483648 | bytes 14680064 | tf_op jit(solution)/shard_map/mix/pallas_call | solution.py:221
  484.0 1.7 collective-permute-start.21
  488.7 14.3 %pick.3 = (bf16[24,128,256]{2,1,0:T(8,128)(2,1)}, bf16[24,128,256]{2,1,0:T(8,128)(2,1)}, bf16[24,128,256]{2,1,0:T(8,128)(2,1)}, bf16[24,128,256]{2,1,0:T(8,128)(2,1)}) custom-call(s32[24]{0:T(128)} %get-tuple-element.80.first_ref, s32[24]{0:T(128)} %get-tuple-element.79.second_ref, bf16[32,2,128,1024]{3,2,1,0:T(8,128)(2,1)} %bitcast.32, ...), custom_call_target="tpu_custom_call" | custom-call | bytes 12582912 | tf_op jit(solution)/shard_map/pick/pallas_call | solution.py:74
  505.0 18.2 %collective-permute-done.31 = bf16[1024,256]{1,0:T(8,128)(2,1)} collective-permute-done((bf16[1024,256]{1,0:T(8,128)(2,1)}, bf16[1024,256]{1,0:T(8,128)(2,1)}, u32[]{:S(2)}, u32[]{:S(2)}) %collective-permute-start.31) | collective-permute-done | bytes 524320 | tf_op jit(solution)/shard_map/ppermute | solution.py:27
  524.5 2.3 pad_maximum_fusion.3.refs_4_
  528.2 1.6 add_convert_fusion.2
  529.9 1.6 add_convert_fusion.3
  531.5 6.0 broadcast.77
  538.9 46.1 %collective-permute-done.32 = bf16[1024,256]{1,0:T(8,128)(2,1)S(1)} collective-permute-done((bf16[1024,256]{1,0:T(8,128)(2,1)}, bf16[1024,256]{1,0:T(8,128)(2,1)S(1)}, u32[]{:S(2)}, u32[]{:S(2)}) %collective-permute-start.32) | collective-permute-done | bytes 524320 | tf_op jit(solution)/shard_map/ppermute | solution.py:27
  588.4 14.9 %stats.3 = (f32[2,64,128]{2,1,0:T(8,128)}, f32[2,64,128]{2,1,0:T(8,128)}) custom-call(s32[32]{0:T(128)} %get-tuple-element.82.refs_0_, s32[32]{0:T(128)} %get-tuple-element.83.refs_1_, s32[32]{0:T(128)} %get-tuple-element.81.refs_2_, s32[32]{0:T(128)} %pad_add_fusion.5.refs_3_, bf16[2048,256]{1,0:T(8,128)(2,1)} %pad_maximum_fusion.3.refs_4_, ...), custom_call_target="tpu_custom_call" | custom-call | flops 1073741824 | bytes 7340032 | tf_op jit(solution)/shard_map/stats/pallas_call | solution.py:221
  603.3 1.5 collective-permute-start.37
  605.1 2.6 collective-permute-done.37.refs_13_
  607.7 1.5 collective-permute-done.38.refs_14_
  609.9 18.4 %mix.3 = (f32[1024,256]{1,0:T(8,128)}, f32[1024,256]{1,0:T(8,128)}, f32[1024,256]{1,0:T(8,128)}, f32[1024,256]{1,0:T(8,128)}) custom-call(s32[32]{0:T(128)} %get-tuple-element.82.refs_0_, s32[32]{0:T(128)} %get-tuple-element.83.refs_1_, s32[32]{0:T(128)} %get-tuple-element.81.refs_2_, s32[32]{0:T(128)} %pad_add_fusion.5.refs_3_, ...), custom_call_target="tpu_custom_call" | custom-call | flops 2147483648 | bytes 14680064 | tf_op jit(solution)/shard_map/mix/pallas_call | solution.py:221
  628.7 4.0 collective-permute-start.25
  635.4 13.9 %collective-permute-done.40 = f32[1024,256]{1,0:T(8,128)S(1)} collective-permute-done((f32[1024,256]{1,0:T(8,128)}, f32[1024,256]{1,0:T(8,128)S(1)}, u32[]{:S(2)}, u32[]{:S(2)}) %collective-permute-start.40) | collective-permute-done | bytes 1048608 | tf_op jit(solution)/shard_map/ppermute | solution.py:27
  650.8 10.0 %collective-permute-done.24 = bf16[1024,512]{1,0:T(8,128)(2,1)S(1)} collective-permute-done((bf16[1024,512]{1,0:T(8,128)(2,1)}, bf16[1024,512]{1,0:T(8,128)(2,1)S(1)}, u32[]{:S(2)}, u32[]{:S(2)}) %collective-permute-start.24) | collective-permute-done | bytes 1048608 | tf_op jit(solution)/shard_map/ppermute | solution.py:49
  660.9 2.1 collective-permute-start.26
  663.0 1.6 add_convert_fusion
  665.2 14.5 %collective-permute-done.29 = bf16[1024,512]{1,0:T(8,128)(2,1)} collective-permute-done((bf16[1024,512]{1,0:T(8,128)(2,1)}, bf16[1024,512]{1,0:T(8,128)(2,1)}, u32[]{:S(2)}, u32[]{:S(2)}) %collective-permute-start.29) | collective-permute-done | bytes 1048608 | tf_op jit(solution)/shard_map/ppermute | solution.py:47
  680.8 1.6 add_convert_fusion.1
  685.2 2.3 constant_dynamic-update-slice_fusion.5
  688.6 2.5 select_dynamic-update-slice_fusion.9
  695.3 5.3 collective-permute-start.44
  700.6 42.5 %collective-permute-done.42 = bf16[1024,512]{1,0:T(8,128)(2,1)S(1)} collective-permute-done((bf16[1024,512]{1,0:T(8,128)(2,1)}, bf16[1024,512]{1,0:T(8,128)(2,1)S(1)}, u32[]{:S(2)}, u32[]{:S(2)}) %collective-permute-start.42) | collective-permute-done | bytes 1048608 | tf_op jit(solution)/shard_map/ppermute | solution.py:45
  746.3 24.7 %collective-permute-done.43 = bf16[1024,512]{1,0:T(8,128)(2,1)S(1)} collective-permute-done((bf16[1024,512]{1,0:T(8,128)(2,1)S(1)}, bf16[1024,512]{1,0:T(8,128)(2,1)S(1)}, u32[]{:S(2)}, u32[]{:S(2)}) %collective-permute-start.43) | collective-permute-done | bytes 1048608 | tf_op jit(solution)/shard_map/ppermute | solution.py:49
  771.0 1.9 collective-permute-start.45
  773.5 18.8 %collective-permute-done.48 = bf16[1024,512]{1,0:T(8,128)(2,1)} collective-permute-done((bf16[1024,512]{1,0:T(8,128)(2,1)}, bf16[1024,512]{1,0:T(8,128)(2,1)}, u32[]{:S(2)}, u32[]{:S(2)}) %collective-permute-start.48) | collective-permute-done | bytes 1048608 | tf_op jit(solution)/shard_map/ppermute | solution.py:47
  792.3 2.4 constant_dynamic-update-slice_fusion.2
  798.5 2.3 constant_dynamic-update-slice_fusion
  800.8 2.5 select_dynamic-update-slice_fusion.5
  804.6 23.2 %convolution_convert_fusion = bf16[1024,1024]{1,0:T(8,128)(2,1)} fusion(bf16[1024,8192]{1,0:T(8,128)(2,1)} %select_dynamic-update-slice_fusion.4, bf16[8192,1024]{1,0:T(8,128)(2,1)} %all-gather.8.cloned.1.call-done), kind=kOutput, calls=%fused_computation.10 | convolution fusion | flops 17180917760 | bytes 35651584 | tf_op jit(solution)/shard_map/dot_general | solution.py:342
  (146 shorter events, 53.3 us)
Async XLA Ops:
  6.5 242.0 %all-gather.6.cloned.1.call-start = ((), (), s32[]{:S(2)}) async-start(), calls=%async_computation.1 | async-start | bytes 10485760 | tf_op jit(solution)/shard_map/all_gather | solution.py:294
  7.2 9.1 %collective-permute-start.1 = (s32[16,4]{0,1:T(4,128)S(1)}, s32[16,4]{0,1:T(4,128)S(1)}, u32[]{:S(2)}, u32[]{:S(2)}) collective-permute-start(s32[16,4]{0,1:T(4,128)S(1)} %get-tuple-element.78), channel_id=1, source_target_pairs={{0,8},{8,0},{16,24},{24,16},{1,9},{9,1},{17,25},{25,17},{2,10},{10... | collective-permute-start | bytes 776 | tf_op jit(solution)/shard_map/ppermute | solution.py:27
  10.2 6.1 collective-permute-start
  11.7 4.6 collective-permute-start.2
  32.5 236.9 %all-gather.4.cloned.1.call-start = ((), (), s32[]{:S(2)}) async-start(), calls=%async_computation | async-start | bytes 10485760 | tf_op jit(solution)/shard_map/all_gather | solution.py:294
  33.2 771.4 %all-gather.8.cloned.1.call-start = ((), (), s32[]{:S(2)}) async-start(), calls=%async_computation.2 | async-start | bytes 20971520 | tf_op jit(solution)/shard_map/all_gather | solution.py:321
  33.3 93.2 %collective-permute-start.4 = (bf16[1024,1024]{1,0:T(8,128)(2,1)}, bf16[1024,1024]{1,0:T(8,128)(2,1)}, u32[]{:S(2)}, u32[]{:S(2)}) collective-permute-start(bf16[1024,1024]{1,0:T(8,128)(2,1)} %param.6), channel_id=1, source_target_pairs={{0,4},{1,5},{2,6},{3,7},{4,0},{5,1},{6,2},{7,3},{8,12},{9,13},{10,... | collective-permute-start | bytes 6291464 | tf_op jit(solution)/shard_map/ppermute | solution.py:45
  36.4 92.7 %collective-permute-start.6 = (bf16[1024,1024]{1,0:T(8,128)(2,1)}, bf16[1024,1024]{1,0:T(8,128)(2,1)}, u32[]{:S(2)}, u32[]{:S(2)}) collective-permute-start(bf16[1024,1024]{1,0:T(8,128)(2,1)} %param.6), channel_id=1, source_target_pairs={{0,2},{1,3},{2,4},{3,5},{4,6},{5,7},{8,10},{9,11},{10,12},{11,13},... | collective-permute-start | bytes 6291464 | tf_op jit(solution)/shard_map/ppermute | solution.py:46
  126.4 50.6 %collective-permute-start.5 = (bf16[1024,1024]{1,0:T(8,128)(2,1)}, bf16[1024,1024]{1,0:T(8,128)(2,1)S(1)}, u32[]{:S(2)}, u32[]{:S(2)}) collective-permute-start(bf16[1024,1024]{1,0:T(8,128)(2,1)} %collective-permute-done.4), channel_id=1, source_target_pairs={{4,6},{5,7},{2,0},{3,1},{12,14},{13,15},{10,8},{11,9},{20,22},{21,... | collective-permute-start | bytes 6291464 | tf_op jit(solution)/shard_map/ppermute | solution.py:49
  127.7 92.3 %collective-permute-start.10 = (bf16[1024,1024]{1,0:T(8,128)(2,1)}, bf16[1024,1024]{1,0:T(8,128)(2,1)}, u32[]{:S(2)}, u32[]{:S(2)}) collective-permute-start(bf16[1024,1024]{1,0:T(8,128)(2,1)} %param.6), channel_id=1, source_target_pairs={{2,0},{3,1},{4,2},{5,3},{6,4},{7,5},{10,8},{11,9},{12,10},{13,11},... | collective-permute-start | bytes 6291464 | tf_op jit(solution)/shard_map/ppermute | solution.py:47
  129.0 94.6 %collective-permute-start.3 = (bf16[1024,1024]{1,0:T(8,128)(2,1)}, bf16[1024,1024]{1,0:T(8,128)(2,1)}, u32[]{:S(2)}, u32[]{:S(2)}) collective-permute-start(bf16[1024,1024]{1,0:T(8,128)(2,1)} %param.6), channel_id=1, source_target_pairs={{0,1},{1,0},{2,3},{3,2},{4,5},{5,4},{6,7},{7,6},{8,9},{9,8},{10,11... | collective-permute-start | bytes 6291464 | tf_op jit(solution)/shard_map/ppermute | solution.py:43
  129.1 97.6 %collective-permute-start.8 = (bf16[1024,1024]{1,0:T(8,128)(2,1)}, bf16[1024,1024]{1,0:T(8,128)(2,1)}, u32[]{:S(2)}, u32[]{:S(2)}) collective-permute-start(bf16[1024,1024]{1,0:T(8,128)(2,1)} %collective-permute-done.6), channel_id=1, source_target_pairs={{0,1},{1,0},{2,3},{3,2},{4,5},{5,4},{6,7},{7,6},{8,9},{9,8},{10,11... | collective-permute-start | bytes 6291464 | tf_op jit(solution)/shard_map/ppermute | solution.py:43
  177.0 49.7 %collective-permute-start.7 = (bf16[1024,1024]{1,0:T(8,128)(2,1)S(1)}, bf16[1024,1024]{1,0:T(8,128)(2,1)}, u32[]{:S(2)}, u32[]{:S(2)}) collective-permute-start(bf16[1024,1024]{1,0:T(8,128)(2,1)S(1)} %collective-permute-done.5), channel_id=1, source_target_pairs={{0,1},{1,0},{6,7},{7,6},{8,9},{9,8},{14,15},{15,14},{16,17},{17,16... | collective-permute-start | bytes 6291464 | tf_op jit(solution)/shard_map/ppermute | solution.py:51
  178.9 52.4 %collective-permute-start.9 = (bf16[1024,1024]{1,0:T(8,128)(2,1)}, bf16[1024,1024]{1,0:T(8,128)(2,1)}, u32[]{:S(2)}, u32[]{:S(2)}) collective-permute-start(bf16[1024,1024]{1,0:T(8,128)(2,1)} %collective-permute-done.4), channel_id=1, source_target_pairs={{0,1},{1,0},{2,3},{3,2},{4,5},{5,4},{6,7},{7,6},{8,9},{9,8},{10,11... | collective-permute-start | bytes 6291464 | tf_op jit(solution)/shard_map/ppermute | solution.py:43
  220.1 16.0 %collective-permute-start.11 = (bf16[1024,1024]{1,0:T(8,128)(2,1)}, bf16[1024,1024]{1,0:T(8,128)(2,1)}, u32[]{:S(2)}, u32[]{:S(2)}) collective-permute-start(bf16[1024,1024]{1,0:T(8,128)(2,1)} %collective-permute-done.10), channel_id=1, source_target_pairs={{0,1},{1,0},{2,3},{3,2},{4,5},{5,4},{6,7},{7,6},{8,9},{9,8},{10,11... | collective-permute-start | bytes 6291464 | tf_op jit(solution)/shard_map/ppermute | solution.py:43
  238.8 5.8 copy-start
  264.5 176.5 %collective-permute-start.14 = (bf16[24,128,256]{2,1,0:T(8,128)(2,1)}, bf16[24,128,256]{2,1,0:T(8,128)(2,1)S(1)}, u32[]{:S(2)}, u32[]{:S(2)}) collective-permute-start(bf16[24,128,256]{2,1,0:T(8,128)(2,1)} %get-tuple-element.31), channel_id=1, source_target_pairs={{0,8},{8,0},{16,24},{24,16},{1,9},{9,1},{17,25},{25,17},{2,10},{10... | collective-permute-start | bytes 4718600 | tf_op jit(solution)/shard_map/ppermute | solution.py:27
  266.9 174.1 %collective-permute-start.15 = (bf16[24,128,256]{2,1,0:T(8,128)(2,1)}, bf16[24,128,256]{2,1,0:T(8,128)(2,1)S(1)}, u32[]{:S(2)}, u32[]{:S(2)}) collective-permute-start(bf16[24,128,256]{2,1,0:T(8,128)(2,1)} %get-tuple-element.32), channel_id=1, source_target_pairs={{0,16},{8,24},{16,0},{24,8},{1,17},{9,25},{17,1},{25,9},{2,18},{10... | collective-permute-start | bytes 4718600 | tf_op jit(solution)/shard_map/ppermute | solution.py:27
  267.4 193.1 %collective-permute-start.16 = (bf16[24,128,256]{2,1,0:T(8,128)(2,1)}, bf16[24,128,256]{2,1,0:T(8,128)(2,1)}, u32[]{:S(2)}, u32[]{:S(2)}) collective-permute-start(bf16[24,128,256]{2,1,0:T(8,128)(2,1)} %get-tuple-element.33), channel_id=1, source_target_pairs={{0,8},{8,0},{16,24},{24,16},{1,9},{9,1},{17,25},{25,17},{2,10},{10... | collective-permute-start | bytes 4718600 | tf_op jit(solution)/shard_map/ppermute | solution.py:27
  269.3 191.1 %collective-permute-start.17 = (bf16[24,128,256]{2,1,0:T(8,128)(2,1)}, bf16[24,128,256]{2,1,0:T(8,128)(2,1)}, u32[]{:S(2)}, u32[]{:S(2)}) collective-permute-start(bf16[24,128,256]{2,1,0:T(8,128)(2,1)} %get-tuple-element.34), channel_id=1, source_target_pairs={{0,16},{8,24},{16,0},{24,8},{1,17},{9,25},{17,1},{25,9},{2,18},{10... | collective-permute-start | bytes 4718600 | tf_op jit(solution)/shard_map/ppermute | solution.py:27
  288.5 125.1 %collective-permute-start.12 = (bf16[1024,256]{1,0:T(8,128)(2,1)}, bf16[1024,256]{1,0:T(8,128)(2,1)}, u32[]{:S(2)}, u32[]{:S(2)}) collective-permute-start(bf16[1024,256]{1,0:T(8,128)(2,1)} %get-tuple-element.74), channel_id=1, source_target_pairs={{0,16},{8,24},{16,0},{24,8},{1,17},{9,25},{17,1},{25,9},{2,18},{10... | collective-permute-start | bytes 1572872 | tf_op jit(solution)/shard_map/ppermute | solution.py:27
  413.6 25.2 %collective-permute-start.13 = (bf16[1024,256]{1,0:T(8,128)(2,1)}, bf16[1024,256]{1,0:T(8,128)(2,1)S(1)}, u32[]{:S(2)}, u32[]{:S(2)}) collective-permute-start(bf16[1024,256]{1,0:T(8,128)(2,1)} %get-tuple-element.73), channel_id=1, source_target_pairs={{0,8},{8,0},{16,24},{24,16},{1,9},{9,1},{17,25},{25,17},{2,10},{10... | collective-permute-start | bytes 1572872 | tf_op jit(solution)/shard_map/ppermute | solution.py:27
  441.0 1.1 copy-start.1
  441.0 1.7 copy-start.2
  457.6 28.8 %copy-start.6 = (bf16[1024,512]{1,0:T(8,128)(2,1)S(1)}, bf16[1024,512]{1,0:T(8,128)(2,1)}, u32[]{:S(2)}) copy-start(bf16[1024,512]{1,0:T(8,128)(2,1)} %fusion.9) | copy-start | bytes 3145732
  457.6 6.1 collective-permute-start.18
  458.9 6.0 collective-permute-start.19
  463.6 1.3 copy-start.9
  464.9 0.6 copy-start.11
  484.0 39.7 %collective-permute-start.21 = (f32[1024,256]{1,0:T(8,128)}, f32[1024,256]{1,0:T(8,128)}, u32[]{:S(2)}, u32[]{:S(2)}) collective-permute-start(f32[1024,256]{1,0:T(8,128)} %get-tuple-element.40), channel_id=1, source_target_pairs={{0,8},{8,0},{16,24},{24,16},{1,9},{9,1},{17,25},{25,17},{2,10},{10... | collective-permute-start | bytes 3145736 | tf_op jit(solution)/shard_map/ppermute | solution.py:27
  485.7 41.1 %collective-permute-start.20 = (f32[1024,256]{1,0:T(8,128)}, f32[1024,256]{1,0:T(8,128)}, u32[]{:S(2)}, u32[]{:S(2)}) collective-permute-start(f32[1024,256]{1,0:T(8,128)} %get-tuple-element.38), channel_id=1, source_target_pairs={{0,16},{8,24},{16,0},{24,8},{1,17},{9,25},{17,1},{25,9},{2,18},{10... | collective-permute-start | bytes 3145736 | tf_op jit(solution)/shard_map/ppermute | solution.py:27
  487.3 35.9 %collective-permute-start.31 = (bf16[1024,256]{1,0:T(8,128)(2,1)}, bf16[1024,256]{1,0:T(8,128)(2,1)}, u32[]{:S(2)}, u32[]{:S(2)}) collective-permute-start(bf16[1024,256]{1,0:T(8,128)(2,1)} %get-tuple-element.70), channel_id=1, source_target_pairs={{0,16},{8,24},{16,0},{24,8},{1,17},{9,25},{17,1},{25,9},{2,18},{10... | collective-permute-start | bytes 1572872 | tf_op jit(solution)/shard_map/ppermute | solution.py:27
  503.1 82.0 %copy-start.5 = (bf16[1024,256]{1,0:T(8,128)(2,1)S(1)}, bf16[1024,256]{1,0:T(8,128)(2,1)}, u32[]{:S(2)}) copy-start(bf16[1024,256]{1,0:T(8,128)(2,1)} %get-tuple-element.69) | copy-start | bytes 1572868
  503.1 83.0 %collective-permute-start.33 = (bf16[24,128,256]{2,1,0:T(8,128)(2,1)}, bf16[24,128,256]{2,1,0:T(8,128)(2,1)S(1)}, u32[]{:S(2)}, u32[]{:S(2)}) collective-permute-start(bf16[24,128,256]{2,1,0:T(8,128)(2,1)} %get-tuple-element.44), channel_id=1, source_target_pairs={{0,8},{8,0},{16,24},{24,16},{1,9},{9,1},{17,25},{25,17},{2,10},{10... | collective-permute-start | bytes 4718600 | tf_op jit(solution)/shard_map/ppermute | solution.py:27
  504.3 81.8 %collective-permute-start.34 = (bf16[24,128,256]{2,1,0:T(8,128)(2,1)}, bf16[24,128,256]{2,1,0:T(8,128)(2,1)S(1)}, u32[]{:S(2)}, u32[]{:S(2)}) collective-permute-start(bf16[24,128,256]{2,1,0:T(8,128)(2,1)} %get-tuple-element.45), channel_id=1, source_target_pairs={{0,16},{8,24},{16,0},{24,8},{1,17},{9,25},{17,1},{25,9},{2,18},{10... | collective-permute-start | bytes 4718600 | tf_op jit(solution)/shard_map/ppermute | solution.py:27
  523.3 81.8 %collective-permute-start.35 = (bf16[24,128,256]{2,1,0:T(8,128)(2,1)}, bf16[24,128,256]{2,1,0:T(8,128)(2,1)}, u32[]{:S(2)}, u32[]{:S(2)}) collective-permute-start(bf16[24,128,256]{2,1,0:T(8,128)(2,1)} %get-tuple-element.48), channel_id=1, source_target_pairs={{0,8},{8,0},{16,24},{24,16},{1,9},{9,1},{17,25},{25,17},{2,10},{10... | collective-permute-start | bytes 4718600 | tf_op jit(solution)/shard_map/ppermute | solution.py:27
  523.7 81.4 %collective-permute-start.36 = (bf16[24,128,256]{2,1,0:T(8,128)(2,1)}, bf16[24,128,256]{2,1,0:T(8,128)(2,1)}, u32[]{:S(2)}, u32[]{:S(2)}) collective-permute-start(bf16[24,128,256]{2,1,0:T(8,128)(2,1)} %get-tuple-element.49), channel_id=1, source_target_pairs={{0,16},{8,24},{16,0},{24,8},{1,17},{9,25},{17,1},{25,9},{2,18},{10... | collective-permute-start | bytes 4718600 | tf_op jit(solution)/shard_map/ppermute | solution.py:27
  526.8 58.3 %collective-permute-start.32 = (bf16[1024,256]{1,0:T(8,128)(2,1)}, bf16[1024,256]{1,0:T(8,128)(2,1)S(1)}, u32[]{:S(2)}, u32[]{:S(2)}) collective-permute-start(bf16[1024,256]{1,0:T(8,128)(2,1)} %get-tuple-element.69), channel_id=1, source_target_pairs={{0,8},{8,0},{16,24},{24,16},{1,9},{9,1},{17,25},{25,17},{2,10},{10... | collective-permute-start | bytes 1572872 | tf_op jit(solution)/shard_map/ppermute | solution.py:27
  585.1 47.7 %collective-permute-start.23 = (bf16[1024,512]{1,0:T(8,128)(2,1)}, bf16[1024,512]{1,0:T(8,128)(2,1)}, u32[]{:S(2)}, u32[]{:S(2)}) collective-permute-start(bf16[1024,512]{1,0:T(8,128)(2,1)} %get-tuple-element.71), channel_id=1, source_target_pairs={{0,4},{1,5},{2,6},{3,7},{4,0},{5,1},{6,2},{7,3},{8,12},{9,13},{10,... | collective-permute-start | bytes 3145736 | tf_op jit(solution)/shard_map/ppermute | solution.py:45
  586.1 1.1 copy-start.3
  587.2 1.1 copy-start.4
  603.3 4.5 collective-permute-start.37
  604.8 4.5 collective-permute-start.38
  607.7 1.5 copy-start.8
  628.3 21.0 %collective-permute-start.40 = (f32[1024,256]{1,0:T(8,128)}, f32[1024,256]{1,0:T(8,128)S(1)}, u32[]{:S(2)}, u32[]{:S(2)}) collective-permute-start(f32[1024,256]{1,0:T(8,128)} %get-tuple-element.55), channel_id=1, source_target_pairs={{0,8},{8,0},{16,24},{24,16},{1,9},{9,1},{17,25},{25,17},{2,10},{10... | collective-permute-start | bytes 3145736 | tf_op jit(solution)/shard_map/ppermute | solution.py:27
  628.7 22.1 %collective-permute-start.25 = (bf16[1024,512]{1,0:T(8,128)(2,1)}, bf16[1024,512]{1,0:T(8,128)(2,1)}, u32[]{:S(2)}, u32[]{:S(2)}) collective-permute-start(bf16[1024,512]{1,0:T(8,128)(2,1)} %get-tuple-element.71), channel_id=1, source_target_pairs={{0,2},{1,3},{2,4},{3,5},{4,6},{5,7},{8,10},{9,11},{10,12},{11,13},... | collective-permute-start | bytes 3145736 | tf_op jit(solution)/shard_map/ppermute | solution.py:46
  632.7 28.1 %collective-permute-start.24 = (bf16[1024,512]{1,0:T(8,128)(2,1)}, bf16[1024,512]{1,0:T(8,128)(2,1)S(1)}, u32[]{:S(2)}, u32[]{:S(2)}) collective-permute-start(bf16[1024,512]{1,0:T(8,128)(2,1)} %collective-permute-done.23), channel_id=1, source_target_pairs={{4,6},{5,7},{2,0},{3,1},{12,14},{13,15},{10,8},{11,9},{20,22},{21,... | collective-permute-start | bytes 3145736 | tf_op jit(solution)/shard_map/ppermute | solution.py:49
  634.0 30.6 %collective-permute-start.22 = (bf16[1024,512]{1,0:T(8,128)(2,1)}, bf16[1024,512]{1,0:T(8,128)(2,1)S(1)}, u32[]{:S(2)}, u32[]{:S(2)}) collective-permute-start(bf16[1024,512]{1,0:T(8,128)(2,1)} %get-tuple-element.71), channel_id=1, source_target_pairs={{0,1},{1,0},{2,3},{3,2},{4,5},{5,4},{6,7},{7,6},{8,9},{9,8},{10,11... | collective-permute-start | bytes 3145736 | tf_op jit(solution)/shard_map/ppermute | solution.py:43
  634.1 45.6 %collective-permute-start.29 = (bf16[1024,512]{1,0:T(8,128)(2,1)}, bf16[1024,512]{1,0:T(8,128)(2,1)}, u32[]{:S(2)}, u32[]{:S(2)}) collective-permute-start(bf16[1024,512]{1,0:T(8,128)(2,1)} %get-tuple-element.71), channel_id=1, source_target_pairs={{2,0},{3,1},{4,2},{5,3},{6,4},{7,5},{10,8},{11,9},{12,10},{13,11},... | collective-permute-start | bytes 3145736 | tf_op jit(solution)/shard_map/ppermute | solution.py:47
  649.3 1.5 copy-start.7
  649.3 31.5 %collective-permute-start.39 = (f32[1024,256]{1,0:T(8,128)}, f32[1024,256]{1,0:T(8,128)}, u32[]{:S(2)}, u32[]{:S(2)}) collective-permute-start(f32[1024,256]{1,0:T(8,128)} %get-tuple-element.53), channel_id=1, source_target_pairs={{0,16},{8,24},{16,0},{24,8},{1,17},{9,25},{17,1},{25,9},{2,18},{10... | collective-permute-start | bytes 3145736 | tf_op jit(solution)/shard_map/ppermute | solution.py:27
  650.8 33.0 %collective-permute-start.27 = (bf16[1024,512]{1,0:T(8,128)(2,1)}, bf16[1024,512]{1,0:T(8,128)(2,1)}, u32[]{:S(2)}, u32[]{:S(2)}) collective-permute-start(bf16[1024,512]{1,0:T(8,128)(2,1)} %collective-permute-done.25), channel_id=1, source_target_pairs={{0,1},{1,0},{2,3},{3,2},{4,5},{5,4},{6,7},{7,6},{8,9},{9,8},{10,11... | collective-permute-start | bytes 3145736 | tf_op jit(solution)/shard_map/ppermute | solution.py:43
  660.9 23.0 %collective-permute-start.26 = (bf16[1024,512]{1,0:T(8,128)(2,1)S(1)}, bf16[1024,512]{1,0:T(8,128)(2,1)S(1)}, u32[]{:S(2)}, u32[]{:S(2)}) collective-permute-start(bf16[1024,512]{1,0:T(8,128)(2,1)S(1)} %collective-permute-done.24), channel_id=1, source_target_pairs={{0,1},{1,0},{6,7},{7,6},{8,9},{9,8},{14,15},{15,14},{16,17},{17,16... | collective-permute-start | bytes 3145736 | tf_op jit(solution)/shard_map/ppermute | solution.py:51
  664.7 22.9 %collective-permute-start.28 = (bf16[1024,512]{1,0:T(8,128)(2,1)}, bf16[1024,512]{1,0:T(8,128)(2,1)S(1)}, u32[]{:S(2)}, u32[]{:S(2)}) collective-permute-start(bf16[1024,512]{1,0:T(8,128)(2,1)} %collective-permute-done.23), channel_id=1, source_target_pairs={{0,1},{1,0},{2,3},{3,2},{4,5},{5,4},{6,7},{7,6},{8,9},{9,8},{10,11... | collective-permute-start | bytes 3145736 | tf_op jit(solution)/shard_map/ppermute | solution.py:43
  679.7 11.4 %collective-permute-start.30 = (bf16[1024,512]{1,0:T(8,128)(2,1)}, bf16[1024,512]{1,0:T(8,128)(2,1)S(1)}, u32[]{:S(2)}, u32[]{:S(2)}) collective-permute-start(bf16[1024,512]{1,0:T(8,128)(2,1)} %collective-permute-done.29), channel_id=1, source_target_pairs={{0,1},{1,0},{2,3},{3,2},{4,5},{5,4},{6,7},{7,6},{8,9},{9,8},{10,11... | collective-permute-start | bytes 3145736 | tf_op jit(solution)/shard_map/ppermute | solution.py:43
  693.9 49.2 %collective-permute-start.42 = (bf16[1024,512]{1,0:T(8,128)(2,1)}, bf16[1024,512]{1,0:T(8,128)(2,1)S(1)}, u32[]{:S(2)}, u32[]{:S(2)}) collective-permute-start(bf16[1024,512]{1,0:T(8,128)(2,1)} %get-tuple-element.67), channel_id=1, source_target_pairs={{0,4},{1,5},{2,6},{3,7},{4,0},{5,1},{6,2},{7,3},{8,12},{9,13},{10,... | collective-permute-start | bytes 3145736 | tf_op jit(solution)/shard_map/ppermute | solution.py:45
  695.3 50.4 %collective-permute-start.44 = (bf16[1024,512]{1,0:T(8,128)(2,1)}, bf16[1024,512]{1,0:T(8,128)(2,1)}, u32[]{:S(2)}, u32[]{:S(2)}) collective-permute-start(bf16[1024,512]{1,0:T(8,128)(2,1)} %get-tuple-element.67), channel_id=1, source_target_pairs={{0,2},{1,3},{2,4},{3,5},{4,6},{5,7},{8,10},{9,11},{10,12},{11,13},... | collective-permute-start | bytes 3145736 | tf_op jit(solution)/shard_map/ppermute | solution.py:46
  743.1 27.9 %collective-permute-start.43 = (bf16[1024,512]{1,0:T(8,128)(2,1)S(1)}, bf16[1024,512]{1,0:T(8,128)(2,1)S(1)}, u32[]{:S(2)}, u32[]{:S(2)}) collective-permute-start(bf16[1024,512]{1,0:T(8,128)(2,1)S(1)} %collective-permute-done.42), channel_id=1, source_target_pairs={{4,6},{5,7},{2,0},{3,1},{12,14},{13,15},{10,8},{11,9},{20,22},{21,... | collective-permute-start | bytes 3145736 | tf_op jit(solution)/shard_map/ppermute | solution.py:49
  744.4 47.9 %collective-permute-start.48 = (bf16[1024,512]{1,0:T(8,128)(2,1)}, bf16[1024,512]{1,0:T(8,128)(2,1)}, u32[]{:S(2)}, u32[]{:S(2)}) collective-permute-start(bf16[1024,512]{1,0:T(8,128)(2,1)} %get-tuple-element.67), channel_id=1, source_target_pairs={{2,0},{3,1},{4,2},{5,3},{6,4},{7,5},{10,8},{11,9},{12,10},{13,11},... | collective-permute-start | bytes 3145736 | tf_op jit(solution)/shard_map/ppermute | solution.py:47
  745.7 46.6 %collective-permute-start.41 = (bf16[1024,512]{1,0:T(8,128)(2,1)}, bf16[1024,512]{1,0:T(8,128)(2,1)}, u32[]{:S(2)}, u32[]{:S(2)}) collective-permute-start(bf16[1024,512]{1,0:T(8,128)(2,1)} %get-tuple-element.67), channel_id=1, source_target_pairs={{0,1},{1,0},{2,3},{3,2},{4,5},{5,4},{6,7},{7,6},{8,9},{9,8},{10,11... | collective-permute-start | bytes 3145736 | tf_op jit(solution)/shard_map/ppermute | solution.py:43
  745.8 50.3 %collective-permute-start.46 = (bf16[1024,512]{1,0:T(8,128)(2,1)}, bf16[1024,512]{1,0:T(8,128)(2,1)}, u32[]{:S(2)}, u32[]{:S(2)}) collective-permute-start(bf16[1024,512]{1,0:T(8,128)(2,1)} %collective-permute-done.44), channel_id=1, source_target_pairs={{0,1},{1,0},{2,3},{3,2},{4,5},{5,4},{6,7},{7,6},{8,9},{9,8},{10,11... | collective-permute-start | bytes 3145736 | tf_op jit(solution)/shard_map/ppermute | solution.py:43
  771.0 25.0 %collective-permute-start.45 = (bf16[1024,512]{1,0:T(8,128)(2,1)S(1)}, bf16[1024,512]{1,0:T(8,128)(2,1)S(1)}, u32[]{:S(2)}, u32[]{:S(2)}) collective-permute-start(bf16[1024,512]{1,0:T(8,128)(2,1)S(1)} %collective-permute-done.43), channel_id=1, source_target_pairs={{0,1},{1,0},{6,7},{7,6},{8,9},{9,8},{14,15},{15,14},{16,17},{17,16... | collective-permute-start | bytes 3145736 | tf_op jit(solution)/shard_map/ppermute | solution.py:51
  772.9 25.5 %collective-permute-start.47 = (bf16[1024,512]{1,0:T(8,128)(2,1)S(1)}, bf16[1024,512]{1,0:T(8,128)(2,1)}, u32[]{:S(2)}, u32[]{:S(2)}) collective-permute-start(bf16[1024,512]{1,0:T(8,128)(2,1)S(1)} %collective-permute-done.42), channel_id=1, source_target_pairs={{0,1},{1,0},{2,3},{3,2},{4,5},{5,4},{6,7},{7,6},{8,9},{9,8},{10,11... | collective-permute-start | bytes 3145736 | tf_op jit(solution)/shard_map/ppermute | solution.py:43
  792.3 11.0 %collective-permute-start.49 = (bf16[1024,512]{1,0:T(8,128)(2,1)}, bf16[1024,512]{1,0:T(8,128)(2,1)S(1)}, u32[]{:S(2)}, u32[]{:S(2)}) collective-permute-start(bf16[1024,512]{1,0:T(8,128)(2,1)} %collective-permute-done.48), channel_id=1, source_target_pairs={{0,1},{1,0},{2,3},{3,2},{4,5},{5,4},{6,7},{7,6},{8,9},{9,8},{10,11... | collective-permute-start | bytes 3145736 | tf_op jit(solution)/shard_map/ppermute | solution.py:43
  (1 other events, 0.6 us)
Sparse Core Ops, SparseCore 0:
  32.6 89.4 all-gather.5
  123.9 87.4 all-gather.3
  264.6 220.6 all-gather.7

commit v5 on v4

--- a/solution.py
+++ b/solution.py
@@ -203,7 +203,7 @@
     slots = received[0].shape[0]
     per_step = 8 if spans % 8 == 0 else spans
     steps = spans // per_step
-    together = 2 if per_step % 2 == 0 else 1
+    together = 2 if per_step % 2 == 0 and not stats else 1
     step_rows = per_step * span
 
     in_specs = [pl.BlockSpec((step_rows, part), lambda c, i, *t: (c * steps + i, 0))] * AXES
@@ -277,7 +277,7 @@
     members = lax.axis_size("fsdp")
     passes = 2 if local_width % (2 * AXES * HEAD_DIM) == 0 else 1
     part = local_width // (passes * AXES)
-    share = AXES * part
+    share = local_width // passes
     span_count = neighbor_shard.shape[0]
     capacity = max(2, 3 * span_count * NEIGH // (2 * peers))
 
@@ -317,15 +317,17 @@
         ])
         if step > 0:
             received.append([send_blocks(step, 0, own_queries[0]), send_blocks(step, 1, queries)])
-    w_output = after(w_output, own_queries[-1])
-    w_output_columns = lax.all_gather(w_output, "dp", axis=0, tiled=True)
-
-    attended = jnp.zeros((row_count, members * local_width), jnp.bfloat16)
+
+    attended = gathered
+    if width != local_width:
+        attended = jnp.zeros((row_count, members * local_width), jnp.bfloat16)
     for step in range(passes):
         common = dict(step=step, part=part, spans=span_count)
         mine = span_call(
             stats_kernel, places, asked[step], stored, received[step][0], [], planes=1, **common
         )
+        if step == passes - 1:
+            output_columns = lax.all_gather(after(w_output, mine), "dp", axis=0, tiled=True)
         theirs = [over_dp(mine[axis], 3 ^ (1 << axis)) for axis in range(AXES)]
         partial = span_call(
             mix_kernel, places, asked[step], stored, received[step][0] + received[step][1], list(mine) + theirs,
@@ -339,7 +341,7 @@
         for owner, piece in pieces:
             start = owner * local_width + step * share
             attended = lax.dynamic_update_slice(attended, piece, (0, start))
-    summed = jnp.dot(attended, w_output_columns, preferred_element_type=jnp.float32)
+    summed = jnp.dot(attended, output_columns, preferred_element_type=jnp.float32)
     return summed.astype(jnp.bfloat16)
 
 

time: 836 us -> 857 us (1.025)
  the two profiles are of different devices: /device:TPU:0 before, /device:TPU:11 now
where the time goes in v5:
time: 857 us; the launch traced here: 855 us
  waiting for transfers between devices  493 us (58%)
  Pallas kernels  106 us (12%)
  starting transfers between devices  89.9 us (10%)
  other arithmetic  57.2 us (7%)
  matrix products  54.1 us (6%)
  local copies, waits for them, and re-layouts  41.5 us (5%)
  between operations  13.4 us (2%)
    ppermute x23, waiting for transfers between devices, over_dp(): lax.ppermute(value, 'dp', [(i, i ^ bit) for i in range(lax.axis_size('dp'...  247 us
    ppermute x3, waiting for transfers between devices, pieces_over_fsdp(): lax.ppermute(piece, 'fsdp', chip_pairs([(0, 2), (1, 3), (2, 0), (3, 1)]))  131 us
    pallas_call x4, Pallas kernels, span_call(): pl.pallas_call(functools.partial(kernel, spans, span, together), grid_spe...  75 us
    ppermute x3, waiting for transfers between devices, pieces_over_fsdp(): back3 = lax.ppermute(piece, 'fsdp', chip_pairs([(1, 0), (2, 1), (3, 2)]))  56.2 us
    ppermute x3, waiting for transfers between devices, pieces_over_fsdp(): back1 = lax.ppermute(piece, 'fsdp', chip_pairs([(0, 1), (1, 2), (2, 3)]))  54.6 us
    ppermute x12, starting transfers between devices, swap(): return lax.ppermute(value, 'fsdp', [(i, i ^ 1) for i in range(members)])  40.7 us
    dot_general x2, matrix products, work(): jnp.dot(normed, columns[step], preferred_element_type=jnp.float32)  30.9 us
    pallas_call x2, Pallas kernels, pick_blocks(): pl.pallas_call(pick_kernel, grid_spec=pltpu.PrefetchScalarGridSpec(num_sc...  30.9 us
  transfers between devices with their start and end apart: 53, of which 22 were waited for; matrix products, arithmetic and copies ran while one was open for 14% of the time, Pallas kernels for 11%

profile of v5, /device:TPU:11, one launch (start us, length us, event | category | flops | bytes accessed | tf_op | source)
XLA Modules:
  0.0 854.8 jit_solution(13034463815689464918)
XLA Ops:
  6.5 4.5 fusion.21
  18.5 15.6 %pick.2 = (bf16[24,128,256]{2,1,0:T(8,128)(2,1)}, bf16[24,128,256]{2,1,0:T(8,128)(2,1)}, bf16[24,128,256]{2,1,0:T(8,128)(2,1)}, bf16[24,128,256]{2,1,0:T(8,128)(2,1)}) custom-call(s32[24]{0:T(128)} %get-tuple-element.80.first_ref, s32[24]{0:T(128)} %get-tuple-element.79.second_ref, bf16[32,2,128,1024]{3,2,1,0:T(8,128)(2,1)} %bitcast.28, ...), custom_call_target="tpu_custom_call" | custom-call | bytes 12582912 | tf_op jit(solution)/shard_map/pick/pallas_call | solution.py:74
  34.2 2.4 collective-permute-start.1
  38.5 88.6 %collective-permute-done.1 = bf16[1024,1024]{1,0:T(8,128)(2,1)} collective-permute-done((bf16[1024,1024]{1,0:T(8,128)(2,1)}, bf16[1024,1024]{1,0:T(8,128)(2,1)}, u32[]{:S(2)}, u32[]{:S(2)}) %collective-permute-start.1) | collective-permute-done | bytes 2097184 | tf_op jit(solution)/shard_map/ppermute | solution.py:45
  127.1 2.0 collective-permute-start.2
  132.9 39.1 %collective-permute-done.3 = bf16[1024,1024]{1,0:T(8,128)(2,1)} collective-permute-done((bf16[1024,1024]{1,0:T(8,128)(2,1)}, bf16[1024,1024]{1,0:T(8,128)(2,1)}, u32[]{:S(2)}, u32[]{:S(2)}) %collective-permute-start.3) | collective-permute-done | bytes 2097184 | tf_op jit(solution)/shard_map/ppermute | solution.py:46
  172.8 2.0 collective-permute-start.4
  174.7 4.3 collective-permute-start.6
  179.1 6.0 broadcast_in_dim.36
  185.0 3.1 constant_dynamic-update-slice_fusion.11
  188.2 29.6 %collective-permute-done.7 = bf16[1024,1024]{1,0:T(8,128)(2,1)} collective-permute-done((bf16[1024,1024]{1,0:T(8,128)(2,1)}, bf16[1024,1024]{1,0:T(8,128)(2,1)}, u32[]{:S(2)}, u32[]{:S(2)}) %collective-permute-start.7) | collective-permute-done | bytes 2097184 | tf_op jit(solution)/shard_map/ppermute | solution.py:47
  217.7 2.4 collective-permute-start.8
  220.1 15.3 %pick.3 = (bf16[24,128,256]{2,1,0:T(8,128)(2,1)}, bf16[24,128,256]{2,1,0:T(8,128)(2,1)}, bf16[24,128,256]{2,1,0:T(8,128)(2,1)}, bf16[24,128,256]{2,1,0:T(8,128)(2,1)}) custom-call(s32[24]{0:T(128)} %get-tuple-element.80.first_ref, s32[24]{0:T(128)} %get-tuple-element.79.second_ref, bf16[32,2,128,1024]{3,2,1,0:T(8,128)(2,1)} %bitcast.30, ...), custom_call_target="tpu_custom_call" | custom-call | bytes 12582912 | tf_op jit(solution)/shard_map/pick/pallas_call | solution.py:74
  236.0 3.1 constant_dynamic-update-slice_fusion.10
  239.0 3.9 select_dynamic-update-slice_fusion.3
  242.9 3.9 select_dynamic-update-slice_fusion.2
  246.8 3.1 constant_dynamic-update-slice_fusion.9
  249.9 3.2 constant_dynamic-update-slice_fusion.8
  253.0 3.9 select_dynamic-update-slice_fusion.1
  257.0 3.9 select_dynamic-update-slice_fusion
  260.9 7.2 fusion
  268.1 15.9 %fusion.6 = bf16[1024,512]{1,0:T(8,128)(2,1)} fusion(bf16[8192,512]{1,0:T(8,128)(2,1)} %all-gather.4.cloned.1.call-done, bf16[1024,8192]{1,0:T(8,128)(2,1)} %select_dynamic-update-slice_fusion, f32[1024]{0:T(1024)S(1)} %add_rsqrt_fusion), kind=kOutput, calls=%fused_computation.11 | convolution fusion | flops 8615624704 | bytes 26218496 | tf_op jit(solution)/shard_map/dot_general | solution.py:312
  284.0 2.3 collective-permute-start.34
  286.3 15.0 %fusion.9 = bf16[1024,512]{1,0:T(8,128)(2,1)S(1)} fusion(bf16[8192,512]{1,0:T(8,128)(2,1)} %all-gather.6.cloned.1.call-done, bf16[1024,8192]{1,0:T(8,128)(2,1)} %select_dynamic-update-slice_fusion, f32[1024]{0:T(1024)S(1)} %add_rsqrt_fusion), kind=kOutput, calls=%fused_computation.12 | convolution fusion | flops 8615624704 | bytes 26218496 | tf_op jit(solution)/shard_map/dot_general | solution.py:312
  303.5 27.8 %collective-permute-done.32 = bf16[1024,256]{1,0:T(8,128)(2,1)S(1)} collective-permute-done((bf16[1024,256]{1,0:T(8,128)(2,1)S(1)}, bf16[1024,256]{1,0:T(8,128)(2,1)S(1)}, u32[]{:S(2)}, u32[]{:S(2)}) %collective-permute-start.32) | collective-permute-done | bytes 524320 | tf_op jit(solution)/shard_map/ppermute | solution.py:27
  335.2 14.9 %stats.3 = (f32[2,64,128]{2,1,0:T(8,128)}, f32[2,64,128]{2,1,0:T(8,128)}) custom-call(s32[32]{0:T(128)} %get-tuple-element.82.refs_0_, s32[32]{0:T(128)} %get-tuple-element.83.refs_1_, s32[32]{0:T(128)} %get-tuple-element.81.refs_2_, s32[32]{0:T(128)} %pad_add_fusion.5.refs_3_, bf16[2048,256]{1,0:T(8,128)(2,1)} %pad_maximum_fusion.3.refs_4_, ...), custom_call_target="tpu_custom_call" | custom-call | flops 1073741824 | bytes 7340032 | tf_op jit(solution)/shard_map/stats/pallas_call | solution.py:221
  350.4 2.0 collective-permute-start.15
  355.3 136.0 %collective-permute-done.13 = bf16[1024,256]{1,0:T(8,128)(2,1)S(1)} collective-permute-done((bf16[1024,256]{1,0:T(8,128)(2,1)S(1)}, bf16[1024,256]{1,0:T(8,128)(2,1)S(1)}, u32[]{:S(2)}, u32[]{:S(2)}) %collective-permute-start.13) | collective-permute-done | bytes 524320 | tf_op jit(solution)/shard_map/ppermute | solution.py:27
  493.1 22.0 %collective-permute-done.12 = bf16[1024,256]{1,0:T(8,128)(2,1)S(1)} collective-permute-done((bf16[1024,256]{1,0:T(8,128)(2,1)S(1)}, bf16[1024,256]{1,0:T(8,128)(2,1)S(1)}, u32[]{:S(2)}, u32[]{:S(2)}) %collective-permute-start.12) | collective-permute-done | bytes 524320 | tf_op jit(solution)/shard_map/ppermute | solution.py:27
  518.5 14.9 %stats.2 = (f32[2,64,128]{2,1,0:T(8,128)}, f32[2,64,128]{2,1,0:T(8,128)}) custom-call(s32[32]{0:T(128)} %get-tuple-element.82.refs_0_, s32[32]{0:T(128)} %get-tuple-element.83.refs_1_, s32[32]{0:T(128)} %get-tuple-element.81.refs_2_, s32[32]{0:T(128)} %pad_add_fusion.5.refs_3_, bf16[2048,256]{1,0:T(8,128)(2,1)} %pad_maximum_fusion.refs_4_, ...), custom_call_target="tpu_custom_call" | custom-call | flops 1073741824 | bytes 7340032 | tf_op jit(solution)/shard_map/stats/pallas_call | solution.py:221
  535.5 3.1 collective-permute-done.18.refs_13_
  539.9 22.5 %mix.2 = (f32[1024,256]{1,0:T(8,128)}, f32[1024,256]{1,0:T(8,128)}, f32[1024,256]{1,0:T(8,128)}, f32[1024,256]{1,0:T(8,128)}) custom-call(s32[32]{0:T(128)} %get-tuple-element.82.refs_0_, s32[32]{0:T(128)} %get-tuple-element.83.refs_1_, s32[32]{0:T(128)} %get-tuple-element.81.refs_2_, s32[32]{0:T(128)} %pad_add_fusion.5.refs_3_, ...), custom_call_target="tpu_custom_call" | custom-call | flops 2147483648 | bytes 14680064 | tf_op jit(solution)/shard_map/mix/pallas_call | solution.py:221
  565.5 22.7 %collective-permute-done.20 = f32[1024,256]{1,0:T(8,128)S(1)} collective-permute-done((f32[1024,256]{1,0:T(8,128)}, f32[1024,256]{1,0:T(8,128)S(1)}, u32[]{:S(2)}, u32[]{:S(2)}) %collective-permute-start.20) | collective-permute-done | bytes 1048608 | tf_op jit(solution)/shard_map/ppermute | solution.py:27
  592.3 3.3 collective-permute-start.25
  595.7 2.2 collective-permute-start.37
  597.8 21.2 %collective-permute-done.35.refs_9_ = bf16[24,128,256]{2,1,0:T(8,128)(2,1)S(1)} collective-permute-done((bf16[24,128,256]{2,1,0:T(8,128)(2,1)}, bf16[24,128,256]{2,1,0:T(8,128)(2,1)S(1)}, u32[]{:S(2)}, u32[]{:S(2)}) %collective-permute-start.35) | collective-permute-done | bytes 1572896 | tf_op jit(solution)/shard_map/ppermute | solution.py:27
  619.0 2.8 collective-permute-done.36.refs_10_
  624.4 22.7 %mix.3 = (f32[1024,256]{1,0:T(8,128)}, f32[1024,256]{1,0:T(8,128)}, f32[1024,256]{1,0:T(8,128)}, f32[1024,256]{1,0:T(8,128)}) custom-call(s32[32]{0:T(128)} %get-tuple-element.82.refs_0_, s32[32]{0:T(128)} %get-tuple-element.83.refs_1_, s32[32]{0:T(128)} %get-tuple-element.81.refs_2_, s32[32]{0:T(128)} %pad_add_fusion.5.refs_3_, ...), custom_call_target="tpu_custom_call" | custom-call | flops 2147483648 | bytes 14680064 | tf_op jit(solution)/shard_map/mix/pallas_call | solution.py:221
  647.1 2.4 collective-permute-start.39
  649.5 2.3 collective-permute-start.24
  651.8 5.7 collective-permute-start.22
  660.6 7.5 collective-permute-done.39
  668.1 5.7 collective-permute-start.27
  676.2 7.4 collective-permute-start.28
  683.6 8.0 collective-permute-done.29
  691.6 6.2 collective-permute-start.30
  700.5 2.5 select_dynamic-update-slice_fusion.11
  703.0 2.5 select_dynamic-update-slice_fusion.10
  705.6 2.3 constant_dynamic-update-slice_fusion.5
  709.0 2.6 select_dynamic-update-slice_fusion.9
  714.4 2.8 collective-permute-start.44
  717.3 42.4 %collective-permute-done.42 = bf16[1024,512]{1,0:T(8,128)(2,1)S(1)} collective-permute-done((bf16[1024,512]{1,0:T(8,128)(2,1)}, bf16[1024,512]{1,0:T(8,128)(2,1)S(1)}, u32[]{:S(2)}, u32[]{:S(2)}) %collective-permute-start.42) | collective-permute-done | bytes 1048608 | tf_op jit(solution)/shard_map/ppermute | solution.py:45
  759.7 4.7 collective-permute-start.43
  764.4 2.1 collective-permute-start.48
  767.8 14.4 %collective-permute-done.44 = bf16[1024,512]{1,0:T(8,128)(2,1)} collective-permute-done((bf16[1024,512]{1,0:T(8,128)(2,1)}, bf16[1024,512]{1,0:T(8,128)(2,1)}, u32[]{:S(2)}, u32[]{:S(2)}) %collective-permute-start.44) | collective-permute-done | bytes 1048608 | tf_op jit(solution)/shard_map/ppermute | solution.py:46
  782.6 3.3 collective-permute-done.43
  786.6 3.2 collective-permute-start.47
  789.9 18.6 %collective-permute-done.48 = bf16[1024,512]{1,0:T(8,128)(2,1)} collective-permute-done((bf16[1024,512]{1,0:T(8,128)(2,1)}, bf16[1024,512]{1,0:T(8,128)(2,1)}, u32[]{:S(2)}, u32[]{:S(2)}) %collective-permute-start.48) | collective-permute-done | bytes 1048608 | tf_op jit(solution)/shard_map/ppermute | solution.py:47
  810.3 2.3 constant_dynamic-update-slice_fusion.2
  812.6 2.5 select_dynamic-update-slice_fusion.7
  815.1 2.6 select_dynamic-update-slice_fusion.6
  818.7 2.4 constant_dynamic-update-slice_fusion
  821.1 2.6 select_dynamic-update-slice_fusion.5
  825.0 23.2 %convolution_convert_fusion = bf16[1024,1024]{1,0:T(8,128)(2,1)} fusion(bf16[1024,8192]{1,0:T(8,128)(2,1)} %select_dynamic-update-slice_fusion.4, bf16[8192,1024]{1,0:T(8,128)(2,1)} %all-gather.8.cloned.1.call-done), kind=kOutput, calls=%fused_computation.10 | convolution fusion | flops 17180917760 | bytes 35651584 | tf_op jit(solution)/shard_map/dot_general | solution.py:344
  (147 shorter events, 60.9 us)
Async XLA Ops:
  6.5 261.6 %all-gather.4.cloned.1.call-start = ((), (), s32[]{:S(2)}) async-start(), calls=%async_computation | async-start | bytes 10485760 | tf_op jit(solution)/shard_map/all_gather | solution.py:294
  11.1 275.3 %all-gather.6.cloned.1.call-start = ((), (), s32[]{:S(2)}) async-start(), calls=%async_computation.1 | async-start | bytes 10485760 | tf_op jit(solution)/shard_map/all_gather | solution.py:294
  11.8 2.7 collective-permute-start.9
  13.1 2.6 collective-permute-start.10
  13.3 3.3 collective-permute-start.11
  34.1 790.9 %all-gather.8.cloned.1.call-start = ((), (), s32[]{:S(2)}) async-start(), calls=%async_computation.2 | async-start | bytes 20971520 | tf_op jit(solution)/shard_map/all_gather | solution.py:330
  34.2 92.9 %collective-permute-start.1 = (bf16[1024,1024]{1,0:T(8,128)(2,1)}, bf16[1024,1024]{1,0:T(8,128)(2,1)}, u32[]{:S(2)}, u32[]{:S(2)}) collective-permute-start(bf16[1024,1024]{1,0:T(8,128)(2,1)} %param.6), channel_id=1, source_target_pairs={{0,4},{1,5},{2,6},{3,7},{4,0},{5,1},{6,2},{7,3},{8,12},{9,13},{10,... | collective-permute-start | bytes 6291464 | tf_op jit(solution)/shard_map/ppermute | solution.py:45
  36.6 135.5 %collective-permute-start.3 = (bf16[1024,1024]{1,0:T(8,128)(2,1)}, bf16[1024,1024]{1,0:T(8,128)(2,1)}, u32[]{:S(2)}, u32[]{:S(2)}) collective-permute-start(bf16[1024,1024]{1,0:T(8,128)(2,1)} %param.6), channel_id=1, source_target_pairs={{0,2},{1,3},{2,4},{3,5},{4,6},{5,7},{8,10},{9,11},{10,12},{11,13},... | collective-permute-start | bytes 6291464 | tf_op jit(solution)/shard_map/ppermute | solution.py:46
  127.1 45.7 %collective-permute-start.2 = (bf16[1024,1024]{1,0:T(8,128)(2,1)}, bf16[1024,1024]{1,0:T(8,128)(2,1)S(1)}, u32[]{:S(2)}, u32[]{:S(2)}) collective-permute-start(bf16[1024,1024]{1,0:T(8,128)(2,1)} %collective-permute-done.1), channel_id=1, source_target_pairs={{4,6},{5,7},{2,0},{3,1},{12,14},{13,15},{10,8},{11,9},{20,22},{21,... | collective-permute-start | bytes 6291464 | tf_op jit(solution)/shard_map/ppermute | solution.py:49
  129.1 88.6 %collective-permute-start.7 = (bf16[1024,1024]{1,0:T(8,128)(2,1)}, bf16[1024,1024]{1,0:T(8,128)(2,1)}, u32[]{:S(2)}, u32[]{:S(2)}) collective-permute-start(bf16[1024,1024]{1,0:T(8,128)(2,1)} %param.6), channel_id=1, source_target_pairs={{2,0},{3,1},{4,2},{5,3},{6,4},{7,5},{10,8},{11,9},{12,10},{13,11},... | collective-permute-start | bytes 6291464 | tf_op jit(solution)/shard_map/ppermute | solution.py:47
  131.1 104.9 %collective-permute-start = (bf16[1024,1024]{1,0:T(8,128)(2,1)}, bf16[1024,1024]{1,0:T(8,128)(2,1)}, u32[]{:S(2)}, u32[]{:S(2)}) collective-permute-start(bf16[1024,1024]{1,0:T(8,128)(2,1)} %param.6), channel_id=1, source_target_pairs={{0,1},{1,0},{2,3},{3,2},{4,5},{5,4},{6,7},{7,6},{8,9},{9,8},{10,11... | collective-permute-start | bytes 6291464 | tf_op jit(solution)/shard_map/ppermute | solution.py:43
  172.0 70.9 %collective-permute-start.5 = (bf16[1024,1024]{1,0:T(8,128)(2,1)}, bf16[1024,1024]{1,0:T(8,128)(2,1)}, u32[]{:S(2)}, u32[]{:S(2)}) collective-permute-start(bf16[1024,1024]{1,0:T(8,128)(2,1)} %collective-permute-done.3), channel_id=1, source_target_pairs={{0,1},{1,0},{2,3},{3,2},{4,5},{5,4},{6,7},{7,6},{8,9},{9,8},{10,11... | collective-permute-start | bytes 6291464 | tf_op jit(solution)/shard_map/ppermute | solution.py:43
  172.8 70.1 %collective-permute-start.4 = (bf16[1024,1024]{1,0:T(8,128)(2,1)S(1)}, bf16[1024,1024]{1,0:T(8,128)(2,1)}, u32[]{:S(2)}, u32[]{:S(2)}) collective-permute-start(bf16[1024,1024]{1,0:T(8,128)(2,1)S(1)} %collective-permute-done.2), channel_id=1, source_target_pairs={{0,1},{1,0},{6,7},{7,6},{8,9},{9,8},{14,15},{15,14},{16,17},{17,16... | collective-permute-start | bytes 6291464 | tf_op jit(solution)/shard_map/ppermute | solution.py:51
  174.7 75.1 %collective-permute-start.6 = (bf16[1024,1024]{1,0:T(8,128)(2,1)}, bf16[1024,1024]{1,0:T(8,128)(2,1)}, u32[]{:S(2)}, u32[]{:S(2)}) collective-permute-start(bf16[1024,1024]{1,0:T(8,128)(2,1)} %collective-permute-done.1), channel_id=1, source_target_pairs={{0,1},{1,0},{2,3},{3,2},{4,5},{5,4},{6,7},{7,6},{8,9},{9,8},{10,11... | collective-permute-start | bytes 6291464 | tf_op jit(solution)/shard_map/ppermute | solution.py:43
  217.7 39.3 %collective-permute-start.8 = (bf16[1024,1024]{1,0:T(8,128)(2,1)}, bf16[1024,1024]{1,0:T(8,128)(2,1)}, u32[]{:S(2)}, u32[]{:S(2)}) collective-permute-start(bf16[1024,1024]{1,0:T(8,128)(2,1)} %collective-permute-done.7), channel_id=1, source_target_pairs={{0,1},{1,0},{2,3},{3,2},{4,5},{5,4},{6,7},{7,6},{8,9},{9,8},{10,11... | collective-permute-start | bytes 6291464 | tf_op jit(solution)/shard_map/ppermute | solution.py:43
  284.0 49.5 %collective-permute-start.33 = (bf16[24,128,256]{2,1,0:T(8,128)(2,1)}, bf16[24,128,256]{2,1,0:T(8,128)(2,1)S(1)}, u32[]{:S(2)}, u32[]{:S(2)}) collective-permute-start(bf16[24,128,256]{2,1,0:T(8,128)(2,1)} %get-tuple-element.44), channel_id=1, source_target_pairs={{0,8},{8,0},{16,24},{24,16},{1,9},{9,1},{17,25},{25,17},{2,10},{10... | collective-permute-start | bytes 4718600 | tf_op jit(solution)/shard_map/ppermute | solution.py:27
  284.0 49.5 %collective-permute-start.34 = (bf16[24,128,256]{2,1,0:T(8,128)(2,1)}, bf16[24,128,256]{2,1,0:T(8,128)(2,1)S(1)}, u32[]{:S(2)}, u32[]{:S(2)}) collective-permute-start(bf16[24,128,256]{2,1,0:T(8,128)(2,1)} %get-tuple-element.45), channel_id=1, source_target_pairs={{0,16},{8,24},{16,0},{24,8},{1,17},{9,25},{17,1},{25,9},{2,18},{10... | collective-permute-start | bytes 4718600 | tf_op jit(solution)/shard_map/ppermute | solution.py:27
  301.4 29.9 %collective-permute-start.32 = (bf16[1024,256]{1,0:T(8,128)(2,1)S(1)}, bf16[1024,256]{1,0:T(8,128)(2,1)S(1)}, u32[]{:S(2)}, u32[]{:S(2)}) collective-permute-start(bf16[1024,256]{1,0:T(8,128)(2,1)S(1)} %get-tuple-element.69), channel_id=1, source_target_pairs={{0,8},{8,0},{16,24},{24,16},{1,9},{9,1},{17,25},{25,17},{2,10},{10... | collective-permute-start | bytes 1572872 | tf_op jit(solution)/shard_map/ppermute | solution.py:27
  301.6 30.8 %collective-permute-start.31 = (bf16[1024,256]{1,0:T(8,128)(2,1)S(1)}, bf16[1024,256]{1,0:T(8,128)(2,1)S(1)}, u32[]{:S(2)}, u32[]{:S(2)}) collective-permute-start(bf16[1024,256]{1,0:T(8,128)(2,1)S(1)} %get-tuple-element.70), channel_id=1, source_target_pairs={{0,16},{8,24},{16,0},{24,8},{1,17},{9,25},{17,1},{25,9},{2,18},{10... | collective-permute-start | bytes 1572872 | tf_op jit(solution)/shard_map/ppermute | solution.py:27
  333.5 1.1 copy-start
  333.5 1.7 copy-start.1
  350.1 166.1 %collective-permute-start.14 = (bf16[24,128,256]{2,1,0:T(8,128)(2,1)}, bf16[24,128,256]{2,1,0:T(8,128)(2,1)S(1)}, u32[]{:S(2)}, u32[]{:S(2)}) collective-permute-start(bf16[24,128,256]{2,1,0:T(8,128)(2,1)} %get-tuple-element.31), channel_id=1, source_target_pairs={{0,8},{8,0},{16,24},{24,16},{1,9},{9,1},{17,25},{25,17},{2,10},{10... | collective-permute-start | bytes 4718600 | tf_op jit(solution)/shard_map/ppermute | solution.py:27
  350.4 165.7 %collective-permute-start.15 = (bf16[24,128,256]{2,1,0:T(8,128)(2,1)}, bf16[24,128,256]{2,1,0:T(8,128)(2,1)S(1)}, u32[]{:S(2)}, u32[]{:S(2)}) collective-permute-start(bf16[24,128,256]{2,1,0:T(8,128)(2,1)} %get-tuple-element.32), channel_id=1, source_target_pairs={{0,16},{8,24},{16,0},{24,8},{1,17},{9,25},{17,1},{25,9},{2,18},{10... | collective-permute-start | bytes 4718600 | tf_op jit(solution)/shard_map/ppermute | solution.py:27
  352.5 183.1 %collective-permute-start.16 = (bf16[24,128,256]{2,1,0:T(8,128)(2,1)}, bf16[24,128,256]{2,1,0:T(8,128)(2,1)}, u32[]{:S(2)}, u32[]{:S(2)}) collective-permute-start(bf16[24,128,256]{2,1,0:T(8,128)(2,1)} %get-tuple-element.33), channel_id=1, source_target_pairs={{0,8},{8,0},{16,24},{24,16},{1,9},{9,1},{17,25},{25,17},{2,10},{10... | collective-permute-start | bytes 4718600 | tf_op jit(solution)/shard_map/ppermute | solution.py:27
  352.7 182.8 %collective-permute-start.17 = (bf16[24,128,256]{2,1,0:T(8,128)(2,1)}, bf16[24,128,256]{2,1,0:T(8,128)(2,1)}, u32[]{:S(2)}, u32[]{:S(2)}) collective-permute-start(bf16[24,128,256]{2,1,0:T(8,128)(2,1)} %get-tuple-element.34), channel_id=1, source_target_pairs={{0,16},{8,24},{16,0},{24,8},{1,17},{9,25},{17,1},{25,9},{2,18},{10... | collective-permute-start | bytes 4718600 | tf_op jit(solution)/shard_map/ppermute | solution.py:27
  354.4 136.9 %collective-permute-start.13 = (bf16[1024,256]{1,0:T(8,128)(2,1)S(1)}, bf16[1024,256]{1,0:T(8,128)(2,1)S(1)}, u32[]{:S(2)}, u32[]{:S(2)}) collective-permute-start(bf16[1024,256]{1,0:T(8,128)(2,1)S(1)} %get-tuple-element.73), channel_id=1, source_target_pairs={{0,8},{8,0},{16,24},{24,16},{1,9},{9,1},{17,25},{25,17},{2,10},{10... | collective-permute-start | bytes 1572872 | tf_op jit(solution)/shard_map/ppermute | solution.py:27
  491.3 23.8 %collective-permute-start.12 = (bf16[1024,256]{1,0:T(8,128)(2,1)S(1)}, bf16[1024,256]{1,0:T(8,128)(2,1)S(1)}, u32[]{:S(2)}, u32[]{:S(2)}) collective-permute-start(bf16[1024,256]{1,0:T(8,128)(2,1)S(1)} %get-tuple-element.74), channel_id=1, source_target_pairs={{0,16},{8,24},{16,0},{24,8},{1,17},{9,25},{17,1},{25,9},{2,18},{10... | collective-permute-start | bytes 1572872 | tf_op jit(solution)/shard_map/ppermute | solution.py:27
  516.2 1.1 copy-start.2
  517.3 1.2 copy-start.3
  533.4 5.3 collective-permute-start.18
  534.0 61.6 %copy-start.7 = (f32[2,64,128]{2,1,0:T(8,128)S(1)}, f32[2,64,128]{2,1,0:T(8,128)}, u32[]{:S(2)}) copy-start(f32[2,64,128]{2,1,0:T(8,128)} %get-tuple-element.50.refs_11_) | copy-start | bytes 196612
  534.0 85.0 %copy-start.8 = (f32[2,64,128]{2,1,0:T(8,128)S(1)}, f32[2,64,128]{2,1,0:T(8,128)}, u32[]{:S(2)}) copy-start(f32[2,64,128]{2,1,0:T(8,128)} %get-tuple-element.51.refs_12_) | copy-start | bytes 196612
  534.0 5.3 collective-permute-start.19
  538.6 0.7 copy-start.10
  562.4 25.7 %collective-permute-start.20 = (f32[1024,256]{1,0:T(8,128)}, f32[1024,256]{1,0:T(8,128)S(1)}, u32[]{:S(2)}, u32[]{:S(2)}) collective-permute-start(f32[1024,256]{1,0:T(8,128)} %get-tuple-element.38), channel_id=1, source_target_pairs={{0,16},{8,24},{16,0},{24,8},{1,17},{9,25},{17,1},{25,9},{2,18},{10... | collective-permute-start | bytes 3145736 | tf_op jit(solution)/shard_map/ppermute | solution.py:27
  563.3 26.2 %collective-permute-start.21 = (f32[1024,256]{1,0:T(8,128)}, f32[1024,256]{1,0:T(8,128)S(1)}, u32[]{:S(2)}, u32[]{:S(2)}) collective-permute-start(f32[1024,256]{1,0:T(8,128)} %get-tuple-element.40), channel_id=1, source_target_pairs={{0,8},{8,0},{16,24},{24,16},{1,9},{9,1},{17,25},{25,17},{2,10},{10... | collective-permute-start | bytes 3145736 | tf_op jit(solution)/shard_map/ppermute | solution.py:27
  564.6 54.4 %collective-permute-start.35 = (bf16[24,128,256]{2,1,0:T(8,128)(2,1)}, bf16[24,128,256]{2,1,0:T(8,128)(2,1)S(1)}, u32[]{:S(2)}, u32[]{:S(2)}) collective-permute-start(bf16[24,128,256]{2,1,0:T(8,128)(2,1)} %get-tuple-element.48), channel_id=1, source_target_pairs={{0,8},{8,0},{16,24},{24,16},{1,9},{9,1},{17,25},{25,17},{2,10},{10... | collective-permute-start | bytes 4718600 | tf_op jit(solution)/shard_map/ppermute | solution.py:27
  564.8 57.1 %collective-permute-start.36 = (bf16[24,128,256]{2,1,0:T(8,128)(2,1)}, bf16[24,128,256]{2,1,0:T(8,128)(2,1)S(1)}, u32[]{:S(2)}, u32[]{:S(2)}) collective-permute-start(bf16[24,128,256]{2,1,0:T(8,128)(2,1)} %get-tuple-element.49), channel_id=1, source_target_pairs={{0,16},{8,24},{16,0},{24,8},{1,17},{9,25},{17,1},{25,9},{2,18},{10... | collective-permute-start | bytes 4718600 | tf_op jit(solution)/shard_map/ppermute | solution.py:27
  592.3 57.2 %collective-permute-start.23 = (bf16[1024,512]{1,0:T(8,128)(2,1)}, bf16[1024,512]{1,0:T(8,128)(2,1)}, u32[]{:S(2)}, u32[]{:S(2)}) collective-permute-start(bf16[1024,512]{1,0:T(8,128)(2,1)} %get-tuple-element.71), channel_id=1, source_target_pairs={{0,4},{1,5},{2,6},{3,7},{4,0},{5,1},{6,2},{7,3},{8,12},{9,13},{10,... | collective-permute-start | bytes 3145736 | tf_op jit(solution)/shard_map/ppermute | solution.py:45
  592.3 68.2 %collective-permute-start.25 = (bf16[1024,512]{1,0:T(8,128)(2,1)}, bf16[1024,512]{1,0:T(8,128)(2,1)}, u32[]{:S(2)}, u32[]{:S(2)}) collective-permute-start(bf16[1024,512]{1,0:T(8,128)(2,1)} %get-tuple-element.71), channel_id=1, source_target_pairs={{0,2},{1,3},{2,4},{3,5},{4,6},{5,7},{8,10},{9,11},{10,12},{11,13},... | collective-permute-start | bytes 3145736 | tf_op jit(solution)/shard_map/ppermute | solution.py:46
  595.7 27.5 %collective-permute-start.37 = (f32[2,64,128]{2,1,0:T(8,128)S(1)}, f32[2,64,128]{2,1,0:T(8,128)S(1)}, u32[]{:S(2)}, u32[]{:S(2)}) collective-permute-start(f32[2,64,128]{2,1,0:T(8,128)S(1)} %copy-done.7), channel_id=1, source_target_pairs={{0,16},{8,24},{16,0},{24,8},{1,17},{9,25},{17,1},{25,9},{2,18},{10... | collective-permute-start | bytes 196616 | tf_op jit(solution)/shard_map/ppermute | solution.py:27
  619.0 4.1 copy-start.4
  619.0 4.1 collective-permute-start.38
  621.8 1.3 copy-start.5
  623.1 0.6 copy-start.9
  647.1 21.0 %collective-permute-start.39 = (f32[1024,256]{1,0:T(8,128)}, f32[1024,256]{1,0:T(8,128)S(1)}, u32[]{:S(2)}, u32[]{:S(2)}) collective-permute-start(f32[1024,256]{1,0:T(8,128)} %get-tuple-element.53), channel_id=1, source_target_pairs={{0,16},{8,24},{16,0},{24,8},{1,17},{9,25},{17,1},{25,9},{2,18},{10... | collective-permute-start | bytes 3145736 | tf_op jit(solution)/shard_map/ppermute | solution.py:27
  649.5 24.3 %collective-permute-start.24 = (bf16[1024,512]{1,0:T(8,128)(2,1)}, bf16[1024,512]{1,0:T(8,128)(2,1)S(1)}, u32[]{:S(2)}, u32[]{:S(2)}) collective-permute-start(bf16[1024,512]{1,0:T(8,128)(2,1)} %collective-permute-done.23), channel_id=1, source_target_pairs={{4,6},{5,7},{2,0},{3,1},{12,14},{13,15},{10,8},{11,9},{20,22},{21,... | collective-permute-start | bytes 3145736 | tf_op jit(solution)/shard_map/ppermute | solution.py:49
  651.8 24.4 %collective-permute-start.22 = (bf16[1024,512]{1,0:T(8,128)(2,1)}, bf16[1024,512]{1,0:T(8,128)(2,1)S(1)}, u32[]{:S(2)}, u32[]{:S(2)}) collective-permute-start(bf16[1024,512]{1,0:T(8,128)(2,1)} %get-tuple-element.71), channel_id=1, source_target_pairs={{0,1},{1,0},{2,3},{3,2},{4,5},{5,4},{6,7},{7,6},{8,9},{9,8},{10,11... | collective-permute-start | bytes 3145736 | tf_op jit(solution)/shard_map/ppermute | solution.py:43
  657.5 34.2 %collective-permute-start.29 = (bf16[1024,512]{1,0:T(8,128)(2,1)}, bf16[1024,512]{1,0:T(8,128)(2,1)}, u32[]{:S(2)}, u32[]{:S(2)}) collective-permute-start(bf16[1024,512]{1,0:T(8,128)(2,1)} %get-tuple-element.71), channel_id=1, source_target_pairs={{2,0},{3,1},{4,2},{5,3},{6,4},{7,5},{10,8},{11,9},{12,10},{13,11},... | collective-permute-start | bytes 3145736 | tf_op jit(solution)/shard_map/ppermute | solution.py:47
  660.5 38.4 %collective-permute-start.40 = (f32[1024,256]{1,0:T(8,128)}, f32[1024,256]{1,0:T(8,128)}, u32[]{:S(2)}, u32[]{:S(2)}) collective-permute-start(f32[1024,256]{1,0:T(8,128)} %get-tuple-element.55), channel_id=1, source_target_pairs={{0,8},{8,0},{16,24},{24,16},{1,9},{9,1},{17,25},{25,17},{2,10},{10... | collective-permute-start | bytes 3145736 | tf_op jit(solution)/shard_map/ppermute | solution.py:27
  668.1 5.7 copy-start.6
  668.1 34.9 %collective-permute-start.27 = (bf16[1024,512]{1,0:T(8,128)(2,1)}, bf16[1024,512]{1,0:T(8,128)(2,1)}, u32[]{:S(2)}, u32[]{:S(2)}) collective-permute-start(bf16[1024,512]{1,0:T(8,128)(2,1)} %collective-permute-done.25), channel_id=1, source_target_pairs={{0,1},{1,0},{2,3},{3,2},{4,5},{5,4},{6,7},{7,6},{8,9},{9,8},{10,11... | collective-permute-start | bytes 3145736 | tf_op jit(solution)/shard_map/ppermute | solution.py:43
  673.8 29.2 %collective-permute-start.26 = (bf16[1024,512]{1,0:T(8,128)(2,1)S(1)}, bf16[1024,512]{1,0:T(8,128)(2,1)S(1)}, u32[]{:S(2)}, u32[]{:S(2)}) collective-permute-start(bf16[1024,512]{1,0:T(8,128)(2,1)S(1)} %collective-permute-done.24), channel_id=1, source_target_pairs={{0,1},{1,0},{6,7},{7,6},{8,9},{9,8},{14,15},{15,14},{16,17},{17,16... | collective-permute-start | bytes 3145736 | tf_op jit(solution)/shard_map/ppermute | solution.py:51
  676.2 31.7 %collective-permute-start.28 = (bf16[1024,512]{1,0:T(8,128)(2,1)}, bf16[1024,512]{1,0:T(8,128)(2,1)S(1)}, u32[]{:S(2)}, u32[]{:S(2)}) collective-permute-start(bf16[1024,512]{1,0:T(8,128)(2,1)} %collective-permute-done.23), channel_id=1, source_target_pairs={{0,1},{1,0},{2,3},{3,2},{4,5},{5,4},{6,7},{7,6},{8,9},{9,8},{10,11... | collective-permute-start | bytes 3145736 | tf_op jit(solution)/shard_map/ppermute | solution.py:43
  691.6 20.0 %collective-permute-start.30 = (bf16[1024,512]{1,0:T(8,128)(2,1)}, bf16[1024,512]{1,0:T(8,128)(2,1)S(1)}, u32[]{:S(2)}, u32[]{:S(2)}) collective-permute-start(bf16[1024,512]{1,0:T(8,128)(2,1)} %collective-permute-done.29), channel_id=1, source_target_pairs={{0,1},{1,0},{2,3},{3,2},{4,5},{5,4},{6,7},{7,6},{8,9},{9,8},{10,11... | collective-permute-start | bytes 3145736 | tf_op jit(solution)/shard_map/ppermute | solution.py:43
  714.4 45.3 %collective-permute-start.42 = (bf16[1024,512]{1,0:T(8,128)(2,1)}, bf16[1024,512]{1,0:T(8,128)(2,1)S(1)}, u32[]{:S(2)}, u32[]{:S(2)}) collective-permute-start(bf16[1024,512]{1,0:T(8,128)(2,1)} %get-tuple-element.67), channel_id=1, source_target_pairs={{0,4},{1,5},{2,6},{3,7},{4,0},{5,1},{6,2},{7,3},{8,12},{9,13},{10,... | collective-permute-start | bytes 3145736 | tf_op jit(solution)/shard_map/ppermute | solution.py:45
  714.4 67.7 %collective-permute-start.44 = (bf16[1024,512]{1,0:T(8,128)(2,1)}, bf16[1024,512]{1,0:T(8,128)(2,1)}, u32[]{:S(2)}, u32[]{:S(2)}) collective-permute-start(bf16[1024,512]{1,0:T(8,128)(2,1)} %get-tuple-element.67), channel_id=1, source_target_pairs={{0,2},{1,3},{2,4},{3,5},{4,6},{5,7},{8,10},{9,11},{10,12},{11,13},... | collective-permute-start | bytes 3145736 | tf_op jit(solution)/shard_map/ppermute | solution.py:46
  759.7 26.2 %collective-permute-start.43 = (bf16[1024,512]{1,0:T(8,128)(2,1)S(1)}, bf16[1024,512]{1,0:T(8,128)(2,1)S(1)}, u32[]{:S(2)}, u32[]{:S(2)}) collective-permute-start(bf16[1024,512]{1,0:T(8,128)(2,1)S(1)} %collective-permute-done.42), channel_id=1, source_target_pairs={{4,6},{5,7},{2,0},{3,1},{12,14},{13,15},{10,8},{11,9},{20,22},{21,... | collective-permute-start | bytes 3145736 | tf_op jit(solution)/shard_map/ppermute | solution.py:49
  764.4 44.1 %collective-permute-start.48 = (bf16[1024,512]{1,0:T(8,128)(2,1)}, bf16[1024,512]{1,0:T(8,128)(2,1)}, u32[]{:S(2)}, u32[]{:S(2)}) collective-permute-start(bf16[1024,512]{1,0:T(8,128)(2,1)} %get-tuple-element.67), channel_id=1, source_target_pairs={{2,0},{3,1},{4,2},{5,3},{6,4},{7,5},{10,8},{11,9},{12,10},{13,11},... | collective-permute-start | bytes 3145736 | tf_op jit(solution)/shard_map/ppermute | solution.py:47
  766.6 43.7 %collective-permute-start.41 = (bf16[1024,512]{1,0:T(8,128)(2,1)}, bf16[1024,512]{1,0:T(8,128)(2,1)}, u32[]{:S(2)}, u32[]{:S(2)}) collective-permute-start(bf16[1024,512]{1,0:T(8,128)(2,1)} %get-tuple-element.67), channel_id=1, source_target_pairs={{0,1},{1,0},{2,3},{3,2},{4,5},{5,4},{6,7},{7,6},{8,9},{9,8},{10,11... | collective-permute-start | bytes 3145736 | tf_op jit(solution)/shard_map/ppermute | solution.py:43
  782.2 32.9 %collective-permute-start.46 = (bf16[1024,512]{1,0:T(8,128)(2,1)}, bf16[1024,512]{1,0:T(8,128)(2,1)}, u32[]{:S(2)}, u32[]{:S(2)}) collective-permute-start(bf16[1024,512]{1,0:T(8,128)(2,1)} %collective-permute-done.44), channel_id=1, source_target_pairs={{0,1},{1,0},{2,3},{3,2},{4,5},{5,4},{6,7},{7,6},{8,9},{9,8},{10,11... | collective-permute-start | bytes 3145736 | tf_op jit(solution)/shard_map/ppermute | solution.py:43
  785.9 29.1 %collective-permute-start.45 = (bf16[1024,512]{1,0:T(8,128)(2,1)S(1)}, bf16[1024,512]{1,0:T(8,128)(2,1)S(1)}, u32[]{:S(2)}, u32[]{:S(2)}) collective-permute-start(bf16[1024,512]{1,0:T(8,128)(2,1)S(1)} %collective-permute-done.43), channel_id=1, source_target_pairs={{0,1},{1,0},{6,7},{7,6},{8,9},{9,8},{14,15},{15,14},{16,17},{17,16... | collective-permute-start | bytes 3145736 | tf_op jit(solution)/shard_map/ppermute | solution.py:51
  786.6 32.1 %collective-permute-start.47 = (bf16[1024,512]{1,0:T(8,128)(2,1)S(1)}, bf16[1024,512]{1,0:T(8,128)(2,1)}, u32[]{:S(2)}, u32[]{:S(2)}) collective-permute-start(bf16[1024,512]{1,0:T(8,128)(2,1)S(1)} %collective-permute-done.42), channel_id=1, source_target_pairs={{0,1},{1,0},{2,3},{3,2},{4,5},{5,4},{6,7},{7,6},{8,9},{9,8},{10,11... | collective-permute-start | bytes 3145736 | tf_op jit(solution)/shard_map/ppermute | solution.py:43
  808.5 15.2 %collective-permute-start.49 = (bf16[1024,512]{1,0:T(8,128)(2,1)}, bf16[1024,512]{1,0:T(8,128)(2,1)S(1)}, u32[]{:S(2)}, u32[]{:S(2)}) collective-permute-start(bf16[1024,512]{1,0:T(8,128)(2,1)} %collective-permute-done.48), channel_id=1, source_target_pairs={{0,1},{1,0},{2,3},{3,2},{4,5},{5,4},{6,7},{7,6},{8,9},{9,8},{10,11... | collective-permute-start | bytes 3145736 | tf_op jit(solution)/shard_map/ppermute | solution.py:43
  (2 other events, 1.2 us)
Sparse Core Ops, SparseCore 0:
  11.2 88.4 all-gather.3
  101.5 87.4 all-gather.5
  350.2 220.2 all-gather.7

commit v6 on v5

--- a/solution.py
+++ b/solution.py
@@ -47,16 +47,17 @@
     back3 = lax.ppermute(piece, "fsdp", chip_pairs([(1, 0), (2, 1), (3, 2)]))
     own_there = swap(piece)
     ends = lax.ppermute(back2, "fsdp", chip_pairs([(2, 3), (1, 0)]))
-    there1, there2, there3 = swap(back1), swap(back2), swap(back3)
+    there2 = swap(back2)
+    there1, there3 = swap(back1), swap(back3)
     ends_there = lax.ppermute(ends, "fsdp", [(0, 1), (1, 0), (6, 7), (7, 6)])
     found = []
     for step, (here, there) in enumerate((
         (piece, own_there),
+        (back2, there2),
         (jnp.where(chip == 0, ends, back1), jnp.where(chip == 0, ends_there, there1)),
-        (back2, there2),
         (jnp.where(chip == 3, ends, back3), jnp.where(chip == 3, ends_there, there3)),
     )):
-        owner = (chip + 4 - step) % 4
+        owner = (chip + 4 - (0, 2, 1, 3)[step]) % 4
         found.append((owner * 2 + core, here))
         found.append((owner * 2 + 1 - core, there))
     return found
@@ -337,6 +338,7 @@
         mixed = jnp.concatenate(
             [(partial[axis] + others[axis]).astype(jnp.bfloat16) for axis in range(AXES)], axis=1
         )
+        mixed = lax.optimization_barrier(mixed)
         pieces = pieces_over_fsdp(mixed)
         for owner, piece in pieces:
             start = owner * local_width + step * share

time: 857 us -> 864 us (level)
  the two profiles are of different devices: /device:TPU:11 before, /device:TPU:25 now
where the time goes in v6:
time: 864 us; the launch traced here: 851 us
  waiting for transfers between devices  447 us (52%)
  starting transfers between devices  140 us (16%)
  Pallas kernels  104 us (12%)
  matrix products  54.1 us (6%)
  other arithmetic  48.4 us (6%)
  local copies, waits for them, and re-layouts  43.8 us (5%)
  between operations  13.6 us (2%)
    ppermute x23, waiting for transfers between devices, over_dp(): lax.ppermute(value, 'dp', [(i, i ^ bit) for i in range(lax.axis_size('dp'...  224 us
    ppermute x3, waiting for transfers between devices, pieces_over_fsdp(): lax.ppermute(piece, 'fsdp', chip_pairs([(0, 2), (1, 3), (2, 0), (3, 1)]))  152 us
    pallas_call x4, Pallas kernels, span_call(): pl.pallas_call(functools.partial(kernel, spans, span, together), grid_spe...  74.8 us
    ppermute x3, starting transfers between devices, pieces_over_fsdp(): lax.ppermute(piece, 'fsdp', chip_pairs([(0, 2), (1, 3), (2, 0), (3, 1)]))  74.2 us
    ppermute x3, waiting for transfers between devices, pieces_over_fsdp(): ends = lax.ppermute(back2, 'fsdp', chip_pairs([(2, 3), (1, 0)]))  67 us
    dot_general x2, matrix products, work(): jnp.dot(normed, columns[step], preferred_element_type=jnp.float32)  30.9 us
    pallas_call x2, Pallas kernels, pick_blocks(): pl.pallas_call(pick_kernel, grid_spec=pltpu.PrefetchScalarGridSpec(num_sc...  29.2 us
    ppermute x23, starting transfers between devices, over_dp(): lax.ppermute(value, 'dp', [(i, i ^ bit) for i in range(lax.axis_size('dp'...  23.6 us
  transfers between devices with their start and end apart: 53, of which 15 were waited for; matrix products, arithmetic and copies ran while one was open for 13% of the time, Pallas kernels for 10%

profile of v6, /device:TPU:25, one launch (start us, length us, event | category | flops | bytes accessed | tf_op | source)
XLA Modules:
  0.0 851.4 jit_solution(14757409228539051981)
XLA Ops:
  6.5 4.5 fusion.21
  15.7 1.9 collective-permute-done.11
  19.5 14.7 %pick.2 = (bf16[24,128,256]{2,1,0:T(8,128)(2,1)}, bf16[24,128,256]{2,1,0:T(8,128)(2,1)}, bf16[24,128,256]{2,1,0:T(8,128)(2,1)}, bf16[24,128,256]{2,1,0:T(8,128)(2,1)}) custom-call(s32[24]{0:T(128)} %get-tuple-element.76.first_ref, s32[24]{0:T(128)} %get-tuple-element.75.second_ref, bf16[32,2,128,1024]{3,2,1,0:T(8,128)(2,1)} %bitcast.28, ...), custom_call_target="tpu_custom_call" | custom-call | bytes 12582912 | tf_op jit(solution)/shard_map/pick/pallas_call | solution.py:75
  35.7 92.3 %collective-permute-done.1 = bf16[1024,1024]{1,0:T(8,128)(2,1)} collective-permute-done((bf16[1024,1024]{1,0:T(8,128)(2,1)}, bf16[1024,1024]{1,0:T(8,128)(2,1)}, u32[]{:S(2)}, u32[]{:S(2)}) %collective-permute-start.1) | collective-permute-done | bytes 2097184 | tf_op jit(solution)/shard_map/ppermute | solution.py:45
  129.3 5.5 collective-permute-start.7
  136.4 40.4 %collective-permute-done.3 = bf16[1024,1024]{1,0:T(8,128)(2,1)S(1)} collective-permute-done((bf16[1024,1024]{1,0:T(8,128)(2,1)}, bf16[1024,1024]{1,0:T(8,128)(2,1)S(1)}, u32[]{:S(2)}, u32[]{:S(2)}) %collective-permute-start.3) | collective-permute-done | bytes 2097184 | tf_op jit(solution)/shard_map/ppermute | solution.py:49
  176.8 3.2 collective-permute-start.5
  180.2 6.0 broadcast_in_dim.36
  186.1 3.2 constant_dynamic-update-slice_fusion.11
  189.3 14.5 %pick.3 = (bf16[24,128,256]{2,1,0:T(8,128)(2,1)}, bf16[24,128,256]{2,1,0:T(8,128)(2,1)}, bf16[24,128,256]{2,1,0:T(8,128)(2,1)}, bf16[24,128,256]{2,1,0:T(8,128)(2,1)}) custom-call(s32[24]{0:T(128)} %get-tuple-element.76.first_ref, s32[24]{0:T(128)} %get-tuple-element.75.second_ref, bf16[32,2,128,1024]{3,2,1,0:T(8,128)(2,1)} %bitcast.30, ...), custom_call_target="tpu_custom_call" | custom-call | bytes 12582912 | tf_op jit(solution)/shard_map/pick/pallas_call | solution.py:75
  204.5 3.1 constant_dynamic-update-slice_fusion.10
  207.6 3.1 constant_dynamic-update-slice_fusion.9
  210.7 3.1 constant_dynamic-update-slice_fusion.8
  213.7 3.9 select_dynamic-update-slice_fusion.3
  217.6 3.9 select_dynamic-update-slice_fusion.2
  221.5 2.3 select_dynamic-update-slice_fusion.1
  223.8 3.9 select_dynamic-update-slice_fusion
  227.7 7.2 fusion
  234.9 15.9 %fusion.6 = bf16[1024,512]{1,0:T(8,128)(2,1)} fusion(bf16[8192,512]{1,0:T(8,128)(2,1)} %all-gather.4.cloned.1.call-done, bf16[1024,8192]{1,0:T(8,128)(2,1)} %select_dynamic-update-slice_fusion, f32[1024]{0:T(1024)S(1)} %add_rsqrt_fusion), kind=kOutput, calls=%fused_computation.11 | convolution fusion | flops 8615624704 | bytes 26218496 | tf_op jit(solution)/shard_map/dot_general | solution.py:313
  250.8 1.7 collective-permute-start.33
  253.4 15.0 %fusion.9 = bf16[1024,512]{1,0:T(8,128)(2,1)S(1)} fusion(bf16[8192,512]{1,0:T(8,128)(2,1)} %all-gather.6.cloned.1.call-done, bf16[1024,8192]{1,0:T(8,128)(2,1)} %select_dynamic-update-slice_fusion, f32[1024]{0:T(1024)S(1)} %add_rsqrt_fusion), kind=kOutput, calls=%fused_computation.12 | convolution fusion | flops 8615624704 | bytes 26218496 | tf_op jit(solution)/shard_map/dot_general | solution.py:313
  268.5 1.6 collective-permute-start.32
  271.5 26.8 %collective-permute-done.32 = bf16[1024,256]{1,0:T(8,128)(2,1)S(1)} collective-permute-done((bf16[1024,256]{1,0:T(8,128)(2,1)S(1)}, bf16[1024,256]{1,0:T(8,128)(2,1)S(1)}, u32[]{:S(2)}, u32[]{:S(2)}) %collective-permute-start.32) | collective-permute-done | bytes 524320 | tf_op jit(solution)/shard_map/ppermute | solution.py:27
  302.0 14.9 %stats.3 = (f32[2,64,128]{2,1,0:T(8,128)}, f32[2,64,128]{2,1,0:T(8,128)}) custom-call(s32[32]{0:T(128)} %get-tuple-element.78.refs_0_, s32[32]{0:T(128)} %get-tuple-element.79.refs_1_, s32[32]{0:T(128)} %get-tuple-element.77.refs_2_, s32[32]{0:T(128)} %pad_add_fusion.5.refs_3_, bf16[2048,256]{1,0:T(8,128)(2,1)} %pad_maximum_fusion.3.refs_4_, ...), custom_call_target="tpu_custom_call" | custom-call | flops 1073741824 | bytes 7340032 | tf_op jit(solution)/shard_map/stats/pallas_call | solution.py:222
  322.4 29.2 %collective-permute-done.14.refs_7_ = bf16[24,128,256]{2,1,0:T(8,128)(2,1)S(1)} collective-permute-done((bf16[24,128,256]{2,1,0:T(8,128)(2,1)}, bf16[24,128,256]{2,1,0:T(8,128)(2,1)S(1)}, u32[]{:S(2)}, u32[]{:S(2)}) %collective-permute-start.14) | collective-permute-done | bytes 1572896 | tf_op jit(solution)/shard_map/ppermute | solution.py:27
  351.6 2.2 collective-permute-start.12
  353.7 75.7 %collective-permute-done.13 = bf16[1024,256]{1,0:T(8,128)(2,1)S(1)} collective-permute-done((bf16[1024,256]{1,0:T(8,128)(2,1)S(1)}, bf16[1024,256]{1,0:T(8,128)(2,1)S(1)}, u32[]{:S(2)}, u32[]{:S(2)}) %collective-permute-start.13) | collective-permute-done | bytes 524320 | tf_op jit(solution)/shard_map/ppermute | solution.py:27
  429.4 2.3 collective-permute-start.35
  435.9 14.9 %stats.2 = (f32[2,64,128]{2,1,0:T(8,128)}, f32[2,64,128]{2,1,0:T(8,128)}) custom-call(s32[32]{0:T(128)} %get-tuple-element.78.refs_0_, s32[32]{0:T(128)} %get-tuple-element.79.refs_1_, s32[32]{0:T(128)} %get-tuple-element.77.refs_2_, s32[32]{0:T(128)} %pad_add_fusion.5.refs_3_, bf16[2048,256]{1,0:T(8,128)(2,1)} %pad_maximum_fusion.refs_4_, ...), custom_call_target="tpu_custom_call" | custom-call | flops 1073741824 | bytes 7340032 | tf_op jit(solution)/shard_map/stats/pallas_call | solution.py:222
  452.5 42.4 %collective-permute-done.18.refs_13_ = f32[2,64,128]{2,1,0:T(8,128)S(1)} collective-permute-done((f32[2,64,128]{2,1,0:T(8,128)}, f32[2,64,128]{2,1,0:T(8,128)S(1)}, u32[]{:S(2)}, u32[]{:S(2)}) %collective-permute-start.18) | collective-permute-done | bytes 65568 | tf_op jit(solution)/shard_map/ppermute | solution.py:27
  496.2 22.5 %mix.2 = (f32[1024,256]{1,0:T(8,128)}, f32[1024,256]{1,0:T(8,128)}, f32[1024,256]{1,0:T(8,128)}, f32[1024,256]{1,0:T(8,128)}) custom-call(s32[32]{0:T(128)} %get-tuple-element.78.refs_0_, s32[32]{0:T(128)} %get-tuple-element.79.refs_1_, s32[32]{0:T(128)} %get-tuple-element.77.refs_2_, s32[32]{0:T(128)} %pad_add_fusion.5.refs_3_, ...), custom_call_target="tpu_custom_call" | custom-call | flops 2147483648 | bytes 14680064 | tf_op jit(solution)/shard_map/mix/pallas_call | solution.py:222
  518.7 1.7 collective-permute-start.20
  520.4 1.5 collective-permute-start.21
  522.0 45.1 %collective-permute-done.37.refs_13_ = f32[2,64,128]{2,1,0:T(8,128)S(1)} collective-permute-done((f32[2,64,128]{2,1,0:T(8,128)S(1)}, f32[2,64,128]{2,1,0:T(8,128)S(1)}, u32[]{:S(2)}, u32[]{:S(2)}) %collective-permute-start.37) | collective-permute-done | bytes 65568 | tf_op jit(solution)/shard_map/ppermute | solution.py:27
  569.1 22.6 %mix.3 = (f32[1024,256]{1,0:T(8,128)}, f32[1024,256]{1,0:T(8,128)}, f32[1024,256]{1,0:T(8,128)}, f32[1024,256]{1,0:T(8,128)}) custom-call(s32[32]{0:T(128)} %get-tuple-element.78.refs_0_, s32[32]{0:T(128)} %get-tuple-element.79.refs_1_, s32[32]{0:T(128)} %get-tuple-element.77.refs_2_, s32[32]{0:T(128)} %pad_add_fusion.5.refs_3_, ...), custom_call_target="tpu_custom_call" | custom-call | flops 2147483648 | bytes 14680064 | tf_op jit(solution)/shard_map/mix/pallas_call | solution.py:222
  592.4 1.3 add_convert_fusion.3
  593.8 1.3 add_convert_fusion.2
  595.2 57.2 %collective-permute-start.23 = (bf16[1024,512]{1,0:T(8,128)(2,1)S(1)}, bf16[1024,512]{1,0:T(8,128)(2,1)}, u32[]{:S(2)}, u32[]{:S(2)}) collective-permute-start(bf16[1024,512]{1,0:T(8,128)(2,1)S(1)} %pad_maximum_fusion.2), channel_id=1, source_target_pairs={{0,4},{1,5},{2,6},{3,7},{4,0},{5,1},{6,2},{7,3},{8,12},{9,13},{10,... | collective-permute-start | bytes 3145736 | tf_op jit(solution)/shard_map/ppermute | solution.py:45
  652.4 1.3 collective-permute-start.40
  655.1 3.2 collective-permute-start.22
  658.3 5.2 collective-permute-start.29
  663.6 34.6 %collective-permute-done.23 = bf16[1024,512]{1,0:T(8,128)(2,1)} collective-permute-done((bf16[1024,512]{1,0:T(8,128)(2,1)S(1)}, bf16[1024,512]{1,0:T(8,128)(2,1)}, u32[]{:S(2)}, u32[]{:S(2)}) %collective-permute-start.23) | collective-permute-done | bytes 1048608 | tf_op jit(solution)/shard_map/ppermute | solution.py:45
  699.5 1.4 add_convert_fusion.1
  700.8 1.3 add_convert_fusion
  702.2 1.7 collective-permute-start.24
  704.0 16.8 %collective-permute-start.42 = (bf16[1024,512]{1,0:T(8,128)(2,1)S(1)}, bf16[1024,512]{1,0:T(8,128)(2,1)}, u32[]{:S(2)}, u32[]{:S(2)}) collective-permute-start(bf16[1024,512]{1,0:T(8,128)(2,1)S(1)} %pad_maximum_fusion.5), channel_id=1, source_target_pairs={{0,4},{1,5},{2,6},{3,7},{4,0},{5,1},{6,2},{7,3},{8,12},{9,13},{10,... | collective-permute-start | bytes 3145736 | tf_op jit(solution)/shard_map/ppermute | solution.py:45
  721.2 5.6 collective-permute-done.25
  726.7 4.3 collective-permute-start.27
  732.2 2.3 constant_dynamic-update-slice_fusion.6
  734.6 2.3 constant_dynamic-update-slice_fusion.5
  738.1 4.1 collective-permute-start.48
  742.2 24.7 %collective-permute-done.42 = bf16[1024,512]{1,0:T(8,128)(2,1)} collective-permute-done((bf16[1024,512]{1,0:T(8,128)(2,1)S(1)}, bf16[1024,512]{1,0:T(8,128)(2,1)}, u32[]{:S(2)}, u32[]{:S(2)}) %collective-permute-start.42) | collective-permute-done | bytes 1048608 | tf_op jit(solution)/shard_map/ppermute | solution.py:45
  768.2 2.3 constant_dynamic-update-slice_fusion.4
  770.6 2.5 select_dynamic-update-slice_fusion.11
  774.0 2.5 select_dynamic-update-slice_fusion.10
  777.7 4.9 collective-permute-done.45
  782.6 1.4 collective-permute-start.47
  784.0 21.1 %collective-permute-done.44 = bf16[1024,512]{1,0:T(8,128)(2,1)S(1)} collective-permute-done((bf16[1024,512]{1,0:T(8,128)(2,1)}, bf16[1024,512]{1,0:T(8,128)(2,1)S(1)}, u32[]{:S(2)}, u32[]{:S(2)}) %collective-permute-start.44) | collective-permute-done | bytes 1048608 | tf_op jit(solution)/shard_map/ppermute | solution.py:49
  805.1 3.0 collective-permute-start.46
  808.1 2.6 select_dynamic-update-slice_fusion.8
  812.9 2.3 constant_dynamic-update-slice_fusion.1
  817.6 1.3 select_dynamic-update-slice_fusion.6
  820.3 1.4 select_dynamic-update-slice_fusion.4
  821.7 23.2 %convolution_convert_fusion = bf16[1024,1024]{1,0:T(8,128)(2,1)} fusion(bf16[1024,8192]{1,0:T(8,128)(2,1)} %select_dynamic-update-slice_fusion.4, bf16[8192,1024]{1,0:T(8,128)(2,1)} %all-gather.8.cloned.1.call-done), kind=kOutput, calls=%fused_computation.10 | convolution fusion | flops 17180917760 | bytes 35651584 | tf_op jit(solution)/shard_map/dot_general | solution.py:346
  (149 shorter events, 48.2 us)
Async XLA Ops:
  6.5 228.4 %all-gather.4.cloned.1.call-start = ((), (), s32[]{:S(2)}) async-start(), calls=%async_computation | async-start | bytes 10485760 | tf_op jit(solution)/shard_map/all_gather | solution.py:295
  11.1 242.3 %all-gather.6.cloned.1.call-start = ((), (), s32[]{:S(2)}) async-start(), calls=%async_computation.1 | async-start | bytes 10485760 | tf_op jit(solution)/shard_map/all_gather | solution.py:295
  11.8 2.7 collective-permute-start.9
  13.1 2.6 collective-permute-start.10
  14.3 3.3 collective-permute-start.11
  34.2 787.5 %all-gather.8.cloned.1.call-start = ((), (), s32[]{:S(2)}) async-start(), calls=%async_computation.2 | async-start | bytes 20971520 | tf_op jit(solution)/shard_map/all_gather | solution.py:331
  34.3 93.8 %collective-permute-start.1 = (bf16[1024,1024]{1,0:T(8,128)(2,1)}, bf16[1024,1024]{1,0:T(8,128)(2,1)}, u32[]{:S(2)}, u32[]{:S(2)}) collective-permute-start(bf16[1024,1024]{1,0:T(8,128)(2,1)} %param.6), channel_id=1, source_target_pairs={{0,4},{1,5},{2,6},{3,7},{4,0},{5,1},{6,2},{7,3},{8,12},{9,13},{10,... | collective-permute-start | bytes 6291464 | tf_op jit(solution)/shard_map/ppermute | solution.py:45
  34.5 101.5 %collective-permute-start.4 = (bf16[1024,1024]{1,0:T(8,128)(2,1)}, bf16[1024,1024]{1,0:T(8,128)(2,1)}, u32[]{:S(2)}, u32[]{:S(2)}) collective-permute-start(bf16[1024,1024]{1,0:T(8,128)(2,1)} %param.6), channel_id=1, source_target_pairs={{0,2},{1,3},{2,4},{3,5},{4,6},{5,7},{8,10},{9,11},{10,12},{11,13},... | collective-permute-start | bytes 6291464 | tf_op jit(solution)/shard_map/ppermute | solution.py:46
  128.0 48.8 %collective-permute-start.3 = (bf16[1024,1024]{1,0:T(8,128)(2,1)}, bf16[1024,1024]{1,0:T(8,128)(2,1)S(1)}, u32[]{:S(2)}, u32[]{:S(2)}) collective-permute-start(bf16[1024,1024]{1,0:T(8,128)(2,1)} %collective-permute-done.1), channel_id=1, source_target_pairs={{4,6},{5,7},{2,0},{3,1},{12,14},{13,15},{10,8},{11,9},{20,22},{21,... | collective-permute-start | bytes 6291464 | tf_op jit(solution)/shard_map/ppermute | solution.py:49
  129.3 60.0 %collective-permute-start.7 = (bf16[1024,1024]{1,0:T(8,128)(2,1)}, bf16[1024,1024]{1,0:T(8,128)(2,1)}, u32[]{:S(2)}, u32[]{:S(2)}) collective-permute-start(bf16[1024,1024]{1,0:T(8,128)(2,1)} %param.6), channel_id=1, source_target_pairs={{2,0},{3,1},{4,2},{5,3},{6,4},{7,5},{10,8},{11,9},{12,10},{13,11},... | collective-permute-start | bytes 6291464 | tf_op jit(solution)/shard_map/ppermute | solution.py:47
  134.8 69.7 %collective-permute-start = (bf16[1024,1024]{1,0:T(8,128)(2,1)}, bf16[1024,1024]{1,0:T(8,128)(2,1)}, u32[]{:S(2)}, u32[]{:S(2)}) collective-permute-start(bf16[1024,1024]{1,0:T(8,128)(2,1)} %param.6), channel_id=1, source_target_pairs={{0,1},{1,0},{2,3},{3,2},{4,5},{5,4},{6,7},{7,6},{8,9},{9,8},{10,11... | collective-permute-start | bytes 6291464 | tf_op jit(solution)/shard_map/ppermute | solution.py:43
  135.9 74.7 %collective-permute-start.2 = (bf16[1024,1024]{1,0:T(8,128)(2,1)}, bf16[1024,1024]{1,0:T(8,128)(2,1)}, u32[]{:S(2)}, u32[]{:S(2)}) collective-permute-start(bf16[1024,1024]{1,0:T(8,128)(2,1)} %collective-permute-done.1), channel_id=1, source_target_pairs={{0,1},{1,0},{2,3},{3,2},{4,5},{5,4},{6,7},{7,6},{8,9},{9,8},{10,11... | collective-permute-start | bytes 6291464 | tf_op jit(solution)/shard_map/ppermute | solution.py:43
  135.9 81.7 %collective-permute-start.6 = (bf16[1024,1024]{1,0:T(8,128)(2,1)}, bf16[1024,1024]{1,0:T(8,128)(2,1)}, u32[]{:S(2)}, u32[]{:S(2)}) collective-permute-start(bf16[1024,1024]{1,0:T(8,128)(2,1)} %collective-permute-done.4), channel_id=1, source_target_pairs={{0,1},{1,0},{2,3},{3,2},{4,5},{5,4},{6,7},{7,6},{8,9},{9,8},{10,11... | collective-permute-start | bytes 6291464 | tf_op jit(solution)/shard_map/ppermute | solution.py:43
  176.8 40.8 %collective-permute-start.5 = (bf16[1024,1024]{1,0:T(8,128)(2,1)S(1)}, bf16[1024,1024]{1,0:T(8,128)(2,1)}, u32[]{:S(2)}, u32[]{:S(2)}) collective-permute-start(bf16[1024,1024]{1,0:T(8,128)(2,1)S(1)} %collective-permute-done.3), channel_id=1, source_target_pairs={{0,1},{1,0},{6,7},{7,6},{8,9},{9,8},{14,15},{15,14},{16,17},{17,16... | collective-permute-start | bytes 6291464 | tf_op jit(solution)/shard_map/ppermute | solution.py:52
  189.3 34.5 %collective-permute-start.8 = (bf16[1024,1024]{1,0:T(8,128)(2,1)}, bf16[1024,1024]{1,0:T(8,128)(2,1)}, u32[]{:S(2)}, u32[]{:S(2)}) collective-permute-start(bf16[1024,1024]{1,0:T(8,128)(2,1)} %collective-permute-done.7), channel_id=1, source_target_pairs={{0,1},{1,0},{2,3},{3,2},{4,5},{5,4},{6,7},{7,6},{8,9},{9,8},{10,11... | collective-permute-start | bytes 6291464 | tf_op jit(solution)/shard_map/ppermute | solution.py:43
  250.8 49.5 %collective-permute-start.33 = (bf16[24,128,256]{2,1,0:T(8,128)(2,1)}, bf16[24,128,256]{2,1,0:T(8,128)(2,1)S(1)}, u32[]{:S(2)}, u32[]{:S(2)}) collective-permute-start(bf16[24,128,256]{2,1,0:T(8,128)(2,1)} %get-tuple-element.44), channel_id=1, source_target_pairs={{0,8},{8,0},{16,24},{24,16},{1,9},{9,1},{17,25},{25,17},{2,10},{10... | collective-permute-start | bytes 4718600 | tf_op jit(solution)/shard_map/ppermute | solution.py:27
  252.6 47.7 %collective-permute-start.34 = (bf16[24,128,256]{2,1,0:T(8,128)(2,1)}, bf16[24,128,256]{2,1,0:T(8,128)(2,1)S(1)}, u32[]{:S(2)}, u32[]{:S(2)}) collective-permute-start(bf16[24,128,256]{2,1,0:T(8,128)(2,1)} %get-tuple-element.45), channel_id=1, source_target_pairs={{0,16},{8,24},{16,0},{24,8},{1,17},{9,25},{17,1},{25,9},{2,18},{10... | collective-permute-start | bytes 4718600 | tf_op jit(solution)/shard_map/ppermute | solution.py:27
  268.5 29.7 %collective-permute-start.32 = (bf16[1024,256]{1,0:T(8,128)(2,1)S(1)}, bf16[1024,256]{1,0:T(8,128)(2,1)S(1)}, u32[]{:S(2)}, u32[]{:S(2)}) collective-permute-start(bf16[1024,256]{1,0:T(8,128)(2,1)S(1)} %get-tuple-element.67), channel_id=1, source_target_pairs={{0,8},{8,0},{16,24},{24,16},{1,9},{9,1},{17,25},{25,17},{2,10},{10... | collective-permute-start | bytes 1572872 | tf_op jit(solution)/shard_map/ppermute | solution.py:27
  270.1 29.2 %collective-permute-start.31 = (bf16[1024,256]{1,0:T(8,128)(2,1)S(1)}, bf16[1024,256]{1,0:T(8,128)(2,1)S(1)}, u32[]{:S(2)}, u32[]{:S(2)}) collective-permute-start(bf16[1024,256]{1,0:T(8,128)(2,1)S(1)} %get-tuple-element.68), channel_id=1, source_target_pairs={{0,16},{8,24},{16,0},{24,8},{1,17},{9,25},{17,1},{25,9},{2,18},{10... | collective-permute-start | bytes 1572872 | tf_op jit(solution)/shard_map/ppermute | solution.py:27
  300.3 1.2 copy-start
  300.3 1.7 copy-start.1
  316.9 34.7 %collective-permute-start.14 = (bf16[24,128,256]{2,1,0:T(8,128)(2,1)}, bf16[24,128,256]{2,1,0:T(8,128)(2,1)S(1)}, u32[]{:S(2)}, u32[]{:S(2)}) collective-permute-start(bf16[24,128,256]{2,1,0:T(8,128)(2,1)} %get-tuple-element.31), channel_id=1, source_target_pairs={{0,8},{8,0},{16,24},{24,16},{1,9},{9,1},{17,25},{25,17},{2,10},{10... | collective-permute-start | bytes 4718600 | tf_op jit(solution)/shard_map/ppermute | solution.py:27
  318.1 116.7 %collective-permute-start.15 = (bf16[24,128,256]{2,1,0:T(8,128)(2,1)}, bf16[24,128,256]{2,1,0:T(8,128)(2,1)S(1)}, u32[]{:S(2)}, u32[]{:S(2)}) collective-permute-start(bf16[24,128,256]{2,1,0:T(8,128)(2,1)} %get-tuple-element.32), channel_id=1, source_target_pairs={{0,16},{8,24},{16,0},{24,8},{1,17},{9,25},{17,1},{25,9},{2,18},{10... | collective-permute-start | bytes 4718600 | tf_op jit(solution)/shard_map/ppermute | solution.py:27
  319.2 132.2 %collective-permute-start.16 = (bf16[24,128,256]{2,1,0:T(8,128)(2,1)}, bf16[24,128,256]{2,1,0:T(8,128)(2,1)}, u32[]{:S(2)}, u32[]{:S(2)}) collective-permute-start(bf16[24,128,256]{2,1,0:T(8,128)(2,1)} %get-tuple-element.33), channel_id=1, source_target_pairs={{0,8},{8,0},{16,24},{24,16},{1,9},{9,1},{17,25},{25,17},{2,10},{10... | collective-permute-start | bytes 4718600 | tf_op jit(solution)/shard_map/ppermute | solution.py:27
  320.4 132.1 %collective-permute-start.17 = (bf16[24,128,256]{2,1,0:T(8,128)(2,1)}, bf16[24,128,256]{2,1,0:T(8,128)(2,1)}, u32[]{:S(2)}, u32[]{:S(2)}) collective-permute-start(bf16[24,128,256]{2,1,0:T(8,128)(2,1)} %get-tuple-element.34), channel_id=1, source_target_pairs={{0,16},{8,24},{16,0},{24,8},{1,17},{9,25},{17,1},{25,9},{2,18},{10... | collective-permute-start | bytes 4718600 | tf_op jit(solution)/shard_map/ppermute | solution.py:27
  321.7 107.7 %collective-permute-start.13 = (bf16[1024,256]{1,0:T(8,128)(2,1)S(1)}, bf16[1024,256]{1,0:T(8,128)(2,1)S(1)}, u32[]{:S(2)}, u32[]{:S(2)}) collective-permute-start(bf16[1024,256]{1,0:T(8,128)(2,1)S(1)} %get-tuple-element.69), channel_id=1, source_target_pairs={{0,8},{8,0},{16,24},{24,16},{1,9},{9,1},{17,25},{25,17},{2,10},{10... | collective-permute-start | bytes 1572872 | tf_op jit(solution)/shard_map/ppermute | solution.py:27
  351.6 83.2 %copy-start.2 = (bf16[24,128,256]{2,1,0:T(8,128)(2,1)}, bf16[24,128,256]{2,1,0:T(8,128)(2,1)S(1)}, u32[]{:S(2)}) copy-start(bf16[24,128,256]{2,1,0:T(8,128)(2,1)S(1)} %collective-permute-done.14.refs_7_) | copy-start | bytes 4718596
  351.6 80.2 %collective-permute-start.12 = (bf16[1024,256]{1,0:T(8,128)(2,1)S(1)}, bf16[1024,256]{1,0:T(8,128)(2,1)S(1)}, u32[]{:S(2)}, u32[]{:S(2)}) collective-permute-start(bf16[1024,256]{1,0:T(8,128)(2,1)S(1)} %get-tuple-element.70), channel_id=1, source_target_pairs={{0,16},{8,24},{16,0},{24,8},{1,17},{9,25},{17,1},{25,9},{2,18},{10... | collective-permute-start | bytes 1572872 | tf_op jit(solution)/shard_map/ppermute | solution.py:27
  429.4 92.5 %collective-permute-start.35 = (bf16[24,128,256]{2,1,0:T(8,128)(2,1)}, bf16[24,128,256]{2,1,0:T(8,128)(2,1)}, u32[]{:S(2)}, u32[]{:S(2)}) collective-permute-start(bf16[24,128,256]{2,1,0:T(8,128)(2,1)} %get-tuple-element.48), channel_id=1, source_target_pairs={{0,8},{8,0},{16,24},{24,16},{1,9},{9,1},{17,25},{25,17},{2,10},{10... | collective-permute-start | bytes 4718600 | tf_op jit(solution)/shard_map/ppermute | solution.py:27
  431.7 90.3 %collective-permute-start.36 = (bf16[24,128,256]{2,1,0:T(8,128)(2,1)}, bf16[24,128,256]{2,1,0:T(8,128)(2,1)}, u32[]{:S(2)}, u32[]{:S(2)}) collective-permute-start(bf16[24,128,256]{2,1,0:T(8,128)(2,1)} %get-tuple-element.49), channel_id=1, source_target_pairs={{0,16},{8,24},{16,0},{24,8},{1,17},{9,25},{17,1},{25,9},{2,18},{10... | collective-permute-start | bytes 4718600 | tf_op jit(solution)/shard_map/ppermute | solution.py:27
  434.8 1.1 copy-start.3
  450.8 71.0 %copy-start.7 = (f32[2,64,128]{2,1,0:T(8,128)S(1)}, f32[2,64,128]{2,1,0:T(8,128)}, u32[]{:S(2)}) copy-start(f32[2,64,128]{2,1,0:T(8,128)} %get-tuple-element.50.refs_11_) | copy-start | bytes 196612
  450.8 71.1 %copy-start.8 = (f32[2,64,128]{2,1,0:T(8,128)S(1)}, f32[2,64,128]{2,1,0:T(8,128)}, u32[]{:S(2)}) copy-start(f32[2,64,128]{2,1,0:T(8,128)} %get-tuple-element.51.refs_12_) | copy-start | bytes 196612
  450.8 44.1 %collective-permute-start.18 = (f32[2,64,128]{2,1,0:T(8,128)}, f32[2,64,128]{2,1,0:T(8,128)S(1)}, u32[]{:S(2)}, u32[]{:S(2)}) collective-permute-start(f32[2,64,128]{2,1,0:T(8,128)} %get-tuple-element.35.refs_11_), channel_id=1, source_target_pairs={{0,16},{8,24},{16,0},{24,8},{1,17},{9,25},{17,1},{25,9},{2,18},{10... | collective-permute-start | bytes 196616 | tf_op jit(solution)/shard_map/ppermute | solution.py:27
  451.5 43.5 %collective-permute-start.19 = (f32[2,64,128]{2,1,0:T(8,128)}, f32[2,64,128]{2,1,0:T(8,128)S(1)}, u32[]{:S(2)}, u32[]{:S(2)}) collective-permute-start(f32[2,64,128]{2,1,0:T(8,128)} %get-tuple-element.36.refs_12_), channel_id=1, source_target_pairs={{0,8},{8,0},{16,24},{24,16},{1,9},{9,1},{17,25},{25,17},{2,10},{10... | collective-permute-start | bytes 196616 | tf_op jit(solution)/shard_map/ppermute | solution.py:27
  494.9 0.6 copy-start.10
  518.6 73.8 %copy-start.6 = (f32[1024,256]{1,0:T(8,128)S(1)}, f32[1024,256]{1,0:T(8,128)}, u32[]{:S(2)}) copy-start(f32[1024,256]{1,0:T(8,128)} %get-tuple-element.37) | copy-start | bytes 3145732
  518.7 75.1 %copy-start.5 = (f32[1024,256]{1,0:T(8,128)S(1)}, f32[1024,256]{1,0:T(8,128)}, u32[]{:S(2)}) copy-start(f32[1024,256]{1,0:T(8,128)} %get-tuple-element.39) | copy-start | bytes 3145732
  518.7 73.8 %collective-permute-start.20 = (f32[1024,256]{1,0:T(8,128)}, f32[1024,256]{1,0:T(8,128)}, u32[]{:S(2)}, u32[]{:S(2)}) collective-permute-start(f32[1024,256]{1,0:T(8,128)} %get-tuple-element.38), channel_id=1, source_target_pairs={{0,16},{8,24},{16,0},{24,8},{1,17},{9,25},{17,1},{25,9},{2,18},{10... | collective-permute-start | bytes 3145736 | tf_op jit(solution)/shard_map/ppermute | solution.py:27
  520.4 73.4 %collective-permute-start.21 = (f32[1024,256]{1,0:T(8,128)}, f32[1024,256]{1,0:T(8,128)}, u32[]{:S(2)}, u32[]{:S(2)}) collective-permute-start(f32[1024,256]{1,0:T(8,128)} %get-tuple-element.40), channel_id=1, source_target_pairs={{0,8},{8,0},{16,24},{24,16},{1,9},{9,1},{17,25},{25,17},{2,10},{10... | collective-permute-start | bytes 3145736 | tf_op jit(solution)/shard_map/ppermute | solution.py:27
  521.9 45.3 %collective-permute-start.37 = (f32[2,64,128]{2,1,0:T(8,128)S(1)}, f32[2,64,128]{2,1,0:T(8,128)S(1)}, u32[]{:S(2)}, u32[]{:S(2)}) collective-permute-start(f32[2,64,128]{2,1,0:T(8,128)S(1)} %copy-done.7), channel_id=1, source_target_pairs={{0,16},{8,24},{16,0},{24,8},{1,17},{9,25},{17,1},{25,9},{2,18},{10... | collective-permute-start | bytes 196616 | tf_op jit(solution)/shard_map/ppermute | solution.py:27
  521.9 46.5 %collective-permute-start.38 = (f32[2,64,128]{2,1,0:T(8,128)S(1)}, f32[2,64,128]{2,1,0:T(8,128)S(1)}, u32[]{:S(2)}, u32[]{:S(2)}) collective-permute-start(f32[2,64,128]{2,1,0:T(8,128)S(1)} %copy-done.8), channel_id=1, source_target_pairs={{0,8},{8,0},{16,24},{24,16},{1,9},{9,1},{17,25},{25,17},{2,10},{10... | collective-permute-start | bytes 196616 | tf_op jit(solution)/shard_map/ppermute | solution.py:27
  567.2 1.3 copy-start.9
  591.6 66.7 %collective-permute-start.39 = (f32[1024,256]{1,0:T(8,128)}, f32[1024,256]{1,0:T(8,128)S(1)}, u32[]{:S(2)}, u32[]{:S(2)}) collective-permute-start(f32[1024,256]{1,0:T(8,128)} %get-tuple-element.53), channel_id=1, source_target_pairs={{0,16},{8,24},{16,0},{24,8},{1,17},{9,25},{17,1},{25,9},{2,18},{10... | collective-permute-start | bytes 3145736 | tf_op jit(solution)/shard_map/ppermute | solution.py:27
  595.2 103.0 %collective-permute-start.23 = (bf16[1024,512]{1,0:T(8,128)(2,1)S(1)}, bf16[1024,512]{1,0:T(8,128)(2,1)}, u32[]{:S(2)}, u32[]{:S(2)}) collective-permute-start(bf16[1024,512]{1,0:T(8,128)(2,1)S(1)} %pad_maximum_fusion.2), channel_id=1, source_target_pairs={{0,4},{1,5},{2,6},{3,7},{4,0},{5,1},{6,2},{7,3},{8,12},{9,13},{10,... | collective-permute-start | bytes 3145736 | tf_op jit(solution)/shard_map/ppermute | solution.py:45
  652.4 48.4 %collective-permute-start.40 = (f32[1024,256]{1,0:T(8,128)}, f32[1024,256]{1,0:T(8,128)S(1)}, u32[]{:S(2)}, u32[]{:S(2)}) collective-permute-start(f32[1024,256]{1,0:T(8,128)} %get-tuple-element.55), channel_id=1, source_target_pairs={{0,8},{8,0},{16,24},{24,16},{1,9},{9,1},{17,25},{25,17},{2,10},{10... | collective-permute-start | bytes 3145736 | tf_op jit(solution)/shard_map/ppermute | solution.py:27
  653.8 50.1 %collective-permute-start.26 = (bf16[1024,512]{1,0:T(8,128)(2,1)S(1)}, bf16[1024,512]{1,0:T(8,128)(2,1)}, u32[]{:S(2)}, u32[]{:S(2)}) collective-permute-start(bf16[1024,512]{1,0:T(8,128)(2,1)S(1)} %pad_maximum_fusion.2), channel_id=1, source_target_pairs={{0,2},{1,3},{2,4},{3,5},{4,6},{5,7},{8,10},{9,11},{10,12},{11,13},... | collective-permute-start | bytes 3145736 | tf_op jit(solution)/shard_map/ppermute | solution.py:46
  655.1 48.9 %collective-permute-start.22 = (bf16[1024,512]{1,0:T(8,128)(2,1)S(1)}, bf16[1024,512]{1,0:T(8,128)(2,1)S(1)}, u32[]{:S(2)}, u32[]{:S(2)}) collective-permute-start(bf16[1024,512]{1,0:T(8,128)(2,1)S(1)} %pad_maximum_fusion.2), channel_id=1, source_target_pairs={{0,1},{1,0},{2,3},{3,2},{4,5},{5,4},{6,7},{7,6},{8,9},{9,8},{10,11... | collective-permute-start | bytes 3145736 | tf_op jit(solution)/shard_map/ppermute | solution.py:43
  658.3 62.5 %collective-permute-start.29 = (bf16[1024,512]{1,0:T(8,128)(2,1)S(1)}, bf16[1024,512]{1,0:T(8,128)(2,1)}, u32[]{:S(2)}, u32[]{:S(2)}) collective-permute-start(bf16[1024,512]{1,0:T(8,128)(2,1)S(1)} %pad_maximum_fusion.2), channel_id=1, source_target_pairs={{2,0},{3,1},{4,2},{5,3},{6,4},{7,5},{10,8},{11,9},{12,10},{13,11},... | collective-permute-start | bytes 3145736 | tf_op jit(solution)/shard_map/ppermute | solution.py:47
  698.2 28.6 %collective-permute-start.25 = (bf16[1024,512]{1,0:T(8,128)(2,1)}, bf16[1024,512]{1,0:T(8,128)(2,1)S(1)}, u32[]{:S(2)}, u32[]{:S(2)}) collective-permute-start(bf16[1024,512]{1,0:T(8,128)(2,1)} %collective-permute-done.23), channel_id=1, source_target_pairs={{4,6},{5,7},{2,0},{3,1},{12,14},{13,15},{10,8},{11,9},{20,22},{21,... | collective-permute-start | bytes 3145736 | tf_op jit(solution)/shard_map/ppermute | solution.py:49
  702.2 34.6 %collective-permute-start.24 = (bf16[1024,512]{1,0:T(8,128)(2,1)}, bf16[1024,512]{1,0:T(8,128)(2,1)}, u32[]{:S(2)}, u32[]{:S(2)}) collective-permute-start(bf16[1024,512]{1,0:T(8,128)(2,1)} %collective-permute-done.23), channel_id=1, source_target_pairs={{0,1},{1,0},{2,3},{3,2},{4,5},{5,4},{6,7},{7,6},{8,9},{9,8},{10,11... | collective-permute-start | bytes 3145736 | tf_op jit(solution)/shard_map/ppermute | solution.py:43
  703.9 34.2 %collective-permute-start.28 = (bf16[1024,512]{1,0:T(8,128)(2,1)}, bf16[1024,512]{1,0:T(8,128)(2,1)}, u32[]{:S(2)}, u32[]{:S(2)}) collective-permute-start(bf16[1024,512]{1,0:T(8,128)(2,1)} %collective-permute-done.26), channel_id=1, source_target_pairs={{0,1},{1,0},{2,3},{3,2},{4,5},{5,4},{6,7},{7,6},{8,9},{9,8},{10,11... | collective-permute-start | bytes 3145736 | tf_op jit(solution)/shard_map/ppermute | solution.py:43
  704.0 22.7 %copy-start.4 = (bf16[1024,512]{1,0:T(8,128)(2,1)}, bf16[1024,512]{1,0:T(8,128)(2,1)S(1)}, u32[]{:S(2)}) copy-start(bf16[1024,512]{1,0:T(8,128)(2,1)S(1)} %collective-permute-done.22) | copy-start | bytes 3145732
  704.0 62.9 %collective-permute-start.42 = (bf16[1024,512]{1,0:T(8,128)(2,1)S(1)}, bf16[1024,512]{1,0:T(8,128)(2,1)}, u32[]{:S(2)}, u32[]{:S(2)}) collective-permute-start(bf16[1024,512]{1,0:T(8,128)(2,1)S(1)} %pad_maximum_fusion.5), channel_id=1, source_target_pairs={{0,4},{1,5},{2,6},{3,7},{4,0},{5,1},{6,2},{7,3},{8,12},{9,13},{10,... | collective-permute-start | bytes 3145736 | tf_op jit(solution)/shard_map/ppermute | solution.py:45
  720.8 52.3 %collective-permute-start.30 = (bf16[1024,512]{1,0:T(8,128)(2,1)}, bf16[1024,512]{1,0:T(8,128)(2,1)}, u32[]{:S(2)}, u32[]{:S(2)}) collective-permute-start(bf16[1024,512]{1,0:T(8,128)(2,1)} %collective-permute-done.29), channel_id=1, source_target_pairs={{0,1},{1,0},{2,3},{3,2},{4,5},{5,4},{6,7},{7,6},{8,9},{9,8},{10,11... | collective-permute-start | bytes 3145736 | tf_op jit(solution)/shard_map/ppermute | solution.py:43
  726.7 47.1 %collective-permute-start.27 = (bf16[1024,512]{1,0:T(8,128)(2,1)S(1)}, bf16[1024,512]{1,0:T(8,128)(2,1)}, u32[]{:S(2)}, u32[]{:S(2)}) collective-permute-start(bf16[1024,512]{1,0:T(8,128)(2,1)S(1)} %collective-permute-done.25), channel_id=1, source_target_pairs={{0,1},{1,0},{6,7},{7,6},{8,9},{9,8},{14,15},{15,14},{16,17},{17,16... | collective-permute-start | bytes 3145736 | tf_op jit(solution)/shard_map/ppermute | solution.py:52
  736.8 45.8 %collective-permute-start.45 = (bf16[1024,512]{1,0:T(8,128)(2,1)S(1)}, bf16[1024,512]{1,0:T(8,128)(2,1)S(1)}, u32[]{:S(2)}, u32[]{:S(2)}) collective-permute-start(bf16[1024,512]{1,0:T(8,128)(2,1)S(1)} %pad_maximum_fusion.5), channel_id=1, source_target_pairs={{0,2},{1,3},{2,4},{3,5},{4,6},{5,7},{8,10},{9,11},{10,12},{11,13},... | collective-permute-start | bytes 3145736 | tf_op jit(solution)/shard_map/ppermute | solution.py:46
  738.1 45.9 %collective-permute-start.48 = (bf16[1024,512]{1,0:T(8,128)(2,1)S(1)}, bf16[1024,512]{1,0:T(8,128)(2,1)S(1)}, u32[]{:S(2)}, u32[]{:S(2)}) collective-permute-start(bf16[1024,512]{1,0:T(8,128)(2,1)S(1)} %pad_maximum_fusion.5), channel_id=1, source_target_pairs={{2,0},{3,1},{4,2},{5,3},{6,4},{7,5},{10,8},{11,9},{12,10},{13,11},... | collective-permute-start | bytes 3145736 | tf_op jit(solution)/shard_map/ppermute | solution.py:47
  766.9 38.1 %collective-permute-start.44 = (bf16[1024,512]{1,0:T(8,128)(2,1)}, bf16[1024,512]{1,0:T(8,128)(2,1)S(1)}, u32[]{:S(2)}, u32[]{:S(2)}) collective-permute-start(bf16[1024,512]{1,0:T(8,128)(2,1)} %collective-permute-done.42), channel_id=1, source_target_pairs={{4,6},{5,7},{2,0},{3,1},{12,14},{13,15},{10,8},{11,9},{20,22},{21,... | collective-permute-start | bytes 3145736 | tf_op jit(solution)/shard_map/ppermute | solution.py:49
  773.1 38.7 %collective-permute-start.41 = (bf16[1024,512]{1,0:T(8,128)(2,1)S(1)}, bf16[1024,512]{1,0:T(8,128)(2,1)S(1)}, u32[]{:S(2)}, u32[]{:S(2)}) collective-permute-start(bf16[1024,512]{1,0:T(8,128)(2,1)S(1)} %pad_maximum_fusion.5), channel_id=1, source_target_pairs={{0,1},{1,0},{2,3},{3,2},{4,5},{5,4},{6,7},{7,6},{8,9},{9,8},{10,11... | collective-permute-start | bytes 3145736 | tf_op jit(solution)/shard_map/ppermute | solution.py:43
  773.9 41.3 %collective-permute-start.43 = (bf16[1024,512]{1,0:T(8,128)(2,1)}, bf16[1024,512]{1,0:T(8,128)(2,1)S(1)}, u32[]{:S(2)}, u32[]{:S(2)}) collective-permute-start(bf16[1024,512]{1,0:T(8,128)(2,1)} %collective-permute-done.42), channel_id=1, source_target_pairs={{0,1},{1,0},{2,3},{3,2},{4,5},{5,4},{6,7},{7,6},{8,9},{9,8},{10,11... | collective-permute-start | bytes 3145736 | tf_op jit(solution)/shard_map/ppermute | solution.py:43
  782.6 35.0 %collective-permute-start.47 = (bf16[1024,512]{1,0:T(8,128)(2,1)S(1)}, bf16[1024,512]{1,0:T(8,128)(2,1)S(1)}, u32[]{:S(2)}, u32[]{:S(2)}) collective-permute-start(bf16[1024,512]{1,0:T(8,128)(2,1)S(1)} %collective-permute-done.45), channel_id=1, source_target_pairs={{0,1},{1,0},{2,3},{3,2},{4,5},{5,4},{6,7},{7,6},{8,9},{9,8},{10,11... | collective-permute-start | bytes 3145736 | tf_op jit(solution)/shard_map/ppermute | solution.py:43
  784.0 36.3 %collective-permute-start.49 = (bf16[1024,512]{1,0:T(8,128)(2,1)S(1)}, bf16[1024,512]{1,0:T(8,128)(2,1)S(1)}, u32[]{:S(2)}, u32[]{:S(2)}) collective-permute-start(bf16[1024,512]{1,0:T(8,128)(2,1)S(1)} %collective-permute-done.48), channel_id=1, source_target_pairs={{0,1},{1,0},{2,3},{3,2},{4,5},{5,4},{6,7},{7,6},{8,9},{9,8},{10,11... | collective-permute-start | bytes 3145736 | tf_op jit(solution)/shard_map/ppermute | solution.py:43
  805.1 12.6 %collective-permute-start.46 = (bf16[1024,512]{1,0:T(8,128)(2,1)S(1)}, bf16[1024,512]{1,0:T(8,128)(2,1)S(1)}, u32[]{:S(2)}, u32[]{:S(2)}) collective-permute-start(bf16[1024,512]{1,0:T(8,128)(2,1)S(1)} %collective-permute-done.44), channel_id=1, source_target_pairs={{0,1},{1,0},{6,7},{7,6},{8,9},{9,8},{14,15},{15,14},{16,17},{17,16... | collective-permute-start | bytes 3145736 | tf_op jit(solution)/shard_map/ppermute | solution.py:52
  (2 other events, 1.3 us)
Sparse Core Ops, SparseCore 0:
  11.2 88.2 all-gather.3
  101.4 87.4 all-gather.5
  317.0 276.6 all-gather.7

commit v7 on v6

--- a/solution.py
+++ b/solution.py
@@ -50,16 +50,15 @@
     there2 = swap(back2)
     there1, there3 = swap(back1), swap(back3)
     ends_there = lax.ppermute(ends, "fsdp", [(0, 1), (1, 0), (6, 7), (7, 6)])
-    found = []
-    for step, (here, there) in enumerate((
-        (piece, own_there),
-        (back2, there2),
-        (jnp.where(chip == 0, ends, back1), jnp.where(chip == 0, ends_there, there1)),
-        (jnp.where(chip == 3, ends, back3), jnp.where(chip == 3, ends_there, there3)),
-    )):
-        owner = (chip + 4 - (0, 2, 1, 3)[step]) % 4
-        found.append((owner * 2 + core, here))
-        found.append((owner * 2 + 1 - core, there))
+    found = [(chip * 2 + core, piece), (chip * 2 + 1 - core, own_there)]
+    for step, value, side in (
+        (2, back2, core), (2, there2, 1 - core), (1, back1, core), (3, back3, core), (1, there1, 1 - core), (3, there3, 1 - core)
+    ):
+        found.append(((chip + 4 - step) % 4 * 2 + side, value))
+    at_end = (chip == 0) | (chip == 3)
+    owner = jnp.where(at_end, 3 - chip, chip)
+    found.append((owner * 2 + core, jnp.where(at_end, ends, piece)))
+    found.append((owner * 2 + 1 - core, jnp.where(at_end, ends_there, own_there)))
     return found
 
 
@@ -204,7 +203,7 @@
     slots = received[0].shape[0]
     per_step = 8 if spans % 8 == 0 else spans
     steps = spans // per_step
-    together = 2 if per_step % 2 == 0 and not stats else 1
+    together = 2 if per_step % 2 == 0 else 1
     step_rows = per_step * span
 
     in_specs = [pl.BlockSpec((step_rows, part), lambda c, i, *t: (c * steps + i, 0))] * AXES

time: 864 us -> 834 us (0.965); the launches traced: 851 us -> 830 us
  starting transfers between devices: 140 us -> 79.4 us
  waiting for transfers between devices: 447 us -> 485 us
  local copies, waits for them, and re-layouts: 43.8 us -> 68.8 us
  other arithmetic: 48.4 us -> 33.3 us
    ppermute x3, starting transfers between devices: 74.2 us -> 19.4 us  [pieces_over_fsdp(): lax.ppermute(piece, 'fsdp', chip_pairs([(0, 2), (1, 3), (2, 0), (3, 1)]))]
    ppermute x23, waiting for transfers between devices: 224 us -> 264 us  [over_dp(): lax.ppermute(value, 'dp', [(i, i ^ bit) for i in range(lax.axis_size('dp'...]
    ppermute x3, waiting for transfers between devices: 152 us -> 129 us  [pieces_over_fsdp(): lax.ppermute(piece, 'fsdp', chip_pairs([(0, 2), (1, 3), (2, 0), (3, 1)]))]
    ppermute x3, waiting for transfers between devices: 67 us -> 82.4 us  [pieces_over_fsdp(): ends = lax.ppermute(back2, 'fsdp', chip_pairs([(2, 3), (1, 0)]))]
    dynamic_update_slice x8 -> x16, local copies, waits for them, and re-layouts: 13.7 us -> 27.3 us  [work(): attended = lax.dynamic_update_slice(attended, piece, (0, start))]
    dynamic_update_slice x4 -> x8, local copies, waits for them, and re-layouts: 12.4 us -> 23.3 us  [work(): gathered = lax.dynamic_update_slice(gathered, piece, (0, owner * width))]
  transfers between devices with their start and end apart: 53 -> 53, of which waited for: 15 -> 15; matrix products, arithmetic and copies ran while one was open for 13% -> 15% of each run, Pallas kernels for 10% -> 10%
where the time goes in v7:
time: 834 us; the launch traced here: 830 us
  waiting for transfers between devices  485 us (58%)
  Pallas kernels  96.1 us (12%)
  starting transfers between devices  79.4 us (10%)
  local copies, waits for them, and re-layouts  68.8 us (8%)
  matrix products  54.3 us (7%)
  other arithmetic  33.3 us (4%)
  between operations  13.7 us (2%)
    ppermute x23, waiting for transfers between devices, over_dp(): lax.ppermute(value, 'dp', [(i, i ^ bit) for i in range(lax.axis_size('dp'...  264 us
    ppermute x3, waiting for transfers between devices, pieces_over_fsdp(): lax.ppermute(piece, 'fsdp', chip_pairs([(0, 2), (1, 3), (2, 0), (3, 1)]))  129 us
    ppermute x3, waiting for transfers between devices, pieces_over_fsdp(): ends = lax.ppermute(back2, 'fsdp', chip_pairs([(2, 3), (1, 0)]))  82.4 us
    pallas_call x4, Pallas kernels, span_call(): pl.pallas_call(functools.partial(kernel, spans, span, together), grid_spe...  66.5 us
    dot_general x2, matrix products, work(): jnp.dot(normed, columns[step], preferred_element_type=jnp.float32)  31.1 us
    pallas_call x2, Pallas kernels, pick_blocks(): pl.pallas_call(pick_kernel, grid_spec=pltpu.PrefetchScalarGridSpec(num_sc...  29.6 us
    dynamic_update_slice x16, local copies, waits for them, and re-layouts, work(): attended = lax.dynamic_update_slice(attended, piece, (0, start))  27.3 us
    ppermute x23, starting transfers between devices, over_dp(): lax.ppermute(value, 'dp', [(i, i ^ bit) for i in range(lax.axis_size('dp'...  25.4 us
  transfers between devices with their start and end apart: 53, of which 15 were waited for; matrix products, arithmetic and copies ran while one was open for 15% of the time, Pallas kernels for 10%

profile of v7, /device:TPU:25, one launch (start us, length us, event | category | flops | bytes accessed | tf_op | source)
XLA Modules:
  0.0 830.3 jit_solution(9061180414672668333)
XLA Ops:
  6.5 4.5 fusion.21
  15.7 1.9 collective-permute-done.11
  19.4 15.1 %pick.2 = (bf16[24,128,256]{2,1,0:T(8,128)(2,1)}, bf16[24,128,256]{2,1,0:T(8,128)(2,1)}, bf16[24,128,256]{2,1,0:T(8,128)(2,1)}, bf16[24,128,256]{2,1,0:T(8,128)(2,1)}) custom-call(s32[24]{0:T(128)} %get-tuple-element.76.first_ref, s32[24]{0:T(128)} %get-tuple-element.75.second_ref, bf16[32,2,128,1024]{3,2,1,0:T(8,128)(2,1)} %bitcast.28, ...), custom_call_target="tpu_custom_call" | custom-call | bytes 12582912 | tf_op jit(solution)/shard_map/pick/pallas_call | solution.py:74
  36.0 5.4 collective-permute-start.4
  41.4 86.7 %collective-permute-done.1 = bf16[1024,1024]{1,0:T(8,128)(2,1)} collective-permute-done((bf16[1024,1024]{1,0:T(8,128)(2,1)S(1)}, bf16[1024,1024]{1,0:T(8,128)(2,1)}, u32[]{:S(2)}, u32[]{:S(2)}) %collective-permute-start.1) | collective-permute-done | bytes 2097184 | tf_op jit(solution)/shard_map/ppermute | solution.py:45
  130.6 46.3 %collective-permute-done.7 = bf16[1024,1024]{1,0:T(8,128)(2,1)} collective-permute-done((bf16[1024,1024]{1,0:T(8,128)(2,1)}, bf16[1024,1024]{1,0:T(8,128)(2,1)}, u32[]{:S(2)}, u32[]{:S(2)}) %collective-permute-start.7) | collective-permute-done | bytes 2097184 | tf_op jit(solution)/shard_map/ppermute | solution.py:49
  176.9 3.3 collective-permute-start.8
  180.4 6.0 broadcast_in_dim.36
  186.4 1.6 constant_dynamic-update-slice_fusion.23
  188.0 14.5 %pick.3 = (bf16[24,128,256]{2,1,0:T(8,128)(2,1)}, bf16[24,128,256]{2,1,0:T(8,128)(2,1)}, bf16[24,128,256]{2,1,0:T(8,128)(2,1)}, bf16[24,128,256]{2,1,0:T(8,128)(2,1)}) custom-call(s32[24]{0:T(128)} %get-tuple-element.76.first_ref, s32[24]{0:T(128)} %get-tuple-element.75.second_ref, bf16[32,2,128,1024]{3,2,1,0:T(8,128)(2,1)} %bitcast.30, ...), custom_call_target="tpu_custom_call" | custom-call | bytes 12582912 | tf_op jit(solution)/shard_map/pick/pallas_call | solution.py:74
  203.0 3.1 constant_dynamic-update-slice_fusion.22
  206.2 3.1 constant_dynamic-update-slice_fusion.21
  209.3 3.1 constant_dynamic-update-slice_fusion.20
  212.3 3.1 constant_dynamic-update-slice_fusion.19
  215.4 3.1 constant_dynamic-update-slice_fusion.18
  218.5 3.1 constant_dynamic-update-slice_fusion.17
  221.6 3.2 constant_dynamic-update-slice_fusion.16
  224.7 3.9 select_dynamic-update-slice_fusion.1
  228.6 3.9 select_dynamic-update-slice_fusion
  232.5 7.2 fusion
  239.8 15.9 %fusion.6 = bf16[1024,512]{1,0:T(8,128)(2,1)} fusion(bf16[8192,512]{1,0:T(8,128)(2,1)} %all-gather.4.cloned.1.call-done, bf16[1024,8192]{1,0:T(8,128)(2,1)} %select_dynamic-update-slice_fusion, f32[1024]{0:T(1024)S(1)} %add_rsqrt_fusion), kind=kOutput, calls=%fused_computation.9 | convolution fusion | flops 8615624704 | bytes 26218496 | tf_op jit(solution)/shard_map/dot_general | solution.py:312
  255.6 1.8 collective-permute-start.33
  258.3 15.2 %fusion.9 = bf16[1024,512]{1,0:T(8,128)(2,1)S(1)} fusion(bf16[8192,512]{1,0:T(8,128)(2,1)} %all-gather.6.cloned.1.call-done, bf16[1024,8192]{1,0:T(8,128)(2,1)} %select_dynamic-update-slice_fusion, f32[1024]{0:T(1024)S(1)} %add_rsqrt_fusion), kind=kOutput, calls=%fused_computation.10 | convolution fusion | flops 8615624704 | bytes 26218496 | tf_op jit(solution)/shard_map/dot_general | solution.py:312
  273.6 1.5 collective-permute-start.32
  276.5 27.1 %collective-permute-done.32 = bf16[1024,256]{1,0:T(8,128)(2,1)S(1)} collective-permute-done((bf16[1024,256]{1,0:T(8,128)(2,1)S(1)}, bf16[1024,256]{1,0:T(8,128)(2,1)S(1)}, u32[]{:S(2)}, u32[]{:S(2)}) %collective-permute-start.32) | collective-permute-done | bytes 524320 | tf_op jit(solution)/shard_map/ppermute | solution.py:27
  307.3 14.9 %stats.3 = (f32[2,64,128]{2,1,0:T(8,128)}, f32[2,64,128]{2,1,0:T(8,128)}) custom-call(s32[32]{0:T(128)} %get-tuple-element.78.refs_0_, s32[32]{0:T(128)} %get-tuple-element.79.refs_1_, s32[32]{0:T(128)} %get-tuple-element.77.refs_2_, s32[32]{0:T(128)} %pad_add_fusion.5.refs_3_, bf16[2048,256]{1,0:T(8,128)(2,1)} %pad_maximum_fusion.3.refs_4_, ...), custom_call_target="tpu_custom_call" | custom-call | flops 1073741824 | bytes 7340032 | tf_op jit(solution)/shard_map/stats/pallas_call | solution.py:221
  327.8 49.2 %collective-permute-done.14.refs_7_ = bf16[24,128,256]{2,1,0:T(8,128)(2,1)S(1)} collective-permute-done((bf16[24,128,256]{2,1,0:T(8,128)(2,1)}, bf16[24,128,256]{2,1,0:T(8,128)(2,1)S(1)}, u32[]{:S(2)}, u32[]{:S(2)}) %collective-permute-start.14) | collective-permute-done | bytes 1572896 | tf_op jit(solution)/shard_map/ppermute | solution.py:27
  377.0 3.0 collective-permute-start.12
  380.0 78.7 %collective-permute-done.13 = bf16[1024,256]{1,0:T(8,128)(2,1)S(1)} collective-permute-done((bf16[1024,256]{1,0:T(8,128)(2,1)S(1)}, bf16[1024,256]{1,0:T(8,128)(2,1)S(1)}, u32[]{:S(2)}, u32[]{:S(2)}) %collective-permute-start.13) | collective-permute-done | bytes 524320 | tf_op jit(solution)/shard_map/ppermute | solution.py:27
  458.7 2.3 collective-permute-start.35
  461.0 1.4 collective-permute-start.36
  465.7 14.9 %stats.2 = (f32[2,64,128]{2,1,0:T(8,128)}, f32[2,64,128]{2,1,0:T(8,128)}) custom-call(s32[32]{0:T(128)} %get-tuple-element.78.refs_0_, s32[32]{0:T(128)} %get-tuple-element.79.refs_1_, s32[32]{0:T(128)} %get-tuple-element.77.refs_2_, s32[32]{0:T(128)} %pad_add_fusion.5.refs_3_, bf16[2048,256]{1,0:T(8,128)(2,1)} %pad_maximum_fusion.refs_4_, ...), custom_call_target="tpu_custom_call" | custom-call | flops 1073741824 | bytes 7340032 | tf_op jit(solution)/shard_map/stats/pallas_call | solution.py:221
  480.7 1.5 collective-permute-start.19
  482.3 50.5 %collective-permute-done.18.refs_13_ = f32[2,64,128]{2,1,0:T(8,128)S(1)} collective-permute-done((f32[2,64,128]{2,1,0:T(8,128)}, f32[2,64,128]{2,1,0:T(8,128)S(1)}, u32[]{:S(2)}, u32[]{:S(2)}) %collective-permute-start.18) | collective-permute-done | bytes 65568 | tf_op jit(solution)/shard_map/ppermute | solution.py:27
  534.0 18.3 %mix.2 = (f32[1024,256]{1,0:T(8,128)}, f32[1024,256]{1,0:T(8,128)}, f32[1024,256]{1,0:T(8,128)}, f32[1024,256]{1,0:T(8,128)}) custom-call(s32[32]{0:T(128)} %get-tuple-element.78.refs_0_, s32[32]{0:T(128)} %get-tuple-element.79.refs_1_, s32[32]{0:T(128)} %get-tuple-element.77.refs_2_, s32[32]{0:T(128)} %pad_add_fusion.5.refs_3_, ...), custom_call_target="tpu_custom_call" | custom-call | flops 2147483648 | bytes 14680064 | tf_op jit(solution)/shard_map/mix/pallas_call | solution.py:221
  552.3 1.7 collective-permute-start.20
  554.0 1.5 collective-permute-start.21
  555.7 41.1 %collective-permute-done.37.refs_13_ = f32[2,64,128]{2,1,0:T(8,128)S(1)} collective-permute-done((f32[2,64,128]{2,1,0:T(8,128)S(1)}, f32[2,64,128]{2,1,0:T(8,128)S(1)}, u32[]{:S(2)}, u32[]{:S(2)}) %collective-permute-start.37) | collective-permute-done | bytes 65568 | tf_op jit(solution)/shard_map/ppermute | solution.py:27
  598.1 18.4 %mix.3 = (f32[1024,256]{1,0:T(8,128)}, f32[1024,256]{1,0:T(8,128)}, f32[1024,256]{1,0:T(8,128)}, f32[1024,256]{1,0:T(8,128)}) custom-call(s32[32]{0:T(128)} %get-tuple-element.78.refs_0_, s32[32]{0:T(128)} %get-tuple-element.79.refs_1_, s32[32]{0:T(128)} %get-tuple-element.77.refs_2_, s32[32]{0:T(128)} %pad_add_fusion.5.refs_3_, ...), custom_call_target="tpu_custom_call" | custom-call | flops 2147483648 | bytes 14680064 | tf_op jit(solution)/shard_map/mix/pallas_call | solution.py:221
  619.3 1.4 collective-permute-start.40
  622.0 3.0 collective-permute-start.22
  625.0 14.1 %collective-permute-done.39 = f32[1024,256]{1,0:T(8,128)S(1)} collective-permute-done((f32[1024,256]{1,0:T(8,128)}, f32[1024,256]{1,0:T(8,128)S(1)}, u32[]{:S(2)}, u32[]{:S(2)}) %collective-permute-start.39) | collective-permute-done | bytes 1048608 | tf_op jit(solution)/shard_map/ppermute | solution.py:27
  639.1 2.3 collective-permute-start.26
  641.4 26.1 %collective-permute-done.23 = bf16[1024,512]{1,0:T(8,128)(2,1)} collective-permute-done((bf16[1024,512]{1,0:T(8,128)(2,1)S(1)}, bf16[1024,512]{1,0:T(8,128)(2,1)}, u32[]{:S(2)}, u32[]{:S(2)}) %collective-permute-start.23) | collective-permute-done | bytes 1048608 | tf_op jit(solution)/shard_map/ppermute | solution.py:45
  668.1 1.4 add_convert_fusion.1
  672.7 19.2 %collective-permute-start.42 = (bf16[1024,512]{1,0:T(8,128)(2,1)S(1)}, bf16[1024,512]{1,0:T(8,128)(2,1)}, u32[]{:S(2)}, u32[]{:S(2)}) collective-permute-start(bf16[1024,512]{1,0:T(8,128)(2,1)S(1)} %pad_maximum_fusion.5), channel_id=1, source_target_pairs={{0,4},{1,5},{2,6},{3,7},{4,0},{5,1},{6,2},{7,3},{8,12},{9,13},{10,... | collective-permute-start | bytes 3145736 | tf_op jit(solution)/shard_map/ppermute | solution.py:45
  695.8 3.9 collective-permute-start.45
  699.7 19.6 %collective-permute-done.29 = bf16[1024,512]{1,0:T(8,128)(2,1)} collective-permute-done((bf16[1024,512]{1,0:T(8,128)(2,1)}, bf16[1024,512]{1,0:T(8,128)(2,1)}, u32[]{:S(2)}, u32[]{:S(2)}) %collective-permute-start.29) | collective-permute-done | bytes 1048608 | tf_op jit(solution)/shard_map/ppermute | solution.py:49
  719.3 2.3 collective-permute-start.30
  721.7 16.4 %collective-permute-done.42 = bf16[1024,512]{1,0:T(8,128)(2,1)} collective-permute-done((bf16[1024,512]{1,0:T(8,128)(2,1)S(1)}, bf16[1024,512]{1,0:T(8,128)(2,1)}, u32[]{:S(2)}, u32[]{:S(2)}) %collective-permute-start.42) | collective-permute-done | bytes 1048608 | tf_op jit(solution)/shard_map/ppermute | solution.py:45
  739.4 2.3 constant_dynamic-update-slice_fusion.13
  741.7 2.3 constant_dynamic-update-slice_fusion.12
  744.0 2.3 constant_dynamic-update-slice_fusion.11
  747.0 2.3 constant_dynamic-update-slice_fusion.10
  749.3 2.3 constant_dynamic-update-slice_fusion.9
  751.6 9.1 %collective-permute-done.44 = bf16[1024,512]{1,0:T(8,128)(2,1)} collective-permute-done((bf16[1024,512]{1,0:T(8,128)(2,1)S(1)}, bf16[1024,512]{1,0:T(8,128)(2,1)}, u32[]{:S(2)}, u32[]{:S(2)}) %collective-permute-start.44) | collective-permute-done | bytes 1048608 | tf_op jit(solution)/shard_map/ppermute | solution.py:46
  761.1 2.3 constant_dynamic-update-slice_fusion.8
  763.4 2.5 select_dynamic-update-slice_fusion.5
  766.4 16.6 %collective-permute-done.48 = bf16[1024,512]{1,0:T(8,128)(2,1)S(1)} collective-permute-done((bf16[1024,512]{1,0:T(8,128)(2,1)}, bf16[1024,512]{1,0:T(8,128)(2,1)S(1)}, u32[]{:S(2)}, u32[]{:S(2)}) %collective-permute-start.48) | collective-permute-done | bytes 1048608 | tf_op jit(solution)/shard_map/ppermute | solution.py:49
  783.0 2.3 collective-permute-start.49
  788.9 2.3 constant_dynamic-update-slice_fusion.5
  792.3 2.3 constant_dynamic-update-slice_fusion.3
  799.2 1.4 select_dynamic-update-slice_fusion.2
  800.6 23.2 %convolution_convert_fusion = bf16[1024,1024]{1,0:T(8,128)(2,1)} fusion(bf16[1024,8192]{1,0:T(8,128)(2,1)} %select_dynamic-update-slice_fusion.2, bf16[8192,1024]{1,0:T(8,128)(2,1)} %all-gather.8.cloned.1.call-done), kind=kOutput, calls=%fused_computation.8 | convolution fusion | flops 17180917760 | bytes 35651584 | tf_op jit(solution)/shard_map/dot_general | solution.py:345
  (155 shorter events, 52.7 us)
Async XLA Ops:
  6.5 233.2 %all-gather.4.cloned.1.call-start = ((), (), s32[]{:S(2)}) async-start(), calls=%async_computation | async-start | bytes 10485760 | tf_op jit(solution)/shard_map/all_gather | solution.py:294
  11.1 247.3 %all-gather.6.cloned.1.call-start = ((), (), s32[]{:S(2)}) async-start(), calls=%async_computation.1 | async-start | bytes 10485760 | tf_op jit(solution)/shard_map/all_gather | solution.py:294
  11.8 2.7 collective-permute-start.9
  13.1 2.6 collective-permute-start.10
  14.3 3.3 collective-permute-start.11
  19.4 15.2 %copy-start = (bf16[1024,1024]{1,0:T(8,128)(2,1)S(1)}, bf16[1024,1024]{1,0:T(8,128)(2,1)}, u32[]{:S(2)}) copy-start(bf16[1024,1024]{1,0:T(8,128)(2,1)} %param.6) | copy-start | bytes 6291460
  34.6 766.0 %all-gather.8.cloned.1.call-start = ((), (), s32[]{:S(2)}) async-start(), calls=%async_computation.2 | async-start | bytes 20971520 | tf_op jit(solution)/shard_map/all_gather | solution.py:330
  34.6 93.5 %collective-permute-start.1 = (bf16[1024,1024]{1,0:T(8,128)(2,1)S(1)}, bf16[1024,1024]{1,0:T(8,128)(2,1)}, u32[]{:S(2)}, u32[]{:S(2)}) collective-permute-start(bf16[1024,1024]{1,0:T(8,128)(2,1)S(1)} %copy-done), channel_id=1, source_target_pairs={{0,4},{1,5},{2,6},{3,7},{4,0},{5,1},{6,2},{7,3},{8,12},{9,13},{10,... | collective-permute-start | bytes 6291464 | tf_op jit(solution)/shard_map/ppermute | solution.py:45
  34.7 95.4 %collective-permute-start.3 = (bf16[1024,1024]{1,0:T(8,128)(2,1)S(1)}, bf16[1024,1024]{1,0:T(8,128)(2,1)}, u32[]{:S(2)}, u32[]{:S(2)}) collective-permute-start(bf16[1024,1024]{1,0:T(8,128)(2,1)S(1)} %copy-done), channel_id=1, source_target_pairs={{0,2},{1,3},{2,4},{3,5},{4,6},{5,7},{8,10},{9,11},{10,12},{11,13},... | collective-permute-start | bytes 6291464 | tf_op jit(solution)/shard_map/ppermute | solution.py:46
  36.0 94.5 %collective-permute-start.4 = (bf16[1024,1024]{1,0:T(8,128)(2,1)S(1)}, bf16[1024,1024]{1,0:T(8,128)(2,1)}, u32[]{:S(2)}, u32[]{:S(2)}) collective-permute-start(bf16[1024,1024]{1,0:T(8,128)(2,1)S(1)} %copy-done), channel_id=1, source_target_pairs={{2,0},{3,1},{4,2},{5,3},{6,4},{7,5},{10,8},{11,9},{12,10},{13,11},... | collective-permute-start | bytes 6291464 | tf_op jit(solution)/shard_map/ppermute | solution.py:47
  128.1 48.8 %collective-permute-start.7 = (bf16[1024,1024]{1,0:T(8,128)(2,1)}, bf16[1024,1024]{1,0:T(8,128)(2,1)}, u32[]{:S(2)}, u32[]{:S(2)}) collective-permute-start(bf16[1024,1024]{1,0:T(8,128)(2,1)} %collective-permute-done.1), channel_id=1, source_target_pairs={{4,6},{5,7},{2,0},{3,1},{12,14},{13,15},{10,8},{11,9},{20,22},{21,... | collective-permute-start | bytes 6291464 | tf_op jit(solution)/shard_map/ppermute | solution.py:49
  129.4 73.6 %collective-permute-start = (bf16[1024,1024]{1,0:T(8,128)(2,1)S(1)}, bf16[1024,1024]{1,0:T(8,128)(2,1)}, u32[]{:S(2)}, u32[]{:S(2)}) collective-permute-start(bf16[1024,1024]{1,0:T(8,128)(2,1)S(1)} %copy-done), channel_id=1, source_target_pairs={{0,1},{1,0},{2,3},{3,2},{4,5},{5,4},{6,7},{7,6},{8,9},{9,8},{10,11... | collective-permute-start | bytes 6291464 | tf_op jit(solution)/shard_map/ppermute | solution.py:43
  130.1 79.2 %collective-permute-start.2 = (bf16[1024,1024]{1,0:T(8,128)(2,1)}, bf16[1024,1024]{1,0:T(8,128)(2,1)}, u32[]{:S(2)}, u32[]{:S(2)}) collective-permute-start(bf16[1024,1024]{1,0:T(8,128)(2,1)} %collective-permute-done.1), channel_id=1, source_target_pairs={{0,1},{1,0},{2,3},{3,2},{4,5},{5,4},{6,7},{7,6},{8,9},{9,8},{10,11... | collective-permute-start | bytes 6291464 | tf_op jit(solution)/shard_map/ppermute | solution.py:43
  130.1 88.4 %collective-permute-start.5 = (bf16[1024,1024]{1,0:T(8,128)(2,1)}, bf16[1024,1024]{1,0:T(8,128)(2,1)}, u32[]{:S(2)}, u32[]{:S(2)}) collective-permute-start(bf16[1024,1024]{1,0:T(8,128)(2,1)} %collective-permute-done.3), channel_id=1, source_target_pairs={{0,1},{1,0},{2,3},{3,2},{4,5},{5,4},{6,7},{7,6},{8,9},{9,8},{10,11... | collective-permute-start | bytes 6291464 | tf_op jit(solution)/shard_map/ppermute | solution.py:43
  130.6 91.0 %collective-permute-start.6 = (bf16[1024,1024]{1,0:T(8,128)(2,1)}, bf16[1024,1024]{1,0:T(8,128)(2,1)}, u32[]{:S(2)}, u32[]{:S(2)}) collective-permute-start(bf16[1024,1024]{1,0:T(8,128)(2,1)} %collective-permute-done.4), channel_id=1, source_target_pairs={{0,1},{1,0},{2,3},{3,2},{4,5},{5,4},{6,7},{7,6},{8,9},{9,8},{10,11... | collective-permute-start | bytes 6291464 | tf_op jit(solution)/shard_map/ppermute | solution.py:43
  176.9 51.7 %collective-permute-start.8 = (bf16[1024,1024]{1,0:T(8,128)(2,1)}, bf16[1024,1024]{1,0:T(8,128)(2,1)}, u32[]{:S(2)}, u32[]{:S(2)}) collective-permute-start(bf16[1024,1024]{1,0:T(8,128)(2,1)} %collective-permute-done.7), channel_id=1, source_target_pairs={{0,1},{1,0},{6,7},{7,6},{8,9},{9,8},{14,15},{15,14},{16,17},{17,16... | collective-permute-start | bytes 6291464 | tf_op jit(solution)/shard_map/ppermute | solution.py:52
  255.6 50.0 %collective-permute-start.33 = (bf16[24,128,256]{2,1,0:T(8,128)(2,1)}, bf16[24,128,256]{2,1,0:T(8,128)(2,1)S(1)}, u32[]{:S(2)}, u32[]{:S(2)}) collective-permute-start(bf16[24,128,256]{2,1,0:T(8,128)(2,1)} %get-tuple-element.44), channel_id=1, source_target_pairs={{0,8},{8,0},{16,24},{24,16},{1,9},{9,1},{17,25},{25,17},{2,10},{10... | collective-permute-start | bytes 4718600 | tf_op jit(solution)/shard_map/ppermute | solution.py:27
  257.4 48.3 %collective-permute-start.34 = (bf16[24,128,256]{2,1,0:T(8,128)(2,1)}, bf16[24,128,256]{2,1,0:T(8,128)(2,1)S(1)}, u32[]{:S(2)}, u32[]{:S(2)}) collective-permute-start(bf16[24,128,256]{2,1,0:T(8,128)(2,1)} %get-tuple-element.45), channel_id=1, source_target_pairs={{0,16},{8,24},{16,0},{24,8},{1,17},{9,25},{17,1},{25,9},{2,18},{10... | collective-permute-start | bytes 4718600 | tf_op jit(solution)/shard_map/ppermute | solution.py:27
  273.6 30.0 %collective-permute-start.32 = (bf16[1024,256]{1,0:T(8,128)(2,1)S(1)}, bf16[1024,256]{1,0:T(8,128)(2,1)S(1)}, u32[]{:S(2)}, u32[]{:S(2)}) collective-permute-start(bf16[1024,256]{1,0:T(8,128)(2,1)S(1)} %get-tuple-element.67), channel_id=1, source_target_pairs={{0,8},{8,0},{16,24},{24,16},{1,9},{9,1},{17,25},{25,17},{2,10},{10... | collective-permute-start | bytes 1572872 | tf_op jit(solution)/shard_map/ppermute | solution.py:27
  275.2 29.5 %collective-permute-start.31 = (bf16[1024,256]{1,0:T(8,128)(2,1)S(1)}, bf16[1024,256]{1,0:T(8,128)(2,1)S(1)}, u32[]{:S(2)}, u32[]{:S(2)}) collective-permute-start(bf16[1024,256]{1,0:T(8,128)(2,1)S(1)} %get-tuple-element.68), channel_id=1, source_target_pairs={{0,16},{8,24},{16,0},{24,8},{1,17},{9,25},{17,1},{25,9},{2,18},{10... | collective-permute-start | bytes 1572872 | tf_op jit(solution)/shard_map/ppermute | solution.py:27
  305.7 1.2 copy-start.1
  305.7 1.7 copy-start.2
  322.2 54.8 %collective-permute-start.14 = (bf16[24,128,256]{2,1,0:T(8,128)(2,1)}, bf16[24,128,256]{2,1,0:T(8,128)(2,1)S(1)}, u32[]{:S(2)}, u32[]{:S(2)}) collective-permute-start(bf16[24,128,256]{2,1,0:T(8,128)(2,1)} %get-tuple-element.31), channel_id=1, source_target_pairs={{0,8},{8,0},{16,24},{24,16},{1,9},{9,1},{17,25},{25,17},{2,10},{10... | collective-permute-start | bytes 4718600 | tf_op jit(solution)/shard_map/ppermute | solution.py:27
  323.5 141.1 %collective-permute-start.15 = (bf16[24,128,256]{2,1,0:T(8,128)(2,1)}, bf16[24,128,256]{2,1,0:T(8,128)(2,1)S(1)}, u32[]{:S(2)}, u32[]{:S(2)}) collective-permute-start(bf16[24,128,256]{2,1,0:T(8,128)(2,1)} %get-tuple-element.32), channel_id=1, source_target_pairs={{0,16},{8,24},{16,0},{24,8},{1,17},{9,25},{17,1},{25,9},{2,18},{10... | collective-permute-start | bytes 4718600 | tf_op jit(solution)/shard_map/ppermute | solution.py:27
  324.7 156.1 %collective-permute-start.16 = (bf16[24,128,256]{2,1,0:T(8,128)(2,1)}, bf16[24,128,256]{2,1,0:T(8,128)(2,1)}, u32[]{:S(2)}, u32[]{:S(2)}) collective-permute-start(bf16[24,128,256]{2,1,0:T(8,128)(2,1)} %get-tuple-element.33), channel_id=1, source_target_pairs={{0,8},{8,0},{16,24},{24,16},{1,9},{9,1},{17,25},{25,17},{2,10},{10... | collective-permute-start | bytes 4718600 | tf_op jit(solution)/shard_map/ppermute | solution.py:27
  325.8 156.4 %collective-permute-start.17 = (bf16[24,128,256]{2,1,0:T(8,128)(2,1)}, bf16[24,128,256]{2,1,0:T(8,128)(2,1)}, u32[]{:S(2)}, u32[]{:S(2)}) collective-permute-start(bf16[24,128,256]{2,1,0:T(8,128)(2,1)} %get-tuple-element.34), channel_id=1, source_target_pairs={{0,16},{8,24},{16,0},{24,8},{1,17},{9,25},{17,1},{25,9},{2,18},{10... | collective-permute-start | bytes 4718600 | tf_op jit(solution)/shard_map/ppermute | solution.py:27
  327.1 131.6 %collective-permute-start.13 = (bf16[1024,256]{1,0:T(8,128)(2,1)S(1)}, bf16[1024,256]{1,0:T(8,128)(2,1)S(1)}, u32[]{:S(2)}, u32[]{:S(2)}) collective-permute-start(bf16[1024,256]{1,0:T(8,128)(2,1)S(1)} %get-tuple-element.69), channel_id=1, source_target_pairs={{0,8},{8,0},{16,24},{24,16},{1,9},{9,1},{17,25},{25,17},{2,10},{10... | collective-permute-start | bytes 1572872 | tf_op jit(solution)/shard_map/ppermute | solution.py:27
  377.0 87.6 %copy-start.3 = (bf16[24,128,256]{2,1,0:T(8,128)(2,1)}, bf16[24,128,256]{2,1,0:T(8,128)(2,1)S(1)}, u32[]{:S(2)}) copy-start(bf16[24,128,256]{2,1,0:T(8,128)(2,1)S(1)} %collective-permute-done.14.refs_7_) | copy-start | bytes 4718596
  377.0 84.0 %collective-permute-start.12 = (bf16[1024,256]{1,0:T(8,128)(2,1)S(1)}, bf16[1024,256]{1,0:T(8,128)(2,1)S(1)}, u32[]{:S(2)}, u32[]{:S(2)}) collective-permute-start(bf16[1024,256]{1,0:T(8,128)(2,1)S(1)} %get-tuple-element.70), channel_id=1, source_target_pairs={{0,16},{8,24},{16,0},{24,8},{1,17},{9,25},{17,1},{25,9},{2,18},{10... | collective-permute-start | bytes 1572872 | tf_op jit(solution)/shard_map/ppermute | solution.py:27
  458.7 96.9 %collective-permute-start.35 = (bf16[24,128,256]{2,1,0:T(8,128)(2,1)}, bf16[24,128,256]{2,1,0:T(8,128)(2,1)}, u32[]{:S(2)}, u32[]{:S(2)}) collective-permute-start(bf16[24,128,256]{2,1,0:T(8,128)(2,1)} %get-tuple-element.48), channel_id=1, source_target_pairs={{0,8},{8,0},{16,24},{24,16},{1,9},{9,1},{17,25},{25,17},{2,10},{10... | collective-permute-start | bytes 4718600 | tf_op jit(solution)/shard_map/ppermute | solution.py:27
  461.0 94.7 %collective-permute-start.36 = (bf16[24,128,256]{2,1,0:T(8,128)(2,1)}, bf16[24,128,256]{2,1,0:T(8,128)(2,1)}, u32[]{:S(2)}, u32[]{:S(2)}) collective-permute-start(bf16[24,128,256]{2,1,0:T(8,128)(2,1)} %get-tuple-element.49), channel_id=1, source_target_pairs={{0,16},{8,24},{16,0},{24,8},{1,17},{9,25},{17,1},{25,9},{2,18},{10... | collective-permute-start | bytes 4718600 | tf_op jit(solution)/shard_map/ppermute | solution.py:27
  464.6 1.1 copy-start.4
  480.6 74.9 %copy-start.7 = (f32[2,64,128]{2,1,0:T(8,128)S(1)}, f32[2,64,128]{2,1,0:T(8,128)}, u32[]{:S(2)}) copy-start(f32[2,64,128]{2,1,0:T(8,128)} %get-tuple-element.50.refs_11_) | copy-start | bytes 196612
  480.6 75.0 %copy-start.8 = (f32[2,64,128]{2,1,0:T(8,128)S(1)}, f32[2,64,128]{2,1,0:T(8,128)}, u32[]{:S(2)}) copy-start(f32[2,64,128]{2,1,0:T(8,128)} %get-tuple-element.51.refs_12_) | copy-start | bytes 196612
  480.6 52.1 %collective-permute-start.18 = (f32[2,64,128]{2,1,0:T(8,128)}, f32[2,64,128]{2,1,0:T(8,128)S(1)}, u32[]{:S(2)}, u32[]{:S(2)}) collective-permute-start(f32[2,64,128]{2,1,0:T(8,128)} %get-tuple-element.35.refs_11_), channel_id=1, source_target_pairs={{0,16},{8,24},{16,0},{24,8},{1,17},{9,25},{17,1},{25,9},{2,18},{10... | collective-permute-start | bytes 196616 | tf_op jit(solution)/shard_map/ppermute | solution.py:27
  480.7 52.0 %collective-permute-start.19 = (f32[2,64,128]{2,1,0:T(8,128)}, f32[2,64,128]{2,1,0:T(8,128)S(1)}, u32[]{:S(2)}, u32[]{:S(2)}) collective-permute-start(f32[2,64,128]{2,1,0:T(8,128)} %get-tuple-element.36.refs_12_), channel_id=1, source_target_pairs={{0,8},{8,0},{16,24},{24,16},{1,9},{9,1},{17,25},{25,17},{2,10},{10... | collective-permute-start | bytes 196616 | tf_op jit(solution)/shard_map/ppermute | solution.py:27
  552.3 65.4 %copy-start.6 = (f32[1024,256]{1,0:T(8,128)S(1)}, f32[1024,256]{1,0:T(8,128)}, u32[]{:S(2)}) copy-start(f32[1024,256]{1,0:T(8,128)} %get-tuple-element.37) | copy-start | bytes 3145732
  552.3 66.7 %copy-start.5 = (f32[1024,256]{1,0:T(8,128)S(1)}, f32[1024,256]{1,0:T(8,128)}, u32[]{:S(2)}) copy-start(f32[1024,256]{1,0:T(8,128)} %get-tuple-element.39) | copy-start | bytes 3145732
  552.3 65.3 %collective-permute-start.20 = (f32[1024,256]{1,0:T(8,128)}, f32[1024,256]{1,0:T(8,128)}, u32[]{:S(2)}, u32[]{:S(2)}) collective-permute-start(f32[1024,256]{1,0:T(8,128)} %get-tuple-element.38), channel_id=1, source_target_pairs={{0,16},{8,24},{16,0},{24,8},{1,17},{9,25},{17,1},{25,9},{2,18},{10... | collective-permute-start | bytes 3145736 | tf_op jit(solution)/shard_map/ppermute | solution.py:27
  554.0 64.9 %collective-permute-start.21 = (f32[1024,256]{1,0:T(8,128)}, f32[1024,256]{1,0:T(8,128)S(1)}, u32[]{:S(2)}, u32[]{:S(2)}) collective-permute-start(f32[1024,256]{1,0:T(8,128)} %get-tuple-element.40), channel_id=1, source_target_pairs={{0,8},{8,0},{16,24},{24,16},{1,9},{9,1},{17,25},{25,17},{2,10},{10... | collective-permute-start | bytes 3145736 | tf_op jit(solution)/shard_map/ppermute | solution.py:27
  555.5 41.3 %collective-permute-start.37 = (f32[2,64,128]{2,1,0:T(8,128)S(1)}, f32[2,64,128]{2,1,0:T(8,128)S(1)}, u32[]{:S(2)}, u32[]{:S(2)}) collective-permute-start(f32[2,64,128]{2,1,0:T(8,128)S(1)} %copy-done.7), channel_id=1, source_target_pairs={{0,16},{8,24},{16,0},{24,8},{1,17},{9,25},{17,1},{25,9},{2,18},{10... | collective-permute-start | bytes 196616 | tf_op jit(solution)/shard_map/ppermute | solution.py:27
  555.6 41.2 %collective-permute-start.38 = (f32[2,64,128]{2,1,0:T(8,128)S(1)}, f32[2,64,128]{2,1,0:T(8,128)S(1)}, u32[]{:S(2)}, u32[]{:S(2)}) collective-permute-start(f32[2,64,128]{2,1,0:T(8,128)S(1)} %copy-done.8), channel_id=1, source_target_pairs={{0,8},{8,0},{16,24},{24,16},{1,9},{9,1},{17,25},{25,17},{2,10},{10... | collective-permute-start | bytes 196616 | tf_op jit(solution)/shard_map/ppermute | solution.py:27
  596.8 0.6 copy-start.9
  597.4 0.6 copy-start.11
  616.5 22.6 %collective-permute-start.39 = (f32[1024,256]{1,0:T(8,128)}, f32[1024,256]{1,0:T(8,128)S(1)}, u32[]{:S(2)}, u32[]{:S(2)}) collective-permute-start(f32[1024,256]{1,0:T(8,128)} %get-tuple-element.53), channel_id=1, source_target_pairs={{0,16},{8,24},{16,0},{24,8},{1,17},{9,25},{17,1},{25,9},{2,18},{10... | collective-permute-start | bytes 3145736 | tf_op jit(solution)/shard_map/ppermute | solution.py:27
  619.2 48.3 %collective-permute-start.23 = (bf16[1024,512]{1,0:T(8,128)(2,1)S(1)}, bf16[1024,512]{1,0:T(8,128)(2,1)}, u32[]{:S(2)}, u32[]{:S(2)}) collective-permute-start(bf16[1024,512]{1,0:T(8,128)(2,1)S(1)} %pad_maximum_fusion.2), channel_id=1, source_target_pairs={{0,4},{1,5},{2,6},{3,7},{4,0},{5,1},{6,2},{7,3},{8,12},{9,13},{10,... | collective-permute-start | bytes 3145736 | tf_op jit(solution)/shard_map/ppermute | solution.py:45
  619.3 50.2 %collective-permute-start.40 = (f32[1024,256]{1,0:T(8,128)}, f32[1024,256]{1,0:T(8,128)S(1)}, u32[]{:S(2)}, u32[]{:S(2)}) collective-permute-start(f32[1024,256]{1,0:T(8,128)} %get-tuple-element.55), channel_id=1, source_target_pairs={{0,8},{8,0},{16,24},{24,16},{1,9},{9,1},{17,25},{25,17},{2,10},{10... | collective-permute-start | bytes 3145736 | tf_op jit(solution)/shard_map/ppermute | solution.py:27
  620.7 50.2 %collective-permute-start.25 = (bf16[1024,512]{1,0:T(8,128)(2,1)S(1)}, bf16[1024,512]{1,0:T(8,128)(2,1)}, u32[]{:S(2)}, u32[]{:S(2)}) collective-permute-start(bf16[1024,512]{1,0:T(8,128)(2,1)S(1)} %pad_maximum_fusion.2), channel_id=1, source_target_pairs={{0,2},{1,3},{2,4},{3,5},{4,6},{5,7},{8,10},{9,11},{10,12},{11,13},... | collective-permute-start | bytes 3145736 | tf_op jit(solution)/shard_map/ppermute | solution.py:46
  622.0 50.7 %collective-permute-start.22 = (bf16[1024,512]{1,0:T(8,128)(2,1)S(1)}, bf16[1024,512]{1,0:T(8,128)(2,1)S(1)}, u32[]{:S(2)}, u32[]{:S(2)}) collective-permute-start(bf16[1024,512]{1,0:T(8,128)(2,1)S(1)} %pad_maximum_fusion.2), channel_id=1, source_target_pairs={{0,1},{1,0},{2,3},{3,2},{4,5},{5,4},{6,7},{7,6},{8,9},{9,8},{10,11... | collective-permute-start | bytes 3145736 | tf_op jit(solution)/shard_map/ppermute | solution.py:43
  639.1 52.8 %collective-permute-start.26 = (bf16[1024,512]{1,0:T(8,128)(2,1)S(1)}, bf16[1024,512]{1,0:T(8,128)(2,1)}, u32[]{:S(2)}, u32[]{:S(2)}) collective-permute-start(bf16[1024,512]{1,0:T(8,128)(2,1)S(1)} %pad_maximum_fusion.2), channel_id=1, source_target_pairs={{2,0},{3,1},{4,2},{5,3},{6,4},{7,5},{10,8},{11,9},{12,10},{13,11},... | collective-permute-start | bytes 3145736 | tf_op jit(solution)/shard_map/ppermute | solution.py:47
  667.5 24.7 %collective-permute-start.24 = (bf16[1024,512]{1,0:T(8,128)(2,1)}, bf16[1024,512]{1,0:T(8,128)(2,1)}, u32[]{:S(2)}, u32[]{:S(2)}) collective-permute-start(bf16[1024,512]{1,0:T(8,128)(2,1)} %collective-permute-done.23), channel_id=1, source_target_pairs={{0,1},{1,0},{2,3},{3,2},{4,5},{5,4},{6,7},{7,6},{8,9},{9,8},{10,11... | collective-permute-start | bytes 3145736 | tf_op jit(solution)/shard_map/ppermute | solution.py:43
  670.9 24.9 %collective-permute-start.27 = (bf16[1024,512]{1,0:T(8,128)(2,1)}, bf16[1024,512]{1,0:T(8,128)(2,1)}, u32[]{:S(2)}, u32[]{:S(2)}) collective-permute-start(bf16[1024,512]{1,0:T(8,128)(2,1)} %collective-permute-done.25), channel_id=1, source_target_pairs={{0,1},{1,0},{2,3},{3,2},{4,5},{5,4},{6,7},{7,6},{8,9},{9,8},{10,11... | collective-permute-start | bytes 3145736 | tf_op jit(solution)/shard_map/ppermute | solution.py:43
  671.4 47.9 %collective-permute-start.29 = (bf16[1024,512]{1,0:T(8,128)(2,1)}, bf16[1024,512]{1,0:T(8,128)(2,1)}, u32[]{:S(2)}, u32[]{:S(2)}) collective-permute-start(bf16[1024,512]{1,0:T(8,128)(2,1)} %collective-permute-done.23), channel_id=1, source_target_pairs={{4,6},{5,7},{2,0},{3,1},{12,14},{13,15},{10,8},{11,9},{20,22},{21,... | collective-permute-start | bytes 3145736 | tf_op jit(solution)/shard_map/ppermute | solution.py:49
  672.7 65.4 %collective-permute-start.42 = (bf16[1024,512]{1,0:T(8,128)(2,1)S(1)}, bf16[1024,512]{1,0:T(8,128)(2,1)}, u32[]{:S(2)}, u32[]{:S(2)}) collective-permute-start(bf16[1024,512]{1,0:T(8,128)(2,1)S(1)} %pad_maximum_fusion.5), channel_id=1, source_target_pairs={{0,4},{1,5},{2,6},{3,7},{4,0},{5,1},{6,2},{7,3},{8,12},{9,13},{10,... | collective-permute-start | bytes 3145736 | tf_op jit(solution)/shard_map/ppermute | solution.py:45
  691.9 54.4 %collective-permute-start.28 = (bf16[1024,512]{1,0:T(8,128)(2,1)}, bf16[1024,512]{1,0:T(8,128)(2,1)}, u32[]{:S(2)}, u32[]{:S(2)}) collective-permute-start(bf16[1024,512]{1,0:T(8,128)(2,1)} %collective-permute-done.26), channel_id=1, source_target_pairs={{0,1},{1,0},{2,3},{3,2},{4,5},{5,4},{6,7},{7,6},{8,9},{9,8},{10,11... | collective-permute-start | bytes 3145736 | tf_op jit(solution)/shard_map/ppermute | solution.py:43
  692.2 68.4 %collective-permute-start.44 = (bf16[1024,512]{1,0:T(8,128)(2,1)S(1)}, bf16[1024,512]{1,0:T(8,128)(2,1)}, u32[]{:S(2)}, u32[]{:S(2)}) collective-permute-start(bf16[1024,512]{1,0:T(8,128)(2,1)S(1)} %pad_maximum_fusion.5), channel_id=1, source_target_pairs={{0,2},{1,3},{2,4},{3,5},{4,6},{5,7},{8,10},{9,11},{10,12},{11,13},... | collective-permute-start | bytes 3145736 | tf_op jit(solution)/shard_map/ppermute | solution.py:46
  695.8 70.1 %collective-permute-start.45 = (bf16[1024,512]{1,0:T(8,128)(2,1)S(1)}, bf16[1024,512]{1,0:T(8,128)(2,1)S(1)}, u32[]{:S(2)}, u32[]{:S(2)}) collective-permute-start(bf16[1024,512]{1,0:T(8,128)(2,1)S(1)} %pad_maximum_fusion.5), channel_id=1, source_target_pairs={{2,0},{3,1},{4,2},{5,3},{6,4},{7,5},{10,8},{11,9},{12,10},{13,11},... | collective-permute-start | bytes 3145736 | tf_op jit(solution)/shard_map/ppermute | solution.py:47
  719.3 46.7 %collective-permute-start.30 = (bf16[1024,512]{1,0:T(8,128)(2,1)}, bf16[1024,512]{1,0:T(8,128)(2,1)S(1)}, u32[]{:S(2)}, u32[]{:S(2)}) collective-permute-start(bf16[1024,512]{1,0:T(8,128)(2,1)} %collective-permute-done.29), channel_id=1, source_target_pairs={{0,1},{1,0},{6,7},{7,6},{8,9},{9,8},{14,15},{15,14},{16,17},{17,16... | collective-permute-start | bytes 3145736 | tf_op jit(solution)/shard_map/ppermute | solution.py:52
  738.1 44.9 %collective-permute-start.48 = (bf16[1024,512]{1,0:T(8,128)(2,1)}, bf16[1024,512]{1,0:T(8,128)(2,1)S(1)}, u32[]{:S(2)}, u32[]{:S(2)}) collective-permute-start(bf16[1024,512]{1,0:T(8,128)(2,1)} %collective-permute-done.42), channel_id=1, source_target_pairs={{4,6},{5,7},{2,0},{3,1},{12,14},{13,15},{10,8},{11,9},{20,22},{21,... | collective-permute-start | bytes 3145736 | tf_op jit(solution)/shard_map/ppermute | solution.py:49
  746.3 41.5 %collective-permute-start.41 = (bf16[1024,512]{1,0:T(8,128)(2,1)S(1)}, bf16[1024,512]{1,0:T(8,128)(2,1)S(1)}, u32[]{:S(2)}, u32[]{:S(2)}) collective-permute-start(bf16[1024,512]{1,0:T(8,128)(2,1)S(1)} %pad_maximum_fusion.5), channel_id=1, source_target_pairs={{0,1},{1,0},{2,3},{3,2},{4,5},{5,4},{6,7},{7,6},{8,9},{9,8},{10,11... | collective-permute-start | bytes 3145736 | tf_op jit(solution)/shard_map/ppermute | solution.py:43
  760.6 30.5 %collective-permute-start.43 = (bf16[1024,512]{1,0:T(8,128)(2,1)}, bf16[1024,512]{1,0:T(8,128)(2,1)S(1)}, u32[]{:S(2)}, u32[]{:S(2)}) collective-permute-start(bf16[1024,512]{1,0:T(8,128)(2,1)} %collective-permute-done.42), channel_id=1, source_target_pairs={{0,1},{1,0},{2,3},{3,2},{4,5},{5,4},{6,7},{7,6},{8,9},{9,8},{10,11... | collective-permute-start | bytes 3145736 | tf_op jit(solution)/shard_map/ppermute | solution.py:43
  765.9 29.7 %collective-permute-start.46 = (bf16[1024,512]{1,0:T(8,128)(2,1)}, bf16[1024,512]{1,0:T(8,128)(2,1)S(1)}, u32[]{:S(2)}, u32[]{:S(2)}) collective-permute-start(bf16[1024,512]{1,0:T(8,128)(2,1)} %collective-permute-done.44), channel_id=1, source_target_pairs={{0,1},{1,0},{2,3},{3,2},{4,5},{5,4},{6,7},{7,6},{8,9},{9,8},{10,11... | collective-permute-start | bytes 3145736 | tf_op jit(solution)/shard_map/ppermute | solution.py:43
  766.0 30.7 %collective-permute-start.47 = (bf16[1024,512]{1,0:T(8,128)(2,1)S(1)}, bf16[1024,512]{1,0:T(8,128)(2,1)S(1)}, u32[]{:S(2)}, u32[]{:S(2)}) collective-permute-start(bf16[1024,512]{1,0:T(8,128)(2,1)S(1)} %collective-permute-done.45), channel_id=1, source_target_pairs={{0,1},{1,0},{2,3},{3,2},{4,5},{5,4},{6,7},{7,6},{8,9},{9,8},{10,11... | collective-permute-start | bytes 3145736 | tf_op jit(solution)/shard_map/ppermute | solution.py:43
  783.0 16.2 %collective-permute-start.49 = (bf16[1024,512]{1,0:T(8,128)(2,1)S(1)}, bf16[1024,512]{1,0:T(8,128)(2,1)S(1)}, u32[]{:S(2)}, u32[]{:S(2)}) collective-permute-start(bf16[1024,512]{1,0:T(8,128)(2,1)S(1)} %collective-permute-done.48), channel_id=1, source_target_pairs={{0,1},{1,0},{6,7},{7,6},{8,9},{9,8},{14,15},{15,14},{16,17},{17,16... | collective-permute-start | bytes 3145736 | tf_op jit(solution)/shard_map/ppermute | solution.py:52
  (2 other events, 1.2 us)
Sparse Core Ops, SparseCore 0:
  11.2 88.2 all-gather.3
  101.3 87.4 all-gather.5
  322.4 269.8 all-gather.7
